TPU v7x, 32 devices: a whole 2x2x4 slice. The times are simulated.
32 devices in a mesh: dp: 8 (over z, x), seq: 4 (over y, core).
Axes of the slice: x: 2, y: 2, z: 4, core: 2. Of those that a mesh axis runs over, the one named last changes fastest.
Arguments:
- tokens: bfloat16 [32, 512, 768], P('dp', 'seq'), may hold values from -6 to 6
- memory_init: bfloat16 [768, 10], replicated, may hold values from -6 to 6
- query_weight: bfloat16 [768, 768], replicated, may hold values from -0.21875 to 0.21875
- query_bias: bfloat16 [768], replicated, may hold values from -3 to 3
- key_weight: bfloat16 [768, 768], replicated, may hold values from -0.21875 to 0.21875
- value_weight: bfloat16 [768, 768], replicated, may hold values from -0.21875 to 0.21875
- value_bias: bfloat16 [768], replicated, may hold values from -3 to 3
- output_weight: bfloat16 [768, 768], replicated, may hold values from -1.75 to 1.75
- output_bias: bfloat16 [768], replicated, may hold values from -3 to 3
- attn_gain: bfloat16 [768], replicated, may hold values from 0.5 to 1.5
- attn_shift: bfloat16 [768], replicated, may hold values from -3 to 3
- inner_weight: bfloat16 [768, 3072], replicated, may hold values from -0.21875 to 0.21875
- inner_bias: bfloat16 [3072], replicated, may hold values from -3 to 3
- outer_weight: bfloat16 [3072, 768], replicated, may hold values from -0.109375 to 0.109375
- outer_bias: bfloat16 [768], replicated, may hold values from -3 to 3
- ffn_gain: bfloat16 [768], replicated, may hold values from 0.5 to 1.5
- ffn_shift: bfloat16 [768], replicated, may hold values from -3 to 3
- out_grad: bfloat16 [32, 512, 768], P('dp', 'seq'), may hold values from -6 to 6
- lm_mask: int32 [32, 512], P('dp', 'seq'), may hold values from 0 to 1, as said below
- doc_segments: int32 [8], replicated, may hold values from 1 to 8, 32 in all
Outputs:
- layer_out: bfloat16 [32, 512, 768], P('dp', 'seq')
- tokens_grad: float32 [32, 512, 768], P('dp', 'seq')
- query_weight_grad: float32 [768, 768], P('dp')
- query_bias_grad: float32 [768], P('dp')
- key_weight_grad: float32 [768, 768], P('dp')
- value_weight_grad: float32 [768, 768], P('dp')
- value_bias_grad: float32 [768], P('dp')
- output_weight_grad: float32 [768, 768], P('dp')
- output_bias_grad: float32 [768], P('dp')
- attn_gain_grad: float32 [768], P('dp')
- attn_shift_grad: float32 [768], P('dp')
- inner_weight_grad: float32 [768, 3072], P('dp')
- inner_bias_grad: float32 [3072], P('dp')
- outer_weight_grad: float32 [3072, 768], P('dp')
- outer_bias_grad: float32 [768], P('dp')
- ffn_gain_grad: float32 [768], P('dp')
- ffn_shift_grad: float32 [768], P('dp')
- memory_init_grad: float32 [768, 10], P('dp')
Inputs may be any that keep to these rules, and one draw needn't show every extreme that they name: `lm_mask`: 1 marks a masked position; the share of ones rises along the segments; some whole segments have no ones.
All inputs are finite; a program needn't handle non-finite values.
Results may differ from a plain program's by a relative error of at most 0.014.
Values may be sent and summed in bfloat16 or wider, within the bound.
No kernel may reach another device: no remote copies, remote signals or barrier semaphores. Data moves between devices by JAX's collectives and lax.ppermute only.
A program may use at most 192 MiB of HBM per device.

v0:
```python
import jax
import jax.numpy as jnp
from jax import lax
from jax.experimental import pallas as pl
from jax.experimental.pallas import tpu as pltpu
from jax.sharding import PartitionSpec as P


HEAD_DIM = 64
EPS = 1e-06
LOG2E = 1.4426950408889634
BLOCK = 768
DIGITS = 16
EXTRA = 16
f32 = jnp.float32
bf16 = jnp.bfloat16


def dot(a, b, ca, cb):
    return lax.dot_general(a, b, (((ca,), (cb,)), ((), ())), preferred_element_type=f32)


def attn_fwd_kernel(q_ref, k_ref, v_ref, ctx_ref, p_ref):
    q = q_ref[...]
    k = k_ref[...]
    v = v_ref[...]
    lanes = lax.broadcasted_iota(jnp.int32, (1, 2 * HEAD_DIM), 1)
    ctx = None
    for h in range(2):
        mask = (lanes // HEAD_DIM) == h
        kh = jnp.where(mask, k, jnp.zeros_like(k))
        vh = jnp.where(mask, v, jnp.zeros_like(v))
        s = dot(q, kh, 1, 1) * (HEAD_DIM ** (-0.5) * LOG2E)
        e = jnp.exp2(s - jnp.max(s, axis=-1, keepdims=True))
        p = (e * (1.0 / jnp.sum(e, axis=-1, keepdims=True))).astype(bf16)
        p_ref[h] = p
        c = dot(p, vh, 1, 0)
        ctx = c if ctx is None else ctx + c
    ctx_ref[...] = ctx.astype(bf16)


def attn_bwd_kernel(q_ref, k_ref, v_ref, ctx_ref, dctx_ref, p_ref, dq_ref, dk_ref, dv_ref):
    q = q_ref[...]
    k = k_ref[...]
    v = v_ref[...]
    dctx = dctx_ref[...]
    prod = dctx.astype(f32) * ctx_ref[...].astype(f32)
    lanes = lax.broadcasted_iota(jnp.int32, (1, 2 * HEAD_DIM), 1)
    scale = HEAD_DIM ** (-0.5)
    dq = None
    dk = None
    dv = None
    for h in range(2):
        mask = (lanes // HEAD_DIM) == h
        zero = jnp.zeros_like(k)
        vh = jnp.where(mask, v, zero)
        kh = jnp.where(mask, k, zero)
        qh = jnp.where(mask, q, zero)
        dh = jnp.where(mask, dctx, zero)
        delta = jnp.sum(jnp.where(mask, prod, 0.0), axis=-1, keepdims=True)
        p = p_ref[h]
        dp = dot(dctx, vh, 1, 1)
        ds = (p.astype(f32) * (dp - delta)).astype(bf16)
        dqh = dot(ds, kh, 1, 0)
        dkh = dot(ds, qh, 0, 0)
        dvh = dot(p, dh, 0, 0)
        dq = dqh if dq is None else dq + dqh
        dk = dkh if dk is None else dk + dkh
        dv = dvh if dv is None else dv + dvh
    dq_ref[...] = (dq * scale).astype(bf16)
    dk_ref[...] = (dk * scale).astype(bf16)
    dv_ref[...] = dv.astype(bf16)


def attention_forward(q, k, v, segs, rows):
    block = 2 * HEAD_DIM
    pairs = q.shape[1] // block
    spec = pl.BlockSpec((rows, block), lambda s, h: (s, h))
    pspec = pl.BlockSpec((2, rows, rows), lambda s, h: (s * pairs + h, 0, 0))
    return pl.pallas_call(
        attn_fwd_kernel,
        grid=(segs, pairs),
        in_specs=[spec, spec, spec],
        out_specs=[spec, pspec],
        out_shape=[
            jax.ShapeDtypeStruct(q.shape, bf16),
            jax.ShapeDtypeStruct((segs * 2 * pairs, rows, rows), bf16),
        ],
        name="attn_fwd",
    )(q, k, v)


def attention_backward(q, k, v, ctx, dctx, p, segs, rows):
    block = 2 * HEAD_DIM
    pairs = q.shape[1] // block
    spec = pl.BlockSpec((rows, block), lambda s, h: (s, h))
    pspec = pl.BlockSpec((2, rows, rows), lambda s, h: (s * pairs + h, 0, 0))
    shape = jax.ShapeDtypeStruct(q.shape, bf16)
    return pl.pallas_call(
        attn_bwd_kernel,
        grid=(segs, pairs),
        in_specs=[spec] * 5 + [pspec],
        out_specs=[spec] * 3,
        out_shape=[shape] * 3,
        name="attn_bwd",
    )(q, k, v, ctx, dctx, p)


def upper_tail(x):
    z = jnp.abs(x) * (0.5 ** 0.5)
    t = 1.0 / (1.0 + 0.5 * z)
    poly = 0.17087277
    for c in (
        -0.82215223,
        1.48851587,
        -1.13520398,
        0.27886807,
        -0.18628806,
        0.09678418,
        0.37409196,
        1.00002368,
        -1.26551223,
    ):
        poly = poly * t + c
    bell = jnp.exp(-0.5 * x * x)
    half = 0.5 * t * bell * jnp.exp(poly)
    return jnp.where(x >= 0, 1.0 - half, half), bell


def normalize(values):
    center = values - jnp.mean(values, axis=-1, keepdims=True)
    inv = lax.rsqrt(jnp.mean(center * center, axis=-1, keepdims=True) + EPS)
    return center * inv, inv


def normalize_back(hat, inv, g):
    a = jnp.mean(g, axis=-1, keepdims=True)
    b = jnp.mean(g * hat, axis=-1, keepdims=True)
    return inv * (g - a - hat * b)


def rows_of(*vectors):
    lines = [jnp.sum(v, axis=0, keepdims=True) for v in vectors]
    pad = 8 - len(lines)
    return jnp.concatenate(lines + [jnp.zeros((pad, lines[0].shape[1]), f32)], axis=0)


def ffn_forward(flat, ctx, wout, vecs, wi, ib, wo, cot_pieces, rows_dev):
    n, width = flat.shape
    inner = wi.shape[1]
    count = len(cot_pieces)

    def kernel(flat_ref, ctx_ref, wout_ref, vec_ref, wi_ref, ib_ref, wo_ref, *refs):
        cot_refs = refs[:count]
        hat1_ref, inv1_ref, n1t_ref, active_ref, slope_ref = refs[count : count + 5]
        out_refs = refs[count + 5 : 2 * count + 5]
        dres_ref, douter_ref, small_ref, low, acc = refs[2 * count + 5 :]
        j = pl.program_id(0)

        @pl.when(j == 0)
        def _():
            resid = flat_ref[...].astype(f32) + dot(ctx_ref[...], wout_ref[...], 1, 0) + vec_ref[0:1]
            hat, inv = normalize(resid)
            hat1_ref[...] = hat
            inv1_ref[...] = jnp.broadcast_to(inv, inv1_ref.shape)
            normed = hat * vec_ref[1:2] + vec_ref[2:3]
            low[...] = normed.astype(bf16)
            n1t_ref[...] = normed.astype(bf16).T
            acc[...] = normed + vec_ref[3:4]

        inner = dot(low[...], wi_ref[...], 1, 0) + ib_ref[...]
        cdf, bell = upper_tail(inner)
        active = (inner * cdf).astype(bf16)
        active_ref[...] = active
        slope_ref[...] = (cdf + inner * bell * 0.3989422804014327).astype(bf16)
        acc[...] += dot(active, wo_ref[...], 1, 0)

        @pl.when(j == pl.num_programs(0) - 1)
        def _():
            valid_rows = cot_refs[0][rows_dev : rows_dev + EXTRA].astype(f32)[0:1]
            for r in cot_refs[1:]:
                valid_rows = valid_rows + r[rows_dev : rows_dev + EXTRA].astype(f32)[0:1]
            scale = 1.0 / jnp.maximum(valid_rows, 1.0)
            lines = [valid_rows * 0.0] * 3
            for k in range(count):
                part = slice(k * rows_dev, (k + 1) * rows_dev)
                hat, inv = normalize(acc[part])
                out_refs[k][...] = (hat * vec_ref[4:5] + vec_ref[5:6]).astype(bf16)
                cot = cot_refs[k][0:rows_dev].astype(f32) * scale
                dres = normalize_back(hat, inv, cot * vec_ref[4:5])
                dres_ref[part] = dres
                low_d = dres.astype(bf16)
                douter_ref[part] = low_d
                for i, v in enumerate((cot * hat, cot, low_d.astype(f32))):
                    lines[i] = lines[i] + jnp.sum(v, axis=0, keepdims=True)
            for i, v in enumerate(lines + [valid_rows]):
                small_ref[i : i + 1] = v

    full = lambda a: pl.BlockSpec(a.shape, lambda j: (0,) * a.ndim)
    whole = lambda shape: pl.BlockSpec(shape, lambda j: (0,) * len(shape))
    cols = pl.BlockSpec((n, BLOCK), lambda j: (0, j))
    outs = [
        (whole, (n, width), f32),
        (whole, (n, 128), f32),
        (whole, (width, n), bf16),
        (None, (n, inner), bf16),
        (None, (n, inner), bf16),
    ]
    outs += [(whole, (rows_dev, width), bf16)] * count
    outs += [(whole, (n, width), f32), (whole, (n, width), bf16), (whole, (8, width), f32)]
    got = pl.pallas_call(
        kernel,
        grid=(inner // BLOCK,),
        in_specs=[
            full(flat),
            full(ctx),
            full(wout),
            full(vecs),
            pl.BlockSpec((width, BLOCK), lambda j: (0, j)),
            pl.BlockSpec((1, BLOCK), lambda j: (0, j)),
            pl.BlockSpec((BLOCK, width), lambda j: (j, 0)),
        ]
        + [full(c) for c in cot_pieces],
        out_specs=[spec(shape) if spec else cols for spec, shape, _ in outs],
        out_shape=[jax.ShapeDtypeStruct(shape, kind) for _, shape, kind in outs],
        scratch_shapes=[pltpu.VMEM((n, width), bf16), pltpu.VMEM((n, width), f32)],
        name="ffn_fwd",
    )(flat, ctx, wout, vecs, wi, ib, wo, *cot_pieces)
    return got[:5], got[5 : 5 + count], got[5 + count :]


def inputs_backward(me, grads, weights, d_resid1, small1, small2, d_inner_bias, rows_dev, nseq, mem_rows):
    _, width = d_resid1.shape
    ib_rows = d_inner_bias.shape[1] // width

    def kernel(me_ref, dq_ref, dk_ref, dv_ref, wq_ref, wk_ref, wv_ref, dres_ref, s1_ref, s2_ref, ib_ref, *outs):
        pieces, small_ref = outs[:nseq], outs[nseq]
        seq_me = me_ref[1]
        first = me_ref[2]
        small_ref[...] = jnp.zeros_like(small_ref)
        d = dres_ref[...]
        for g, w in ((dq_ref, wq_ref), (dk_ref, wk_ref), (dv_ref, wv_ref)):
            d = d + dot(g[...], w[...], 1, 1)
        row = lax.broadcasted_iota(jnp.int32, (rows_dev, 1), 0)
        memory = jnp.zeros((EXTRA, width), f32)
        for k in range(nseq):
            part = d[k * rows_dev : (k + 1) * rows_dev]
            is_mem = jnp.logical_and(row < mem_rows, jnp.logical_and(seq_me == k, first != 0))
            pieces[k][...] = jnp.where(is_mem, 0.0, part).astype(bf16)
            memory = memory + jnp.where(is_mem[:EXTRA], part[:EXTRA], 0.0)
        small_ref[0, 0:1] = jnp.sum(dq_ref[...].astype(f32), axis=0, keepdims=True)
        small_ref[0, 1:2] = jnp.sum(dv_ref[...].astype(f32), axis=0, keepdims=True)
        small_ref[0, 2:5] = s1_ref[0:3]
        small_ref[0, 5:8] = s2_ref[0:3]
        for r in range(ib_rows):
            small_ref[1, r : r + 1] = ib_ref[0:1, r * width : (r + 1) * width]
        lane = lax.broadcasted_iota(jnp.int32, (1, width), 1)
        bits = (s2_ref[3:4].astype(jnp.int32) >> jnp.minimum(lane, DIGITS)) & 1
        small_ref[1, ib_rows : ib_rows + 1] = bits.astype(f32)
        small_ref[2] = memory

    vmem = pl.BlockSpec(memory_space=pltpu.VMEM)
    got = pl.pallas_call(
        kernel,
        in_specs=[pl.BlockSpec(memory_space=pltpu.SMEM)] + [vmem] * 10,
        out_specs=[vmem] * (nseq + 1),
        out_shape=[jax.ShapeDtypeStruct((rows_dev, width), bf16)] * nseq
        + [jax.ShapeDtypeStruct((nseq, EXTRA, width), f32)],
        name="inputs_bwd",
    )(me, *grads, *weights, d_resid1, small1, small2, d_inner_bias)
    return got[:nseq], got[nseq]


class Plan:
    def __init__(self, mesh):
        self.ndp, self.nseq = mesh.shape["dp"], mesh.shape["seq"]
        bits = [("seq", b) for b in range(self.nseq.bit_length() - 1)]
        dp_bits = [("dp", b) for b in range(self.ndp.bit_length() - 1)]
        assert 2 ** len(bits) == self.nseq and 2 ** len(dp_bits) == self.ndp
        rest = bits[2:] + dp_bits[1:]
        self.first = bits[0]
        self.orders = [[bits[1], dp_bits[0]] + rest, [dp_bits[0], bits[1]] + rest]
        self.steps = len(self.orders[0])
        self.places = 1 << self.steps

    def flip(self, device, which):
        axis, b = which
        return device ^ ((1 << b) * (self.nseq if axis == "dp" else 1))

    def perm(self, step):
        devices = range(self.ndp * self.nseq)
        if step < 0:
            return [(d, self.flip(d, self.first)) for d in devices]
        return [(d, self.flip(d, self.orders[d & 1][step])) for d in devices]

    def place(self, dp_diff, seq_diff, half):
        value = {"dp": dp_diff, "seq": seq_diff}
        places = []
        for order in self.orders:
            p = 0
            for axis, b in order:
                p = p * 2 + ((value[axis] >> b) & 1)
            places.append(p)
        return jnp.where(half == 0, places[0], places[1])


def scatter_pieces(plan, me_ref, result, pieces, keep_ref, send_ref, rows, offset=0):
    dp_me = me_ref[0]
    seq_me = me_ref[1]
    for i, (dp, seq) in enumerate(pieces):
        tile = result[i * rows : (i + 1) * rows].astype(bf16)
        half = seq & 1
        at = plan.place(dp ^ dp_me, seq ^ seq_me, half)
        stay = half == (seq_me & 1)

        @pl.when(stay)
        def _(tile=tile, at=at):
            keep_ref[at, offset : offset + rows] = tile

        @pl.when(jnp.logical_not(stay))
        def _(tile=tile, at=at):
            send_ref[at, offset : offset + rows] = tile


def ffn_outer_grad(plan, me, active, d_outer):
    n, inner = active.shape
    width = d_outer.shape[1]
    rows = inner // (plan.ndp * plan.nseq)
    per = BLOCK // rows

    def kernel(me_ref, active_ref, d_ref, keep_ref, send_ref):
        j = pl.program_id(0)
        result = dot(active_ref[...], d_ref[...], 0, 0)
        pieces = [((j * per + i) // plan.nseq, (j * per + i) % plan.nseq) for i in range(per)]
        scatter_pieces(plan, me_ref, result, pieces, keep_ref, send_ref, rows)

    shape = jax.ShapeDtypeStruct((plan.places, rows, width), bf16)
    spec = pl.BlockSpec(shape.shape, lambda j, m: (0, 0, 0))
    return pl.pallas_call(
        kernel,
        grid_spec=pltpu.PrefetchScalarGridSpec(
            num_scalar_prefetch=1,
            grid=(inner // BLOCK,),
            in_specs=[
                pl.BlockSpec((n, BLOCK), lambda j, m: (0, j)),
                pl.BlockSpec((n, width), lambda j, m: (0, 0)),
            ],
            out_specs=[spec, spec],
        ),
        out_shape=[shape, shape],
        name="outer_grad",
    )(me, active, d_outer)


def ffn_backward(plan, me, slope, d_outer, wo, wi, n1t, d_resid2, hat1, inv1, gain1, wout):
    n, inner = slope.shape
    width = d_outer.shape[1]
    rows = width // plan.ndp
    cols = inner // plan.nseq

    def kernel(
        me_ref, slope_ref, douter_ref, wo_ref, wi_ref, n1t_ref, dres2_ref, hat1_ref, inv1_ref, gain_ref, wout_ref,
        keep_ref, send_ref, dres1_ref, dattn_ref, dctx_ref, ib_ref, small_ref, acc,
    ):
        j = pl.program_id(0)
        d_active = dot(douter_ref[...], wo_ref[...], 1, 1)
        d_inner = (d_active * slope_ref[...].astype(f32)).astype(bf16)
        ib_ref[...] = jnp.broadcast_to(jnp.sum(d_inner.astype(f32), axis=0, keepdims=True), ib_ref.shape)
        result = dot(n1t_ref[...], d_inner, 1, 0)
        scatter_pieces(plan, me_ref, result, [(i, j) for i in range(plan.ndp)], keep_ref, send_ref, rows)
        back = dot(d_inner, wi_ref[...], 1, 1)

        @pl.when(j == 0)
        def _():
            acc[...] = dres2_ref[...] + back

        @pl.when(j > 0)
        def _():
            acc[...] += back

        @pl.when(j == pl.num_programs(0) - 1)
        def _():
            d_normed = acc[...]
            hat = hat1_ref[...]
            dres = normalize_back(hat, inv1_ref[:, 0:1], d_normed * gain_ref[...])
            dres1_ref[...] = dres
            low = dres.astype(bf16)
            dattn_ref[...] = low
            dctx_ref[...] = dot(low, wout_ref[...], 1, 1).astype(bf16)
            small_ref[...] = rows_of(d_normed * hat, d_normed, low.astype(f32))

    full = lambda a: pl.BlockSpec(a.shape, lambda j, m: (0,) * a.ndim)
    whole = lambda shape: pl.BlockSpec(shape, lambda j, m: (0,) * len(shape))
    chunk = jax.ShapeDtypeStruct((plan.places, rows, cols), bf16)
    return pl.pallas_call(
        kernel,
        grid_spec=pltpu.PrefetchScalarGridSpec(
            num_scalar_prefetch=1,
            grid=(plan.nseq,),
            in_specs=[
                pl.BlockSpec((n, cols), lambda j, m: (0, j)),
                full(d_outer),
                pl.BlockSpec((cols, width), lambda j, m: (j, 0)),
                pl.BlockSpec((width, cols), lambda j, m: (0, j)),
                full(n1t),
                full(d_resid2),
                full(hat1),
                full(inv1),
                full(gain1),
                full(wout),
            ],
            out_specs=[
                whole(chunk.shape),
                whole(chunk.shape),
                whole((n, width)),
                whole((n, width)),
                whole((n, width)),
                pl.BlockSpec((8, cols), lambda j, m: (0, j)),
                whole((8, width)),
            ],
            scratch_shapes=[pltpu.VMEM((n, width), f32)],
        ),
        out_shape=[
            chunk,
            chunk,
            jax.ShapeDtypeStruct((n, width), f32),
            jax.ShapeDtypeStruct((n, width), bf16),
            jax.ShapeDtypeStruct((n, width), bf16),
            jax.ShapeDtypeStruct((8, inner), f32),
            jax.ShapeDtypeStruct((8, width), f32),
        ],
        name="ffn_bwd",
    )(me, slope, d_outer, wo, wi, n1t, d_resid2, hat1, inv1, gain1, wout)


def attn_weight_grads(plan, me, flat, ctx, grads, small):
    n, width = flat.shape
    rows = width // plan.ndp

    def kernel(me_ref, flat_ref, ctx_ref, d0_ref, d1_ref, d2_ref, d3_ref, small_ref, keep_ref, send_ref, flat_t, ctx_t):
        flat_t[...] = flat_ref[...].T
        ctx_t[...] = ctx_ref[...].T
        for s, d_ref in enumerate((d0_ref, d1_ref, d2_ref, d3_ref)):
            left = ctx_t if s == 3 else flat_t
            result = dot(left[...], d_ref[...], 1, 0)
            pieces = [(i, s) for i in range(plan.ndp)]
            scatter_pieces(plan, me_ref, result, pieces, keep_ref, send_ref, rows)
            below = jnp.concatenate([small_ref[s].astype(bf16)] * plan.ndp, axis=0)
            scatter_pieces(plan, me_ref, below, pieces, keep_ref, send_ref, EXTRA, rows)

    shape = jax.ShapeDtypeStruct((plan.places, rows + EXTRA, width), bf16)
    return pl.pallas_call(
        kernel,
        in_specs=[pl.BlockSpec(memory_space=pltpu.SMEM)] + [pl.BlockSpec(memory_space=pltpu.VMEM)] * 7,
        out_specs=[pl.BlockSpec(memory_space=pltpu.VMEM)] * 2,
        out_shape=[shape, shape],
        scratch_shapes=[pltpu.VMEM((width, n), bf16), pltpu.VMEM((width, n), bf16)],
        name="attn_grad",
    )(me, flat, ctx, *grads, small)


def place_pieces(plan, me, blocks):
    dp = jnp.repeat(jnp.arange(plan.ndp), plan.nseq)
    seq = jnp.tile(jnp.arange(plan.nseq), plan.ndp)
    half = seq & 1
    place = plan.place(dp ^ me[0], seq ^ me[1], half)
    away = half ^ (me[1] & 1)
    flat = blocks.reshape((plan.ndp * plan.nseq,) + blocks.shape[2:])
    order = jnp.zeros((2 * plan.places,), jnp.int32).at[away * plan.places + place].set(jnp.arange(dp.shape[0]))
    both = jnp.take(flat, order, axis=0)
    return both[: plan.places], both[plan.places :]


def make_per_device(mesh):
    plan = Plan(mesh)
    ndp, nseq = plan.ndp, plan.nseq
    devices = ("dp", "seq")

    def total_of(terms):
        total = terms[0].astype(f32)
        for t in terms[1:]:
            total = total + t.astype(f32)
        return total

    def start_chunk(keep, send):
        return [keep, lax.ppermute(send, devices, plan.perm(-1))]

    def step_chunk(terms, step):
        half = terms[0].shape[0] // 2
        send = total_of([t[half:] for t in terms]).astype(bf16)
        got = lax.ppermute(send, devices, plan.perm(step))
        return [t[:half] for t in terms] + [got]

    def swap_seq(x, k):
        return lax.ppermute(x, "seq", [(i, i ^ k) for i in range(nseq)])

    def gather_seq(x):
        x = x[None]
        for b in reversed(range(nseq.bit_length() - 1)):
            x = jnp.concatenate([x, lax.ppermute(x, "seq", [(i, i ^ (1 << b)) for i in range(nseq)])], axis=0)
        count = nseq.bit_length() - 1
        order = []
        for k in range(nseq):
            pos = 0
            for b in range(count):
                pos |= ((k >> b) & 1) << (count - 1 - b)
            order.append(pos)
        return [x[p] for p in order]

    def per_device(
        tokens,
        memory_init,
        query_weight,
        query_bias,
        key_weight,
        value_weight,
        value_bias,
        output_weight,
        output_bias,
        attn_gain,
        attn_shift,
        inner_weight,
        inner_bias,
        outer_weight,
        outer_bias,
        ffn_gain,
        ffn_shift,
        out_grad,
        lm_mask,
        doc_segments,
    ):
        seg_dev, rows_dev, width = tokens.shape
        assert seg_dev == nseq
        rows = rows_dev * nseq
        assert rows < (1 << DIGITS) and ndp * nseq <= 256
        mem_rows = memory_init.shape[1]
        ff = inner_weight.shape[1]
        seq_index = lax.axis_index("seq")
        dp_index = lax.axis_index("dp")
        segs_total = ndp * seg_dev

        def to_segments(x):
            pieces = []
            for k in range(nseq):
                piece = lax.dynamic_index_in_dim(x, seq_index ^ k, axis=0, keepdims=False)
                pieces.append(swap_seq(piece, k) if k else piece)
            return pieces

        def to_rows(pieces, finish):
            out = None
            for k in range(nseq):
                piece = finish(pieces[k])
                if out is None:
                    out = jnp.zeros((nseq,) + piece.shape, piece.dtype)
                out = lax.dynamic_update_index_in_dim(out, piece, seq_index ^ k, axis=0)
            return out

        source = seq_index ^ jnp.arange(nseq, dtype=jnp.int32)
        position = source[:, None] * rows_dev + jnp.arange(rows_dev, dtype=jnp.int32)[None, :]
        is_mem = (position < mem_rows).reshape(rows)
        raw = jnp.concatenate(to_segments(tokens), axis=0)

        here = seq_index * rows_dev + jnp.arange(rows_dev, dtype=jnp.int32)
        valid = jnp.where((here < mem_rows)[None, :], 0, lm_mask)
        counts_here = jnp.sum(valid, axis=1)
        masked = jnp.where(valid[..., None] != 0, out_grad, jnp.zeros_like(out_grad))
        assert rows_dev <= 256
        count_rows = jnp.broadcast_to(counts_here.astype(bf16)[:, None, None], (seg_dev, EXTRA, width))
        cot_pieces = to_segments(jnp.concatenate([masked, count_rows], axis=1))

        seg_global = dp_index * seg_dev + seq_index
        starts = jnp.cumsum(doc_segments) - doc_segments
        is_first = jnp.any(starts == seg_global)
        me = jnp.stack([dp_index, seq_index, is_first.astype(jnp.int32)]).astype(jnp.int32)
        select = (is_first & is_mem)[:, None]
        table = jnp.concatenate([memory_init.T, jnp.zeros((rows_dev - mem_rows, width), bf16)], axis=0)
        table = jnp.concatenate([table] * nseq, axis=0)
        flat = jnp.where(select, table, raw)

        queries = (dot(flat, query_weight, 1, 0) + query_bias.astype(f32)).astype(bf16)
        keys = dot(flat, key_weight, 1, 0).astype(bf16)
        values = (dot(flat, value_weight, 1, 0) + value_bias.astype(f32)).astype(bf16)
        context, probs = attention_forward(queries, keys, values, 1, rows)
        zero = jnp.zeros_like(output_bias)
        vecs = jnp.stack(
            [output_bias, attn_gain, attn_shift, outer_bias, ffn_gain, ffn_shift, zero, zero]
        ).astype(f32)
        (hat1, inv1, n1t, active, slope), out_pieces, (d_resid2, d_outer, small2) = ffn_forward(
            flat,
            context,
            output_weight,
            vecs,
            inner_weight,
            inner_bias.astype(f32)[None],
            outer_weight,
            cot_pieces,
            rows_dev,
        )
        out_pieces = [swap_seq(p, k) if k else p for k, p in enumerate(out_pieces)]
        layer_out = to_rows(out_pieces, lambda p: p)

        aligned = (width // ndp) % 16 == 0 and (ff // (ndp * nseq)) % 16 == 0 and ff // nseq == BLOCK
        if aligned:
            keep, send = ffn_outer_grad(plan, me, active, d_outer)
        else:
            grad = dot(active, d_outer, 0, 0).astype(bf16)
            keep, send = place_pieces(plan, me, grad.reshape(ndp, nseq, -1, width))
        d_outer, keep, send = lax.optimization_barrier((d_outer, keep, send))
        outer = start_chunk(keep, send)
        if aligned:
            keep, send, d_resid1, d_attn, d_context, d_inner_bias, small1 = ffn_backward(
                plan, me, slope, d_outer, outer_weight, inner_weight, n1t, d_resid2, hat1, inv1, vecs[1:2], output_weight
            )
        else:
            d_inner = (dot(d_outer, outer_weight, 1, 1) * slope.astype(f32)).astype(bf16)
            d_inner_bias = jnp.broadcast_to(jnp.sum(d_inner.astype(f32), axis=0), (8, ff))
            grad = dot(n1t, d_inner, 1, 0).astype(bf16)
            grad = grad.reshape(ndp, width // ndp, nseq, ff // nseq).transpose(0, 2, 1, 3)
            keep, send = place_pieces(plan, me, grad)
            d_normed = dot(d_inner, inner_weight, 1, 1) + d_resid2
            d_resid1 = normalize_back(hat1, inv1[:, 0:1], d_normed * vecs[1:2])
            d_attn = d_resid1.astype(bf16)
            d_context = dot(d_attn, output_weight, 1, 1).astype(bf16)
            small1 = rows_of(d_normed * hat1, d_normed, d_attn.astype(f32))
        inner = start_chunk(keep, send)
        outer = step_chunk(outer, 0)
        d_queries, d_keys, d_values = attention_backward(
            queries, keys, values, context, d_context, probs, 1, rows
        )
        outer = step_chunk(outer, 1)
        inner = step_chunk(inner, 0)
        cut_pieces, small = inputs_backward(
            me,
            (d_queries, d_keys, d_values),
            (query_weight, key_weight, value_weight),
            d_resid1,
            small1,
            small2,
            d_inner_bias,
            rows_dev,
            nseq,
            mem_rows,
        )
        cut_pieces = [swap_seq(p, k) if k else p for k, p in enumerate(cut_pieces)]
        ib_rows = ff // width
        attn_grads = (d_queries, d_keys, d_values, d_attn)
        if aligned:
            keep, send = attn_weight_grads(plan, me, flat, context, attn_grads, small)
        else:
            blocks = []
            for s, d in enumerate(attn_grads):
                left = context if s == 3 else flat
                blocks.append(dot(left, d, 0, 0).astype(bf16).reshape(ndp, -1, width))
            blocks = jnp.stack(blocks, axis=1)
            below = jnp.broadcast_to(small.astype(bf16)[None], (ndp,) + small.shape)
            keep, send = place_pieces(plan, me, jnp.concatenate([blocks, below], axis=2))
        attn = start_chunk(keep, send)
        outer = step_chunk(outer, 2)
        inner = step_chunk(inner, 1)
        for step in range(3, plan.steps):
            outer = step_chunk(outer, step)
        for step in range(2, plan.steps):
            inner = step_chunk(inner, step)
        ffn_pieces = gather_seq(jnp.concatenate([total_of(outer)[0], total_of(inner)[0]], axis=0).astype(bf16))
        for step in range(plan.steps):
            attn = step_chunk(attn, step)
        attn_pieces = gather_seq(total_of(attn)[0].astype(bf16))

        def in_order(pieces):
            stack = jnp.stack(pieces)
            return [lax.dynamic_index_in_dim(stack, seq_index ^ s, 0, keepdims=False) for s in range(nseq)]

        part = width // ndp
        attn_parts = in_order(attn_pieces)
        ffn_parts = in_order(ffn_pieces)
        weights = (2.0 ** jnp.arange(DIGITS)).astype(f32)
        total = jnp.sum(attn_parts[1][part + ib_rows, :DIGITS].astype(f32) * weights)
        factor = total / segs_total
        finish = lambda x: x.astype(f32) * factor

        tokens_grad = to_rows(cut_pieces, finish)

        outer_rows = ff // (ndp * nseq)
        g_outer = finish(jnp.concatenate([p[:outer_rows] for p in ffn_parts], axis=0))
        g_inner = finish(jnp.concatenate([p[outer_rows:] for p in ffn_parts], axis=1))
        g_query, g_key, g_value, g_output = [finish(p[:part]) for p in attn_parts[:4]]
        mine = lambda x: lax.dynamic_slice_in_dim(finish(x), dp_index * part, part, axis=1)
        vec_rows = mine(attn_parts[0][part : part + 8])
        g_memory = mine(attn_parts[2][part : part + mem_rows]).T
        inner_part = ff // ndp
        g_inner_bias = lax.dynamic_slice_in_dim(
            finish(attn_parts[1][part : part + ib_rows]).reshape(-1), dp_index * inner_part, inner_part, axis=0
        )
        g_query_bias, g_value_bias, g_gain1, g_shift1, g_output_bias, g_gain2, g_shift2, g_outer_bias = vec_rows
        return (
            layer_out,
            tokens_grad,
            g_query,
            g_query_bias,
            g_key,
            g_value,
            g_value_bias,
            g_output,
            g_output_bias,
            g_gain1,
            g_shift1,
            g_inner,
            g_inner_bias,
            g_outer,
            g_outer_bias,
            g_gain2,
            g_shift2,
            g_memory,
        )

    return per_device


def solution(mesh):
    rows = P("dp", "seq", None)
    in_specs = (rows,) + (P(),) * 16 + (rows, P("dp", "seq"), P())
    out_specs = (
        rows,
        rows,
        P("dp", None),
        P("dp"),
        P("dp", None),
        P("dp", None),
        P("dp"),
        P("dp", None),
        P("dp"),
        P("dp"),
        P("dp"),
        P("dp", None),
        P("dp"),
        P("dp", None),
        P("dp"),
        P("dp"),
        P("dp"),
        P("dp", None),
    )
    return jax.shard_map(
        make_per_device(mesh), mesh=mesh, in_specs=in_specs, out_specs=out_specs, check_vma=False
    )
```

profile of v0, /device:TPU:0, one launch (start us, length us, event | category | flops | bytes accessed | tf_op | source)
XLA Modules:
  0.0 244.1 jit_solution(17537725652306410973)
XLA Ops:
  2.6 2.6 %collective-permute-start.1 = (bf16[128,768]{1,0:T(8,128)(2,1)S(1)}, bf16[128,768]{1,0:T(8,128)(2,1)S(1)}, u32[]{:S(2)}, u32[]{:S(2)}) collective-permute-start(bf16[128,768]{1,0:T(8,128)(2,1)S(1)} %get-tuple-element.105), channel_id=1, source_target_pairs={{0,2},{1,3},{2,0},{3,1},{4,6},{5,7},{6,4},{7,5},{8,10},{9,11},{10,... | collective-permute-start | bytes 589832 | tf_op jit(solution)/shard_map/ppermute | solution.py:495
  20.0 11.4 %attn_fwd.1 = (bf16[512,768]{1,0:T(8,128)(2,1)}, bf16[12,512,512]{2,1,0:T(8,128)(2,1)}) custom-call(bf16[512,768]{1,0:T(8,128)(2,1)} %add_convert_fusion.4.q_ref, bf16[512,768]{1,0:T(8,128)(2,1)} %convolution_convert_fusion.k_ref, bf16[512,768]{1,0:T(8,128)(2,1)} %add_convert_fusion.3.v_ref), custom_call_target="tpu_custom_call" | custom-call | tf_op jit(solution)/shard_map/attn_fwd/pallas_call | solution.py:80
  32.1 21.4 %ffn_fwd.1 = (f32[512,768]{1,0:T(8,128)}, f32[512,128]{1,0:T(8,128)}, bf16[768,512]{1,0:T(8,128)(2,1)}, bf16[512,3072]{1,0:T(8,128)(2,1)}, bf16[512,3072]{1,0:T(...) custom-call(bf16[512,768]{1,0:T(8,128)(2,1)} %copy-done, ...), custom_call_target="tpu_custom_call" | custom-call | tf_op jit(solution)/shard_map/ffn_fwd/pallas_call | solution.py:211
  53.5 8.5 %outer_grad.1 = (bf16[16,96,768]{2,1,0:T(8,128)(2,1)}, bf16[16,96,768]{2,1,0:T(8,128)(2,1)}) custom-call(s32[3]{0:T(128)} %pad_add_fusion.me_ref, bf16[512,3072]{1,0:T(8,128)(2,1)} %get-tuple-element.61.active_ref, bf16[512,768]{1,0:T(8,128)(2,1)} %get-tuple-element.64.d_ref.douter_ref), custom_call_target="tpu_custom_call" | custom-call | tf_op jit(solution)/shard_map/outer_grad/pallas_call | solution.py:339
  62.8 21.7 %ffn_bwd.1 = (bf16[16,96,768]{2,1,0:T(8,128)(2,1)}, bf16[16,96,768]{2,1,0:T(8,128)(2,1)}, f32[512,768]{1,0:T(8,128)}, bf16[512,768]{1,0:T(8,128)(2,1)}, bf16[512...) custom-call(s32[3]{0:T(128)} %pad_add_fusion.me_ref, bf16[512,3072]{1,0:T(8,128)(2,1)} %get-tuple-element.59.slope_ref, ...), custom_call_target="tpu_custom_call" | custom-call | tf_op jit(solution)/shard_map/ffn_bwd/pallas_call | solution.py:395
  84.9 12.4 %attn_bwd.1 = (bf16[512,768]{1,0:T(8,128)(2,1)}, bf16[512,768]{1,0:T(8,128)(2,1)}, bf16[512,768]{1,0:T(8,128)(2,1)}) custom-call(bf16[512,768]{1,0:T(8,128)(2,1)} %add_convert_fusion.4.q_ref, bf16[512,768]{1,0:T(8,128)(2,1)} %convolution_convert_fusion.k_ref, bf16[512,768]{1,0:T(8,128)(2,1)} %add_convert_fusion.3.v_ref, ...), custom_call_target="tpu_custom_call" | custom-call | tf_op jit(solution)/shard_map/attn_bwd/pallas_call | solution.py:99
  97.3 6.3 %inputs_bwd.1 = (bf16[128,768]{1,0:T(8,128)(2,1)}, bf16[128,768]{1,0:T(8,128)(2,1)}, bf16[128,768]{1,0:T(8,128)(2,1)}, bf16[128,768]{1,0:T(8,128)(2,1)}, f32[4,16,768]{2,1,0:T(8,128)}) custom-call(s32[3]{0:T(128)} %pad_add_fusion.me_ref, bf16[512,768]{1,0:T(8,128)(2,1)} %get-tuple-element.71.dq_ref.d0_ref, bf16[512,768]{1,0:T(8,128)(2,1)} %get-tuple-element.72.dk_ref.d1_ref, ...), custom_call_target="tpu_custom_call" | custom-call | tf_op jit(solution)/shard_map/inputs_bwd/pallas_call | solution.py:263
  103.6 10.0 %attn_grad.1 = (bf16[16,112,768]{2,1,0:T(8,128)(2,1)}, bf16[16,112,768]{2,1,0:T(8,128)(2,1)}) custom-call(s32[3]{0:T(128)} %pad_add_fusion.me_ref, bf16[512,768]{1,0:T(8,128)(2,1)} %copy-done, bf16[512,768]{1,0:T(8,128)(2,1)} %get-tuple-element.54.ctx_ref, bf16[512,768]{1,0:T(8,128)(2,1)} %get-tuple-element.71.dq_ref.d0_ref, ...), custom_call_target="tpu_custom_call" | custom-call | tf_op jit(solution)/shard_map/attn_grad/pallas_call | solution.py:452
  113.9 2.7 %add_convert_fusion.2 = bf16[8,96,768]{2,1,0:T(8,128)(2,1)} fusion(bf16[16,96,768]{2,1,0:T(8,128)(2,1)} %collective-permute-done.19, bf16[16,96,768]{2,1,0:T(8,128)(2,1)S(1)} %copy-done.4), kind=kLoop, calls=%fused_computation.2 | loop fusion | flops 2359296 | bytes 3538944 | tf_op jit(solution)/shard_map/convert_element_type | solution.py:490
  116.5 2.1 collective-permute-start.20
  118.7 2.7 %add_convert_fusion.1 = bf16[8,96,768]{2,1,0:T(8,128)(2,1)} fusion(bf16[16,96,768]{2,1,0:T(8,128)(2,1)} %collective-permute-done.24, bf16[16,96,768]{2,1,0:T(8,128)(2,1)S(1)} %copy-done.2), kind=kLoop, calls=%fused_computation.1 | loop fusion | flops 2359296 | bytes 3538944 | tf_op jit(solution)/shard_map/convert_element_type | solution.py:490
  123.8 2.1 collective-permute-start.10
  125.9 7.3 %collective-permute-done.20 = bf16[8,96,768]{2,1,0:T(8,128)(2,1)} collective-permute-done((bf16[8,96,768]{2,1,0:T(8,128)(2,1)}, bf16[8,96,768]{2,1,0:T(8,128)(2,1)}, u32[]{:S(2)}, u32[]{:S(2)}) %collective-permute-start.20) | collective-permute-done | bytes 1179680 | tf_op jit(solution)/shard_map/ppermute | solution.py:491
  136.7 15.4 %collective-permute-done.25 = bf16[8,96,768]{2,1,0:T(8,128)(2,1)} collective-permute-done((bf16[8,96,768]{2,1,0:T(8,128)(2,1)}, bf16[8,96,768]{2,1,0:T(8,128)(2,1)}, u32[]{:S(2)}, u32[]{:S(2)}) %collective-permute-start.25) | collective-permute-done | bytes 1179680 | tf_op jit(solution)/shard_map/ppermute | solution.py:491
  158.7 11.2 %collective-permute-done.26 = bf16[4,96,768]{2,1,0:T(8,128)(2,1)S(1)} collective-permute-done((bf16[4,96,768]{2,1,0:T(8,128)(2,1)S(1)}, bf16[4,96,768]{2,1,0:T(8,128)(2,1)S(1)}, u32[]{:S(2)}, u32[]{:S(2)}) %collective-permute-start.26) | collective-permute-done | bytes 589856 | tf_op jit(solution)/shard_map/ppermute | solution.py:491
  173.1 4.2 %collective-permute-done.10 = bf16[8,112,768]{2,1,0:T(8,128)(2,1)S(1)} collective-permute-done((bf16[8,112,768]{2,1,0:T(8,128)(2,1)S(1)}, bf16[8,112,768]{2,1,0:T(8,128)(2,1)S(1)}, u32[]{:S(2)}, u32[]{:S(2)}) %collective-permute-start.10) | collective-permute-done | bytes 1376288 | tf_op jit(solution)/shard_map/ppermute | solution.py:491
  177.3 2.1 collective-permute-start.27
  184.1 4.1 %collective-permute-start.23 = (bf16[1,96,768]{2,1,0:T(8,128)(2,1)S(1)}, bf16[1,96,768]{2,1,0:T(8,128)(2,1)S(1)}, u32[]{:S(2)}, u32[]{:S(2)}) collective-permute-start(bf16[1,96,768]{2,1,0:T(8,128)(2,1)S(1)} %add_convert_fusion.16), channel_id=1, source_target_pairs={{0,16},{1,17},{2,18},{3,19},{4,20},{5,21},{6,22},{7,23},{8,24},{9,... | collective-permute-start | bytes 442376 | tf_op jit(solution)/shard_map/ppermute | solution.py:491
  189.2 3.6 %collective-permute-done.23 = bf16[1,96,768]{2,1,0:T(8,128)(2,1)S(1)} collective-permute-done((bf16[1,96,768]{2,1,0:T(8,128)(2,1)S(1)}, bf16[1,96,768]{2,1,0:T(8,128)(2,1)S(1)}, u32[]{:S(2)}, u32[]{:S(2)}) %collective-permute-start.23) | collective-permute-done | bytes 147488 | tf_op jit(solution)/shard_map/ppermute | solution.py:491
  198.2 5.1 %collective-permute-done.28 = bf16[1,96,768]{2,1,0:T(8,128)(2,1)S(1)} collective-permute-done((bf16[1,96,768]{2,1,0:T(8,128)(2,1)S(1)}, bf16[1,96,768]{2,1,0:T(8,128)(2,1)S(1)}, u32[]{:S(2)}, u32[]{:S(2)}) %collective-permute-start.28) | collective-permute-done | bytes 147488 | tf_op jit(solution)/shard_map/ppermute | solution.py:491
  204.5 7.7 %collective-permute-done.12 = bf16[2,112,768]{2,1,0:T(8,128)(2,1)S(1)} collective-permute-done((bf16[2,112,768]{2,1,0:T(8,128)(2,1)S(1)}, bf16[2,112,768]{2,1,0:T(8,128)(2,1)S(1)}, u32[]{:S(2)}, u32[]{:S(2)}) %collective-permute-start.12) | collective-permute-done | bytes 344096 | tf_op jit(solution)/shard_map/ppermute | solution.py:491
  214.5 4.5 %collective-permute-done.29 = bf16[1,192,768]{2,1,0:T(8,128)(2,1)S(1)} collective-permute-done((bf16[1,192,768]{2,1,0:T(8,128)(2,1)S(1)}, bf16[1,192,768]{2,1,0:T(8,128)(2,1)S(1)}, u32[]{:S(2)}, u32[]{:S(2)}) %collective-permute-start.29) | collective-permute-done | bytes 294944 | tf_op jit(solution)/shard_map/ppermute | solution.py:500
  222.2 3.2 %collective-permute-done.8 = bf16[128,768]{1,0:T(8,128)(2,1)S(1)} collective-permute-done((bf16[128,768]{1,0:T(8,128)(2,1)S(1)}, bf16[128,768]{1,0:T(8,128)(2,1)S(1)}, u32[]{:S(2)}, u32[]{:S(2)}) %collective-permute-start.8) | collective-permute-done | bytes 196640 | tf_op jit(solution)/shard_map/ppermute | solution.py:495
  226.8 4.6 %collective-permute-done.14 = bf16[1,112,768]{2,1,0:T(8,128)(2,1)S(1)} collective-permute-done((bf16[1,112,768]{2,1,0:T(8,128)(2,1)S(1)}, bf16[1,112,768]{2,1,0:T(8,128)(2,1)S(1)}, u32[]{:S(2)}, u32[]{:S(2)}) %collective-permute-start.14) | collective-permute-done | bytes 172064 | tf_op jit(solution)/shard_map/ppermute | solution.py:500
  (187 shorter events, 64.5 us)
Async XLA Ops:
  2.0 12.2 %collective-permute-start = (bf16[128,768]{1,0:T(8,128)(2,1)S(1)}, bf16[128,768]{1,0:T(8,128)(2,1)S(1)}, u32[]{:S(2)}, u32[]{:S(2)}) collective-permute-start(bf16[128,768]{1,0:T(8,128)(2,1)S(1)} %get-tuple-element.103), channel_id=1, source_target_pairs={{0,1},{1,0},{2,3},{3,2},{4,5},{5,4},{6,7},{7,6},{8,9},{9,8},{10,11... | collective-permute-start | bytes 589832 | tf_op jit(solution)/shard_map/ppermute | solution.py:495
  2.6 11.7 %collective-permute-start.1 = (bf16[128,768]{1,0:T(8,128)(2,1)S(1)}, bf16[128,768]{1,0:T(8,128)(2,1)S(1)}, u32[]{:S(2)}, u32[]{:S(2)}) collective-permute-start(bf16[128,768]{1,0:T(8,128)(2,1)S(1)} %get-tuple-element.105), channel_id=1, source_target_pairs={{0,2},{1,3},{2,0},{3,1},{4,6},{5,7},{6,4},{7,5},{8,10},{9,11},{10,... | collective-permute-start | bytes 589832 | tf_op jit(solution)/shard_map/ppermute | solution.py:495
  5.2 9.5 %collective-permute-start.2 = (bf16[128,768]{1,0:T(8,128)(2,1)S(1)}, bf16[128,768]{1,0:T(8,128)(2,1)S(1)}, u32[]{:S(2)}, u32[]{:S(2)}) collective-permute-start(bf16[128,768]{1,0:T(8,128)(2,1)S(1)} %get-tuple-element.104), channel_id=1, source_target_pairs={{0,3},{1,2},{2,1},{3,0},{4,7},{5,6},{6,5},{7,4},{8,11},{9,10},{10,... | collective-permute-start | bytes 589832 | tf_op jit(solution)/shard_map/ppermute | solution.py:495
  6.6 24.7 %collective-permute-start.3 = (bf16[144,768]{1,0:T(8,128)(2,1)}, bf16[144,768]{1,0:T(8,128)(2,1)S(1)}, u32[]{:S(2)}, u32[]{:S(2)}) collective-permute-start(bf16[144,768]{1,0:T(8,128)(2,1)} %get-tuple-element.100), channel_id=1, source_target_pairs={{0,1},{1,0},{2,3},{3,2},{4,5},{5,4},{6,7},{7,6},{8,9},{9,8},{10,11... | collective-permute-start | bytes 663560 | tf_op jit(solution)/shard_map/ppermute | solution.py:495
  6.8 24.6 %collective-permute-start.4 = (bf16[144,768]{1,0:T(8,128)(2,1)}, bf16[144,768]{1,0:T(8,128)(2,1)}, u32[]{:S(2)}, u32[]{:S(2)}) collective-permute-start(bf16[144,768]{1,0:T(8,128)(2,1)} %get-tuple-element.101), channel_id=1, source_target_pairs={{0,2},{1,3},{2,0},{3,1},{4,6},{5,7},{6,4},{7,5},{8,10},{9,11},{10,... | collective-permute-start | bytes 663560 | tf_op jit(solution)/shard_map/ppermute | solution.py:495
  14.2 17.2 %collective-permute-start.5 = (bf16[144,768]{1,0:T(8,128)(2,1)}, bf16[144,768]{1,0:T(8,128)(2,1)}, u32[]{:S(2)}, u32[]{:S(2)}) collective-permute-start(bf16[144,768]{1,0:T(8,128)(2,1)} %get-tuple-element.98), channel_id=1, source_target_pairs={{0,3},{1,2},{2,1},{3,0},{4,7},{5,6},{6,5},{7,4},{8,11},{9,10},{10,... | collective-permute-start | bytes 663560 | tf_op jit(solution)/shard_map/ppermute | solution.py:495
  62.0 51.9 %collective-permute-start.19 = (bf16[16,96,768]{2,1,0:T(8,128)(2,1)}, bf16[16,96,768]{2,1,0:T(8,128)(2,1)}, u32[]{:S(2)}, u32[]{:S(2)}) collective-permute-start(bf16[16,96,768]{2,1,0:T(8,128)(2,1)} %get-tuple-element.87), channel_id=1, source_target_pairs={{0,1},{1,0},{2,3},{3,2},{4,5},{5,4},{6,7},{7,6},{8,9},{9,8},{10,11... | collective-permute-start | bytes 7077896 | tf_op jit(solution)/shard_map/ppermute | solution.py:486
  84.6 34.1 %collective-permute-start.24 = (bf16[16,96,768]{2,1,0:T(8,128)(2,1)}, bf16[16,96,768]{2,1,0:T(8,128)(2,1)}, u32[]{:S(2)}, u32[]{:S(2)}) collective-permute-start(bf16[16,96,768]{2,1,0:T(8,128)(2,1)} %get-tuple-element.89), channel_id=1, source_target_pairs={{0,1},{1,0},{2,3},{3,2},{4,5},{5,4},{6,7},{7,6},{8,9},{9,8},{10,11... | collective-permute-start | bytes 7077896 | tf_op jit(solution)/shard_map/ppermute | solution.py:486
  113.6 8.3 %collective-permute-start.9 = (bf16[16,112,768]{2,1,0:T(8,128)(2,1)}, bf16[16,112,768]{2,1,0:T(8,128)(2,1)}, u32[]{:S(2)}, u32[]{:S(2)}) collective-permute-start(bf16[16,112,768]{2,1,0:T(8,128)(2,1)} %get-tuple-element.82), channel_id=1, source_target_pairs={{0,1},{1,0},{2,3},{3,2},{4,5},{5,4},{6,7},{7,6},{8,9},{9,8},{10,11... | collective-permute-start | bytes 8257544 | tf_op jit(solution)/shard_map/ppermute | solution.py:486
  116.5 16.6 %collective-permute-start.20 = (bf16[8,96,768]{2,1,0:T(8,128)(2,1)}, bf16[8,96,768]{2,1,0:T(8,128)(2,1)}, u32[]{:S(2)}, u32[]{:S(2)}) collective-permute-start(bf16[8,96,768]{2,1,0:T(8,128)(2,1)} %add_convert_fusion.2), channel_id=1, source_target_pairs={{0,2},{1,5},{2,0},{3,7},{4,6},{5,1},{6,4},{7,3},{8,10},{9,13},{10,... | collective-permute-start | bytes 3538952 | tf_op jit(solution)/shard_map/ppermute | solution.py:491
  121.4 30.7 %collective-permute-start.25 = (bf16[8,96,768]{2,1,0:T(8,128)(2,1)}, bf16[8,96,768]{2,1,0:T(8,128)(2,1)}, u32[]{:S(2)}, u32[]{:S(2)}) collective-permute-start(bf16[8,96,768]{2,1,0:T(8,128)(2,1)} %add_convert_fusion.1), channel_id=1, source_target_pairs={{0,2},{1,5},{2,0},{3,7},{4,6},{5,1},{6,4},{7,3},{8,10},{9,13},{10,... | collective-permute-start | bytes 3538952 | tf_op jit(solution)/shard_map/ppermute | solution.py:491
  121.4 118.0 %collective-permute-start.16 = (bf16[128,768]{1,0:T(8,128)(2,1)S(1)}, bf16[128,768]{1,0:T(8,128)(2,1)}, u32[]{:S(2)}, u32[]{:S(2)}) collective-permute-start(bf16[128,768]{1,0:T(8,128)(2,1)S(1)} %copy-done.29), channel_id=1, source_target_pairs={{0,1},{1,0},{2,3},{3,2},{4,5},{5,4},{6,7},{7,6},{8,9},{9,8},{10,11... | collective-permute-start | bytes 589832 | tf_op jit(solution)/shard_map/ppermute | solution.py:495
  121.4 34.3 %collective-permute-start.6 = (bf16[128,768]{1,0:T(8,128)(2,1)S(1)}, bf16[128,768]{1,0:T(8,128)(2,1)S(1)}, u32[]{:S(2)}, u32[]{:S(2)}) collective-permute-start(bf16[128,768]{1,0:T(8,128)(2,1)S(1)} %copy-done.32), channel_id=1, source_target_pairs={{0,1},{1,0},{2,3},{3,2},{4,5},{5,4},{6,7},{7,6},{8,9},{9,8},{10,11... | collective-permute-start | bytes 589832 | tf_op jit(solution)/shard_map/ppermute | solution.py:495
  123.8 53.5 %collective-permute-start.10 = (bf16[8,112,768]{2,1,0:T(8,128)(2,1)S(1)}, bf16[8,112,768]{2,1,0:T(8,128)(2,1)S(1)}, u32[]{:S(2)}, u32[]{:S(2)}) collective-permute-start(bf16[8,112,768]{2,1,0:T(8,128)(2,1)S(1)} %add_convert_fusion), channel_id=1, source_target_pairs={{0,2},{1,5},{2,0},{3,7},{4,6},{5,1},{6,4},{7,3},{8,10},{9,13},{10,... | collective-permute-start | bytes 4128776 | tf_op jit(solution)/shard_map/ppermute | solution.py:491
  134.6 22.7 %collective-permute-start.21 = (bf16[4,96,768]{2,1,0:T(8,128)(2,1)S(1)}, bf16[4,96,768]{2,1,0:T(8,128)(2,1)S(1)}, u32[]{:S(2)}, u32[]{:S(2)}) collective-permute-start(bf16[4,96,768]{2,1,0:T(8,128)(2,1)S(1)} %add_convert_fusion.7), channel_id=1, source_target_pairs={{0,4},{1,3},{2,6},{3,1},{4,0},{5,7},{6,2},{7,5},{8,12},{9,11},{10,... | collective-permute-start | bytes 1769480 | tf_op jit(solution)/shard_map/ppermute | solution.py:491
  153.6 16.3 %collective-permute-start.26 = (bf16[4,96,768]{2,1,0:T(8,128)(2,1)S(1)}, bf16[4,96,768]{2,1,0:T(8,128)(2,1)S(1)}, u32[]{:S(2)}, u32[]{:S(2)}) collective-permute-start(bf16[4,96,768]{2,1,0:T(8,128)(2,1)S(1)} %add_convert_fusion.6), channel_id=1, source_target_pairs={{0,4},{1,3},{2,6},{3,1},{4,0},{5,7},{6,2},{7,5},{8,12},{9,11},{10,... | collective-permute-start | bytes 1769480 | tf_op jit(solution)/shard_map/ppermute | solution.py:491
  155.7 84.7 %collective-permute-start.17 = (bf16[128,768]{1,0:T(8,128)(2,1)S(1)}, bf16[128,768]{1,0:T(8,128)(2,1)}, u32[]{:S(2)}, u32[]{:S(2)}) collective-permute-start(bf16[128,768]{1,0:T(8,128)(2,1)S(1)} %copy-done.28), channel_id=1, source_target_pairs={{0,2},{1,3},{2,0},{3,1},{4,6},{5,7},{6,4},{7,5},{8,10},{9,11},{10,... | collective-permute-start | bytes 589832 | tf_op jit(solution)/shard_map/ppermute | solution.py:495
  157.4 84.6 %collective-permute-start.18 = (bf16[128,768]{1,0:T(8,128)(2,1)S(1)}, bf16[128,768]{1,0:T(8,128)(2,1)}, u32[]{:S(2)}, u32[]{:S(2)}) collective-permute-start(bf16[128,768]{1,0:T(8,128)(2,1)S(1)} %copy-done.27), channel_id=1, source_target_pairs={{0,3},{1,2},{2,1},{3,0},{4,7},{5,6},{6,5},{7,4},{8,11},{9,10},{10,... | collective-permute-start | bytes 589832 | tf_op jit(solution)/shard_map/ppermute | solution.py:495
  169.8 10.9 %collective-permute-start.22 = (bf16[2,96,768]{2,1,0:T(8,128)(2,1)S(1)}, bf16[2,96,768]{2,1,0:T(8,128)(2,1)S(1)}, u32[]{:S(2)}, u32[]{:S(2)}) collective-permute-start(bf16[2,96,768]{2,1,0:T(8,128)(2,1)S(1)} %add_convert_fusion.10), channel_id=1, source_target_pairs={{0,8},{1,9},{2,10},{3,11},{4,12},{5,13},{6,14},{7,15},{8,0},{9,1},... | collective-permute-start | bytes 884744 | tf_op jit(solution)/shard_map/ppermute | solution.py:491
  180.7 14.7 %collective-permute-start.11 = (bf16[4,112,768]{2,1,0:T(8,128)(2,1)S(1)}, bf16[4,112,768]{2,1,0:T(8,128)(2,1)S(1)}, u32[]{:S(2)}, u32[]{:S(2)}) collective-permute-start(bf16[4,112,768]{2,1,0:T(8,128)(2,1)S(1)} %add_convert_fusion.5), channel_id=1, source_target_pairs={{0,4},{1,3},{2,6},{3,1},{4,0},{5,7},{6,2},{7,5},{8,12},{9,11},{10,... | collective-permute-start | bytes 2064392 | tf_op jit(solution)/shard_map/ppermute | solution.py:491
  184.1 8.8 %collective-permute-start.23 = (bf16[1,96,768]{2,1,0:T(8,128)(2,1)S(1)}, bf16[1,96,768]{2,1,0:T(8,128)(2,1)S(1)}, u32[]{:S(2)}, u32[]{:S(2)}) collective-permute-start(bf16[1,96,768]{2,1,0:T(8,128)(2,1)S(1)} %add_convert_fusion.16), channel_id=1, source_target_pairs={{0,16},{1,17},{2,18},{3,19},{4,20},{5,21},{6,22},{7,23},{8,24},{9,... | collective-permute-start | bytes 442376 | tf_op jit(solution)/shard_map/ppermute | solution.py:491
  192.8 21.1 %collective-permute-start.7 = (bf16[128,768]{1,0:T(8,128)(2,1)S(1)}, bf16[128,768]{1,0:T(8,128)(2,1)S(1)}, u32[]{:S(2)}, u32[]{:S(2)}) collective-permute-start(bf16[128,768]{1,0:T(8,128)(2,1)S(1)} %copy-done.31), channel_id=1, source_target_pairs={{0,2},{1,3},{2,0},{3,1},{4,6},{5,7},{6,4},{7,5},{8,10},{9,11},{10,... | collective-permute-start | bytes 589832 | tf_op jit(solution)/shard_map/ppermute | solution.py:495
  203.2 9.0 %collective-permute-start.12 = (bf16[2,112,768]{2,1,0:T(8,128)(2,1)S(1)}, bf16[2,112,768]{2,1,0:T(8,128)(2,1)S(1)}, u32[]{:S(2)}, u32[]{:S(2)}) collective-permute-start(bf16[2,112,768]{2,1,0:T(8,128)(2,1)S(1)} %add_convert_fusion.8), channel_id=1, source_target_pairs={{0,8},{1,9},{2,10},{3,11},{4,12},{5,13},{6,14},{7,15},{8,0},{9,1},... | collective-permute-start | bytes 1032200 | tf_op jit(solution)/shard_map/ppermute | solution.py:491
  221.1 10.5 %collective-permute-start.30 = (bf16[2,192,768]{2,1,0:T(8,128)(2,1)S(1)}, bf16[2,192,768]{2,1,0:T(8,128)(2,1)S(1)}, u32[]{:S(2)}, u32[]{:S(2)}) collective-permute-start(bf16[2,192,768]{2,1,0:T(8,128)(2,1)S(1)} %pad_maximum_fusion.2), channel_id=1, source_target_pairs={{0,1},{1,0},{2,3},{3,2},{4,5},{5,4},{6,7},{7,6},{8,9},{9,8},{10,11... | collective-permute-start | bytes 1769480 | tf_op jit(solution)/shard_map/ppermute | solution.py:500
  (40 other events, 272.6 us)
where the time goes:
time: 245 us; the launch traced here: 244 us
  Pallas kernels  91.8 us (37%)
  waiting for transfers between devices  71.2 us (29%)
  other arithmetic  34.2 us (14%)
  starting transfers between devices  32.2 us (13%)
  local copies, waits for them, and re-layouts  6.91 us (3%)
  matrix products  5.03 us (2%)
  between operations  2.71 us (1%)
    ppermute x12, waiting for transfers between devices, step_chunk(): got = lax.ppermute(send, devices, plan.perm(step))  57.1 us
    pallas_call x1, Pallas kernels, ffn_backward(): pl.pallas_call(kernel, grid_spec=pltpu.PrefetchScalarGridSpec(num_scalar_...  21.7 us
    pallas_call x1, Pallas kernels, ffn_forward(): pl.pallas_call(kernel, grid=(inner // BLOCK,), in_specs=[full(flat), full...  21.4 us
    ppermute x12, starting transfers between devices, step_chunk(): got = lax.ppermute(send, devices, plan.perm(step))  20.3 us
    convert_element_type x12, other arithmetic, step_chunk(): send = total_of([t[half:] for t in terms]).astype(bf16)  18.4 us
    pallas_call x1, Pallas kernels, attention_backward(): pl.pallas_call(attn_bwd_kernel, grid=(segs, pairs), in_specs=[spec] * 5 +...  12.4 us
    pallas_call x1, Pallas kernels, attention_forward(): pl.pallas_call(attn_fwd_kernel, grid=(segs, pairs), in_specs=[spec, spec,...  11.4 us
    ppermute x4, waiting for transfers between devices, gather_seq(): lax.ppermute(x, 'seq', [(i, i ^ 1 << b) for i in range(nseq)])  10.5 us
  transfers between devices with their start and end apart: 31, of which 14 were waited for; matrix products, arithmetic and copies ran while one was open for 17% of the time, Pallas kernels for 25%

commit v1 on v0

--- a/solution.py
+++ b/solution.py
@@ -10,7 +10,6 @@
 EPS = 1e-06
 LOG2E = 1.4426950408889634
 BLOCK = 768
-DIGITS = 16
 EXTRA = 16
 f32 = jnp.float32
 bf16 = jnp.bfloat16
@@ -193,7 +192,7 @@
                 douter_ref[part] = low_d
                 for i, v in enumerate((cot * hat, cot, low_d.astype(f32))):
                     lines[i] = lines[i] + jnp.sum(v, axis=0, keepdims=True)
-            for i, v in enumerate(lines + [valid_rows]):
+            for i, v in enumerate(lines):
                 small_ref[i : i + 1] = v
 
     full = lambda a: pl.BlockSpec(a.shape, lambda j: (0,) * a.ndim)
@@ -254,9 +253,6 @@
         small_ref[0, 5:8] = s2_ref[0:3]
         for r in range(ib_rows):
             small_ref[1, r : r + 1] = ib_ref[0:1, r * width : (r + 1) * width]
-        lane = lax.broadcasted_iota(jnp.int32, (1, width), 1)
-        bits = (s2_ref[3:4].astype(jnp.int32) >> jnp.minimum(lane, DIGITS)) & 1
-        small_ref[1, ib_rows : ib_rows + 1] = bits.astype(f32)
         small_ref[2] = memory
 
     vmem = pl.BlockSpec(memory_space=pltpu.VMEM)
@@ -352,22 +348,19 @@
     )(me, active, d_outer)
 
 
-def ffn_backward(plan, me, slope, d_outer, wo, wi, n1t, d_resid2, hat1, inv1, gain1, wout):
+def ffn_backward(slope, d_outer, wo, wi, d_resid2, hat1, inv1, gain1, wout):
     n, inner = slope.shape
     width = d_outer.shape[1]
-    rows = width // plan.ndp
-    cols = inner // plan.nseq
 
     def kernel(
-        me_ref, slope_ref, douter_ref, wo_ref, wi_ref, n1t_ref, dres2_ref, hat1_ref, inv1_ref, gain_ref, wout_ref,
-        keep_ref, send_ref, dres1_ref, dattn_ref, dctx_ref, ib_ref, small_ref, acc,
+        slope_ref, douter_ref, wo_ref, wi_ref, dres2_ref, hat1_ref, inv1_ref, gain_ref, wout_ref,
+        dinner_ref, dres1_ref, dattn_ref, dctx_ref, ib_ref, small_ref, acc,
     ):
         j = pl.program_id(0)
         d_active = dot(douter_ref[...], wo_ref[...], 1, 1)
         d_inner = (d_active * slope_ref[...].astype(f32)).astype(bf16)
+        dinner_ref[...] = d_inner
         ib_ref[...] = jnp.broadcast_to(jnp.sum(d_inner.astype(f32), axis=0, keepdims=True), ib_ref.shape)
-        result = dot(n1t_ref[...], d_inner, 1, 0)
-        scatter_pieces(plan, me_ref, result, [(i, j) for i in range(plan.ndp)], keep_ref, send_ref, rows)
         back = dot(d_inner, wi_ref[...], 1, 1)
 
         @pl.when(j == 0)
@@ -389,40 +382,34 @@
             dctx_ref[...] = dot(low, wout_ref[...], 1, 1).astype(bf16)
             small_ref[...] = rows_of(d_normed * hat, d_normed, low.astype(f32))
 
-    full = lambda a: pl.BlockSpec(a.shape, lambda j, m: (0,) * a.ndim)
-    whole = lambda shape: pl.BlockSpec(shape, lambda j, m: (0,) * len(shape))
-    chunk = jax.ShapeDtypeStruct((plan.places, rows, cols), bf16)
+    full = lambda a: pl.BlockSpec(a.shape, lambda j: (0,) * a.ndim)
+    whole = lambda shape: pl.BlockSpec(shape, lambda j: (0,) * len(shape))
+    cols = pl.BlockSpec((n, BLOCK), lambda j: (0, j))
     return pl.pallas_call(
         kernel,
-        grid_spec=pltpu.PrefetchScalarGridSpec(
-            num_scalar_prefetch=1,
-            grid=(plan.nseq,),
-            in_specs=[
-                pl.BlockSpec((n, cols), lambda j, m: (0, j)),
-                full(d_outer),
-                pl.BlockSpec((cols, width), lambda j, m: (j, 0)),
-                pl.BlockSpec((width, cols), lambda j, m: (0, j)),
-                full(n1t),
-                full(d_resid2),
-                full(hat1),
-                full(inv1),
-                full(gain1),
-                full(wout),
-            ],
-            out_specs=[
-                whole(chunk.shape),
-                whole(chunk.shape),
-                whole((n, width)),
-                whole((n, width)),
-                whole((n, width)),
-                pl.BlockSpec((8, cols), lambda j, m: (0, j)),
-                whole((8, width)),
-            ],
-            scratch_shapes=[pltpu.VMEM((n, width), f32)],
-        ),
+        grid=(inner // BLOCK,),
+        in_specs=[
+            cols,
+            full(d_outer),
+            pl.BlockSpec((BLOCK, width), lambda j: (j, 0)),
+            pl.BlockSpec((width, BLOCK), lambda j: (0, j)),
+            full(d_resid2),
+            full(hat1),
+            full(inv1),
+            full(gain1),
+            full(wout),
+        ],
+        out_specs=[
+            cols,
+            whole((n, width)),
+            whole((n, width)),
+            whole((n, width)),
+            pl.BlockSpec((8, BLOCK), lambda j: (0, j)),
+            whole((8, width)),
+        ],
+        scratch_shapes=[pltpu.VMEM((n, width), f32)],
         out_shape=[
-            chunk,
-            chunk,
+            jax.ShapeDtypeStruct((n, inner), bf16),
             jax.ShapeDtypeStruct((n, width), f32),
             jax.ShapeDtypeStruct((n, width), bf16),
             jax.ShapeDtypeStruct((n, width), bf16),
@@ -430,7 +417,94 @@
             jax.ShapeDtypeStruct((8, width), f32),
         ],
         name="ffn_bwd",
-    )(me, slope, d_outer, wo, wi, n1t, d_resid2, hat1, inv1, gain1, wout)
+    )(slope, d_outer, wo, wi, d_resid2, hat1, inv1, gain1, wout)
+
+
+def ffn_inner_grad(plan, me, n1t, d_inner):
+    width, n = n1t.shape
+    inner = d_inner.shape[1]
+    rows = width // plan.ndp
+    cols = inner // plan.nseq
+
+    def kernel(me_ref, n1t_ref, d_ref, keep_ref, send_ref):
+        j = pl.program_id(0)
+        result = dot(n1t_ref[...], d_ref[...], 1, 0)
+        scatter_pieces(plan, me_ref, result, [(i, j) for i in range(plan.ndp)], keep_ref, send_ref, rows)
+
+    shape = jax.ShapeDtypeStruct((plan.places, rows, cols), bf16)
+    spec = pl.BlockSpec(shape.shape, lambda j, m: (0, 0, 0))
+    return pl.pallas_call(
+        kernel,
+        grid_spec=pltpu.PrefetchScalarGridSpec(
+            num_scalar_prefetch=1,
+            grid=(plan.nseq,),
+            in_specs=[
+                pl.BlockSpec((width, n), lambda j, m: (0, 0)),
+                pl.BlockSpec((n, cols), lambda j, m: (0, j)),
+            ],
+            out_specs=[spec, spec],
+        ),
+        out_shape=[shape, shape],
+        name="inner_grad",
+    )(me, n1t, d_inner)
+
+
+def finish_tokens(me, factor, pieces):
+    count = len(pieces)
+
+    def kernel(me_ref, factor_ref, *refs):
+        out_ref = refs[count]
+        for k in range(count):
+            out_ref[me_ref[1] ^ k] = refs[k][...].astype(f32) * factor_ref[0]
+
+    smem = pl.BlockSpec(memory_space=pltpu.SMEM)
+    vmem = pl.BlockSpec(memory_space=pltpu.VMEM)
+    return pl.pallas_call(
+        kernel,
+        in_specs=[smem, smem] + [vmem] * count,
+        out_specs=vmem,
+        out_shape=jax.ShapeDtypeStruct((count,) + pieces[0].shape, f32),
+        name="finish_tok",
+    )(me, factor, *pieces)
+
+
+def finish_weights(me, factor, near, far, split):
+    width = near.shape[2]
+    count = 4
+    shapes = []
+    for start, rows, axis in split:
+        if axis is None:
+            shapes += [(rows, width)] * count
+        else:
+            shapes.append((count * rows, width) if axis == 0 else (rows, count * width))
+
+    def kernel(me_ref, factor_ref, near_ref, far_ref, *outs):
+        for s in range(count):
+            diff = me_ref[1] ^ s
+            at = diff >> 1
+            o = 0
+            for start, rows, axis in split:
+                part = slice(start, start + rows)
+                value = jnp.where((diff & 1) == 0, near_ref[at, part], far_ref[at, part])
+                value = value.astype(f32) * factor_ref[0]
+                if axis is None:
+                    outs[o + s][...] = value
+                    o += count
+                elif axis == 0:
+                    outs[o][s * rows : (s + 1) * rows] = value
+                    o += 1
+                else:
+                    outs[o][:, s * width : (s + 1) * width] = value
+                    o += 1
+
+    smem = pl.BlockSpec(memory_space=pltpu.SMEM)
+    vmem = pl.BlockSpec(memory_space=pltpu.VMEM)
+    return pl.pallas_call(
+        kernel,
+        in_specs=[smem, smem, vmem, vmem],
+        out_specs=[vmem] * len(shapes),
+        out_shape=[jax.ShapeDtypeStruct(shape, f32) for shape in shapes],
+    )(me, factor, near, far)
 
 
 def attn_weight_grads(plan, me, flat, ctx, grads, small):
@@ -495,17 +569,9 @@
         return lax.ppermute(x, "seq", [(i, i ^ k) for i in range(nseq)])
 
     def gather_seq(x):
-        x = x[None]
-        for b in reversed(range(nseq.bit_length() - 1)):
-            x = jnp.concatenate([x, lax.ppermute(x, "seq", [(i, i ^ (1 << b)) for i in range(nseq)])], axis=0)
-        count = nseq.bit_length() - 1
-        order = []
-        for k in range(nseq):
-            pos = 0
-            for b in range(count):
-                pos |= ((k >> b) & 1) << (count - 1 - b)
-            order.append(pos)
-        return [x[p] for p in order]
+        assert nseq == 4
+        near = jnp.stack([x, swap_seq(x, 2)])
+        return near, swap_seq(near, 1)
 
     def per_device(
         tokens,
@@ -532,7 +598,6 @@
         seg_dev, rows_dev, width = tokens.shape
         assert seg_dev == nseq
         rows = rows_dev * nseq
-        assert rows < (1 << DIGITS) and ndp * nseq <= 256
         mem_rows = memory_init.shape[1]
         ff = inner_weight.shape[1]
         seq_index = lax.axis_index("seq")
@@ -565,8 +630,18 @@
         counts_here = jnp.sum(valid, axis=1)
         masked = jnp.where(valid[..., None] != 0, out_grad, jnp.zeros_like(out_grad))
         assert rows_dev <= 256
-        count_rows = jnp.broadcast_to(counts_here.astype(bf16)[:, None, None], (seg_dev, EXTRA, width))
+        assert seg_dev + 8 <= EXTRA
+        low_counts = counts_here.astype(bf16)
+        below = jnp.broadcast_to(jnp.pad(low_counts, (8, EXTRA - 8 - seg_dev))[None, :], (seg_dev, EXTRA))
+        below = jnp.where(jnp.arange(EXTRA)[None, :] < 8, low_counts[:, None], below)
+        count_rows = jnp.broadcast_to(below[:, :, None], (seg_dev, EXTRA, width))
         cot_pieces = to_segments(jnp.concatenate([masked, count_rows], axis=1))
+
+        group = sum(jnp.sum(p[rows_dev + 8 : rows_dev + 8 + seg_dev, :128].astype(f32), axis=0) for p in cot_pieces)
+        total = jnp.broadcast_to(group[None], (8, 128))
+        for b in range(ndp.bit_length() - 1):
+            total = total + lax.ppermute(total, "dp", [(i, i ^ (1 << b)) for i in range(ndp)])
+        factor = total[0, 0] / segs_total
 
         seg_global = dp_index * seg_dev + seq_index
         starts = jnp.cumsum(doc_segments) - doc_segments
@@ -607,28 +682,24 @@
             keep, send = place_pieces(plan, me, grad.reshape(ndp, nseq, -1, width))
         d_outer, keep, send = lax.optimization_barrier((d_outer, keep, send))
         outer = start_chunk(keep, send)
-        if aligned:
-            keep, send, d_resid1, d_attn, d_context, d_inner_bias, small1 = ffn_backward(
-                plan, me, slope, d_outer, outer_weight, inner_weight, n1t, d_resid2, hat1, inv1, vecs[1:2], output_weight
-            )
-        else:
-            d_inner = (dot(d_outer, outer_weight, 1, 1) * slope.astype(f32)).astype(bf16)
-            d_inner_bias = jnp.broadcast_to(jnp.sum(d_inner.astype(f32), axis=0), (8, ff))
-            grad = dot(n1t, d_inner, 1, 0).astype(bf16)
-            grad = grad.reshape(ndp, width // ndp, nseq, ff // nseq).transpose(0, 2, 1, 3)
-            keep, send = place_pieces(plan, me, grad)
-            d_normed = dot(d_inner, inner_weight, 1, 1) + d_resid2
-            d_resid1 = normalize_back(hat1, inv1[:, 0:1], d_normed * vecs[1:2])
-            d_attn = d_resid1.astype(bf16)
-            d_context = dot(d_attn, output_weight, 1, 1).astype(bf16)
-            small1 = rows_of(d_normed * hat1, d_normed, d_attn.astype(f32))
-        inner = start_chunk(keep, send)
+        d_inner, d_resid1, d_attn, d_context, d_inner_bias, small1 = ffn_backward(
+            slope, d_outer, outer_weight, inner_weight, d_resid2, hat1, inv1, vecs[1:2], output_weight
+        )
         outer = step_chunk(outer, 0)
         d_queries, d_keys, d_values = attention_backward(
             queries, keys, values, context, d_context, probs, 1, rows
         )
+        d_queries, d_inner = lax.optimization_barrier((d_queries, d_inner))
         outer = step_chunk(outer, 1)
-        inner = step_chunk(inner, 0)
+        if aligned:
+            keep, send = ffn_inner_grad(plan, me, n1t, d_inner)
+        else:
+            grad = dot(n1t, d_inner, 1, 0).astype(bf16)
+            grad = grad.reshape(ndp, width // ndp, nseq, ff // nseq).transpose(0, 2, 1, 3)
+            keep, send = place_pieces(plan, me, grad)
+        d_queries, keep, send = lax.optimization_barrier((d_queries, keep, send))
+        inner = start_chunk(keep, send)
+        outer = step_chunk(outer, 2)
         cut_pieces, small = inputs_backward(
             me,
             (d_queries, d_keys, d_values),
@@ -655,41 +726,45 @@
             below = jnp.broadcast_to(small.astype(bf16)[None], (ndp,) + small.shape)
             keep, send = place_pieces(plan, me, jnp.concatenate([blocks, below], axis=2))
         attn = start_chunk(keep, send)
-        outer = step_chunk(outer, 2)
-        inner = step_chunk(inner, 1)
+        inner = step_chunk(inner, 0)
         for step in range(3, plan.steps):
             outer = step_chunk(outer, step)
-        for step in range(2, plan.steps):
+        for step in range(1, plan.steps):
             inner = step_chunk(inner, step)
-        ffn_pieces = gather_seq(jnp.concatenate([total_of(outer)[0], total_of(inner)[0]], axis=0).astype(bf16))
         for step in range(plan.steps):
             attn = step_chunk(attn, step)
-        attn_pieces = gather_seq(total_of(attn)[0].astype(bf16))
-
-        def in_order(pieces):
-            stack = jnp.stack(pieces)
-            return [lax.dynamic_index_in_dim(stack, seq_index ^ s, 0, keepdims=False) for s in range(nseq)]
+        ffn_near, ffn_far = gather_seq(jnp.concatenate([total_of(outer)[0], total_of(inner)[0]], axis=0).astype(bf16))
+        attn_near, attn_far = gather_seq(total_of(attn)[0].astype(bf16))
 
         part = width // ndp
-        attn_parts = in_order(attn_pieces)
-        ffn_parts = in_order(ffn_pieces)
-        weights = (2.0 ** jnp.arange(DIGITS)).astype(f32)
-        total = jnp.sum(attn_parts[1][part + ib_rows, :DIGITS].astype(f32) * weights)
-        factor = total / segs_total
-        finish = lambda x: x.astype(f32) * factor
-
-        tokens_grad = to_rows(cut_pieces, finish)
-
         outer_rows = ff // (ndp * nseq)
-        g_outer = finish(jnp.concatenate([p[:outer_rows] for p in ffn_parts], axis=0))
-        g_inner = finish(jnp.concatenate([p[outer_rows:] for p in ffn_parts], axis=1))
-        g_query, g_key, g_value, g_output = [finish(p[:part]) for p in attn_parts[:4]]
-        mine = lambda x: lax.dynamic_slice_in_dim(finish(x), dp_index * part, part, axis=1)
-        vec_rows = mine(attn_parts[0][part : part + 8])
-        g_memory = mine(attn_parts[2][part : part + mem_rows]).T
+        scale = factor.reshape(1)
+        if aligned:
+            tokens_grad = finish_tokens(me, scale, cut_pieces)
+            g_outer, g_inner = finish_weights(me, scale, ffn_near, ffn_far, [(0, outer_rows, 0), (outer_rows, part, 1)])
+            got = finish_weights(me, scale, attn_near, attn_far, [(0, part, None), (part, EXTRA, None)])
+            g_query, g_key, g_value, g_output = got[:4]
+            small_parts = got[4:]
+        else:
+            finish = lambda x: x.astype(f32) * factor
+            tokens_grad = to_rows(cut_pieces, finish)
+
+            def in_order(near, far):
+                stack = jnp.stack([near[0], far[0], near[1], far[1]])
+                return [finish(lax.dynamic_index_in_dim(stack, seq_index ^ k, 0, keepdims=False)) for k in range(nseq)]
+
+            ffn_parts = in_order(ffn_near, ffn_far)
+            g_outer = jnp.concatenate([p[:outer_rows] for p in ffn_parts], axis=0)
+            g_inner = jnp.concatenate([p[outer_rows:] for p in ffn_parts], axis=1)
+            attn_parts = in_order(attn_near, attn_far)
+            g_query, g_key, g_value, g_output = [p[:part] for p in attn_parts]
+            small_parts = [p[part:] for p in attn_parts]
+        mine = lambda x: lax.dynamic_slice_in_dim(x, dp_index * part, part, axis=1)
+        vec_rows = mine(small_parts[0][:8])
+        g_memory = mine(small_parts[2][:mem_rows]).T
         inner_part = ff // ndp
         g_inner_bias = lax.dynamic_slice_in_dim(
-            finish(attn_parts[1][part : part + ib_rows]).reshape(-1), dp_index * inner_part, inner_part, axis=0
+            small_parts[1][:ib_rows].reshape(-1), dp_index * inner_part, inner_part, axis=0
         )
         g_query_bias, g_value_bias, g_gain1, g_shift1, g_output_bias, g_gain2, g_shift2, g_outer_bias = vec_rows
         return (

time: 245 us -> 249 us (1.016)
  waiting for transfers between devices: 71.2 us -> 51.2 us
  starting transfers between devices: 32.2 us -> 43.9 us
  Pallas kernels: 91.8 us -> 101 us
  local copies, waits for them, and re-layouts: 6.91 us -> 14.4 us
  other arithmetic: 34.2 us -> 30 us
    ppermute x12, waiting for transfers between devices: 57.1 us -> 38.6 us  [step_chunk(): got = lax.ppermute(send, devices, plan.perm(step))]
    pallas_call x1 -> x5, Pallas kernels: 21.7 us -> 31 us  [the longest x1 15 us: ffn_backward(): pl.pallas_call(kernel, grid=(inner // BLOCK,), in_specs=[cols, full(d_out...]
    ppermute x4 -> x3, waiting for transfers between devices: 10.5 us -> 2.04 us  [per_device(): lax.ppermute(total, 'dp', [(i, i ^ 1 << b) for i in range(ndp)])]
    ppermute x12 -> x16, waiting for transfers between devices: 3.6 us -> 10.6 us  [swap_seq(): return lax.ppermute(x, 'seq', [(i, i ^ k) for i in range(nseq)])]
    ppermute x12 -> x16, starting transfers between devices: 8.99 us -> 13.2 us  [swap_seq(): return lax.ppermute(x, 'seq', [(i, i ^ k) for i in range(nseq)])]
    ppermute x4 -> x3, starting transfers between devices: 2.1 us -> 6.28 us  [per_device(): lax.ppermute(total, 'dp', [(i, i ^ 1 << b) for i in range(ndp)])]
    ppermute x12, starting transfers between devices: 20.3 us -> 23.8 us  [step_chunk(): got = lax.ppermute(send, devices, plan.perm(step))]
    mul x5 -> x0, other arithmetic: 3.33 us -> none  [per_device(): finish = lambda x: x.astype(f32) * factor]
  transfers between devices with their start and end apart: 31 -> 34, of which waited for: 14 -> 14; matrix products, arithmetic and copies ran while one was open for 17% -> 17% of each run, Pallas kernels for 25% -> 28%
where the time goes in v1:
time: 249 us; the launch traced here: 248 us
  Pallas kernels  101 us (41%)
  waiting for transfers between devices  51.2 us (21%)
  starting transfers between devices  43.9 us (18%)
  other arithmetic  30 us (12%)
  local copies, waits for them, and re-layouts  14.4 us (6%)
  matrix products  5.04 us (2%)
  between operations  2.52 us (1%)
    ppermute x12, waiting for transfers between devices, step_chunk(): got = lax.ppermute(send, devices, plan.perm(step))  38.6 us
    ppermute x12, starting transfers between devices, step_chunk(): got = lax.ppermute(send, devices, plan.perm(step))  23.8 us
    pallas_call x1, Pallas kernels, ffn_forward(): pl.pallas_call(kernel, grid=(inner // BLOCK,), in_specs=[full(flat), full...  21.4 us
    convert_element_type x12, other arithmetic, step_chunk(): send = total_of([t[half:] for t in terms]).astype(bf16)  18.7 us
    pallas_call x1, Pallas kernels, ffn_backward(): pl.pallas_call(kernel, grid=(inner // BLOCK,), in_specs=[cols, full(d_out...  15 us
    ppermute x16, starting transfers between devices, swap_seq(): return lax.ppermute(x, 'seq', [(i, i ^ k) for i in range(nseq)])  13.2 us
    pallas_call x1, Pallas kernels, attention_backward(): pl.pallas_call(attn_bwd_kernel, grid=(segs, pairs), in_specs=[spec] * 5 +...  12.4 us
    pallas_call x1, Pallas kernels, attention_forward(): pl.pallas_call(attn_fwd_kernel, grid=(segs, pairs), in_specs=[spec, spec,...  11.4 us
  transfers between devices with their start and end apart: 34, of which 14 were waited for; matrix products, arithmetic and copies ran while one was open for 17% of the time, Pallas kernels for 28%

profile of v1, /device:TPU:0, one launch (start us, length us, event | category | flops | bytes accessed | tf_op | source)
XLA Modules:
  0.0 248.1 jit_solution(16025823393698881892)
XLA Ops:
  3.2 2.5 %collective-permute-start.1 = (bf16[128,768]{1,0:T(8,128)(2,1)S(1)}, bf16[128,768]{1,0:T(8,128)(2,1)S(1)}, u32[]{:S(2)}, u32[]{:S(2)}) collective-permute-start(bf16[128,768]{1,0:T(8,128)(2,1)S(1)} %get-tuple-element.127), channel_id=1, source_target_pairs={{0,2},{1,3},{2,0},{3,1},{4,6},{5,7},{6,4},{7,5},{8,10},{9,11},{10,... | collective-permute-start | bytes 589832 | tf_op jit(solution)/shard_map/ppermute | solution.py:569
  20.7 11.4 %attn_fwd.1 = (bf16[512,768]{1,0:T(8,128)(2,1)}, bf16[12,512,512]{2,1,0:T(8,128)(2,1)}) custom-call(bf16[512,768]{1,0:T(8,128)(2,1)} %add_convert_fusion.4.q_ref, bf16[512,768]{1,0:T(8,128)(2,1)} %convolution_convert_fusion.k_ref, bf16[512,768]{1,0:T(8,128)(2,1)} %add_convert_fusion.3.v_ref), custom_call_target="tpu_custom_call" | custom-call | tf_op jit(solution)/shard_map/attn_fwd/pallas_call | solution.py:79
  32.1 21.4 %ffn_fwd.1 = (f32[512,768]{1,0:T(8,128)}, f32[512,128]{1,0:T(8,128)}, bf16[768,512]{1,0:T(8,128)(2,1)}, bf16[512,3072]{1,0:T(8,128)(2,1)}, bf16[512,3072]{1,0:T(...) custom-call(bf16[512,768]{1,0:T(8,128)(2,1)} %copy-done, ...), custom_call_target="tpu_custom_call" | custom-call | tf_op jit(solution)/shard_map/ffn_fwd/pallas_call | solution.py:210
  53.5 8.5 %outer_grad.1 = (bf16[16,96,768]{2,1,0:T(8,128)(2,1)}, bf16[16,96,768]{2,1,0:T(8,128)(2,1)}) custom-call(s32[3]{0:T(128)} %pad_add_fusion.me_ref, bf16[512,3072]{1,0:T(8,128)(2,1)} %get-tuple-element.76.active_ref, bf16[512,768]{1,0:T(8,128)(2,1)} %get-tuple-element.79.d_ref.douter_ref), custom_call_target="tpu_custom_call" | custom-call | tf_op jit(solution)/shard_map/outer_grad/pallas_call | solution.py:335
  62.8 15.0 %ffn_bwd.1 = (bf16[512,3072]{1,0:T(8,128)(2,1)}, f32[512,768]{1,0:T(8,128)}, bf16[512,768]{1,0:T(8,128)(2,1)}, bf16[512,768]{1,0:T(8,128)(2,1)}, f32[8,3072]{1,0:T(8,128)}, /*index=5*/f32[8,768]{1,0:T(8,128)}) custom-call(bf16[512,3072]{1,0:T(8,128)(2,1)} %get-tuple-element.74.slope_ref, bf16[512,768]{1,0:T(8,128)(2,1)} %get-tuple-element.79.d_ref.douter_ref, ...), custom_call_target="tpu_custom_call" | custom-call | tf_op jit(solution)/shard_map/ffn_bwd/pallas_call | solution.py:388
  77.8 12.4 %attn_bwd.1 = (bf16[512,768]{1,0:T(8,128)(2,1)}, bf16[512,768]{1,0:T(8,128)(2,1)}, bf16[512,768]{1,0:T(8,128)(2,1)}) custom-call(bf16[512,768]{1,0:T(8,128)(2,1)} %add_convert_fusion.4.q_ref, bf16[512,768]{1,0:T(8,128)(2,1)} %convolution_convert_fusion.k_ref, bf16[512,768]{1,0:T(8,128)(2,1)} %add_convert_fusion.3.v_ref, ...), custom_call_target="tpu_custom_call" | custom-call | tf_op jit(solution)/shard_map/attn_bwd/pallas_call | solution.py:98
  90.2 8.5 %inner_grad.1 = (bf16[16,96,768]{2,1,0:T(8,128)(2,1)}, bf16[16,96,768]{2,1,0:T(8,128)(2,1)}) custom-call(s32[3]{0:T(128)} %pad_add_fusion.me_ref, bf16[768,512]{1,0:T(8,128)(2,1)} %get-tuple-element.88.n1t_ref, bf16[512,3072]{1,0:T(8,128)(2,1)} %get-tuple-element.89.d_ref), custom_call_target="tpu_custom_call" | custom-call | tf_op jit(solution)/shard_map/inner_grad/pallas_call | solution.py:436
  99.0 6.3 %inputs_bwd.1 = (bf16[128,768]{1,0:T(8,128)(2,1)}, bf16[128,768]{1,0:T(8,128)(2,1)}, bf16[128,768]{1,0:T(8,128)(2,1)}, bf16[128,768]{1,0:T(8,128)(2,1)}, f32[4,16,768]{2,1,0:T(8,128)}) custom-call(s32[3]{0:T(128)} %pad_add_fusion.me_ref, bf16[512,768]{1,0:T(8,128)(2,1)} %get-tuple-element.92.dq_ref.d0_ref, bf16[512,768]{1,0:T(8,128)(2,1)} %get-tuple-element.93.dk_ref.d1_ref, ...), custom_call_target="tpu_custom_call" | custom-call | tf_op jit(solution)/shard_map/inputs_bwd/pallas_call | solution.py:259
  105.3 10.0 %attn_grad.1 = (bf16[16,112,768]{2,1,0:T(8,128)(2,1)}, bf16[16,112,768]{2,1,0:T(8,128)(2,1)}) custom-call(s32[3]{0:T(128)} %pad_add_fusion.me_ref, bf16[512,768]{1,0:T(8,128)(2,1)} %copy-done, bf16[512,768]{1,0:T(8,128)(2,1)} %get-tuple-element.69.ctx_ref, bf16[512,768]{1,0:T(8,128)(2,1)} %get-tuple-element.92.dq_ref.d0_ref, ...), custom_call_target="tpu_custom_call" | custom-call | tf_op jit(solution)/shard_map/attn_grad/pallas_call | solution.py:526
  129.3 4.2 %collective-permute-done.23 = bf16[8,96,768]{2,1,0:T(8,128)(2,1)S(1)} collective-permute-done((bf16[8,96,768]{2,1,0:T(8,128)(2,1)S(1)}, bf16[8,96,768]{2,1,0:T(8,128)(2,1)S(1)}, u32[]{:S(2)}, u32[]{:S(2)}) %collective-permute-start.23) | collective-permute-done | bytes 1179680 | tf_op jit(solution)/shard_map/ppermute | solution.py:565
  133.5 2.7 %add_convert_fusion.7 = bf16[4,96,768]{2,1,0:T(8,128)(2,1)} fusion(bf16[8,96,768]{2,1,0:T(8,128)(2,1)S(1)} %collective-permute-done.23, bf16[16,96,768]{2,1,0:T(8,128)(2,1)} %collective-permute-done.22, bf16[16,96,768]{2,1,0:T(8,128)(2,1)} %get-tuple-element.112), kind=kLoop, calls=%fused_computation.12 | loop fusion | flops 1769472 | bytes 2359296 | tf_op jit(solution)/shard_map/convert_element_type | solution.py:564
  138.2 14.2 %collective-permute-done.28 = bf16[8,96,768]{2,1,0:T(8,128)(2,1)S(1)} collective-permute-done((bf16[8,96,768]{2,1,0:T(8,128)(2,1)S(1)}, bf16[8,96,768]{2,1,0:T(8,128)(2,1)S(1)}, u32[]{:S(2)}, u32[]{:S(2)}) %collective-permute-start.28) | collective-permute-done | bytes 1179680 | tf_op jit(solution)/shard_map/ppermute | solution.py:565
  152.5 2.5 %add_convert_fusion.6 = bf16[4,96,768]{2,1,0:T(8,128)(2,1)} fusion(bf16[8,96,768]{2,1,0:T(8,128)(2,1)S(1)} %collective-permute-done.28, bf16[16,96,768]{2,1,0:T(8,128)(2,1)} %collective-permute-done.27, bf16[16,96,768]{2,1,0:T(8,128)(2,1)S(1)} %copy-done.5), kind=kLoop, calls=%fused_computation.11 | loop fusion | flops 1769472 | bytes 2359296 | tf_op jit(solution)/shard_map/convert_element_type | solution.py:564
  162.1 2.6 %collective-permute-start.11 = (f32[8,128]{1,0:T(8,128)S(1)}, f32[8,128]{1,0:T(8,128)S(1)}, u32[]{:S(2)}, u32[]{:S(2)}) collective-permute-start(f32[8,128]{1,0:T(8,128)S(1)} %fusion.16), channel_id=1, source_target_pairs={{0,16},{4,20},{8,24},{12,28},{16,0},{20,4},{24,8},{28,12},{1,17},{... | collective-permute-start | bytes 12296 | tf_op jit(solution)/shard_map/ppermute | solution.py:643
  166.1 5.3 %collective-permute-done.29 = bf16[4,96,768]{2,1,0:T(8,128)(2,1)S(1)} collective-permute-done((bf16[4,96,768]{2,1,0:T(8,128)(2,1)}, bf16[4,96,768]{2,1,0:T(8,128)(2,1)S(1)}, u32[]{:S(2)}, u32[]{:S(2)}) %collective-permute-start.29) | collective-permute-done | bytes 589856 | tf_op jit(solution)/shard_map/ppermute | solution.py:565
  184.8 2.8 %collective-permute-start.26 = (bf16[1,96,768]{2,1,0:T(8,128)(2,1)S(1)}, bf16[1,96,768]{2,1,0:T(8,128)(2,1)S(1)}, u32[]{:S(2)}, u32[]{:S(2)}) collective-permute-start(bf16[1,96,768]{2,1,0:T(8,128)(2,1)S(1)} %add_convert_fusion.16), channel_id=1, source_target_pairs={{0,16},{1,17},{2,18},{3,19},{4,20},{5,21},{6,22},{7,23},{8,24},{9,... | collective-permute-start | bytes 442376 | tf_op jit(solution)/shard_map/ppermute | solution.py:565
  188.7 3.7 %collective-permute-done.26 = bf16[1,96,768]{2,1,0:T(8,128)(2,1)S(1)} collective-permute-done((bf16[1,96,768]{2,1,0:T(8,128)(2,1)S(1)}, bf16[1,96,768]{2,1,0:T(8,128)(2,1)S(1)}, u32[]{:S(2)}, u32[]{:S(2)}) %collective-permute-start.26) | collective-permute-done | bytes 147488 | tf_op jit(solution)/shard_map/ppermute | solution.py:565
  196.3 6.0 %collective-permute-start.18 = (bf16[2,112,768]{2,1,0:T(8,128)(2,1)S(1)}, bf16[2,112,768]{2,1,0:T(8,128)(2,1)S(1)}, u32[]{:S(2)}, u32[]{:S(2)}) collective-permute-start(bf16[2,112,768]{2,1,0:T(8,128)(2,1)S(1)} %add_convert_fusion.8), channel_id=1, source_target_pairs={{0,8},{1,9},{2,10},{3,11},{4,12},{5,13},{6,14},{7,15},{8,0},{9,1},... | collective-permute-start | bytes 1032200 | tf_op jit(solution)/shard_map/ppermute | solution.py:565
  205.1 3.8 %collective-permute-done.18 = bf16[2,112,768]{2,1,0:T(8,128)(2,1)S(1)} collective-permute-done((bf16[2,112,768]{2,1,0:T(8,128)(2,1)S(1)}, bf16[2,112,768]{2,1,0:T(8,128)(2,1)S(1)}, u32[]{:S(2)}, u32[]{:S(2)}) %collective-permute-start.18) | collective-permute-done | bytes 344096 | tf_op jit(solution)/shard_map/ppermute | solution.py:565
  214.6 3.6 %collective-permute-done.19 = bf16[1,112,768]{2,1,0:T(8,128)(2,1)S(1)} collective-permute-done((bf16[1,112,768]{2,1,0:T(8,128)(2,1)S(1)}, bf16[1,112,768]{2,1,0:T(8,128)(2,1)S(1)}, u32[]{:S(2)}, u32[]{:S(2)}) %collective-permute-start.19) | collective-permute-done | bytes 172064 | tf_op jit(solution)/shard_map/ppermute | solution.py:565
  221.5 4.6 %collective-permute-done.20 = bf16[112,768]{1,0:T(8,128)(2,1)S(1)} collective-permute-done((bf16[112,768]{1,0:T(8,128)(2,1)S(1)}, bf16[112,768]{1,0:T(8,128)(2,1)S(1)}, u32[]{:S(2)}, u32[]{:S(2)}) %collective-permute-start.20) | collective-permute-done | bytes 172064 | tf_op jit(solution)/shard_map/ppermute | solution.py:569
  228.7 4.6 %collective-permute-done.14.refs_3_ = bf16[128,768]{1,0:T(8,128)(2,1)S(1)} collective-permute-done((bf16[128,768]{1,0:T(8,128)(2,1)S(1)}, bf16[128,768]{1,0:T(8,128)(2,1)S(1)}, u32[]{:S(2)}, u32[]{:S(2)}) %collective-permute-start.14) | collective-permute-done | bytes 196640 | tf_op jit(solution)/shard_map/ppermute | solution.py:569
  234.0 2.5 finish_tok.1
  238.2 2.8 %shard_map.332 = (f32[384,768]{1,0:T(8,128)}, f32[96,3072]{1,0:T(8,128)}) custom-call(s32[3]{0:T(128)} %pad_add_fusion.me_ref, f32[1]{0:T(128)} %bitcast.20.factor_ref, bf16[2,192,768]{2,1,0:T(8,128)(2,1)} %copy-done.6, bf16[2,192,768]{2,1,0:T(8,128)(2,1)} %collective-permute-done.33.far_ref), custom_call_target="tpu_custom_call" | custom-call | tf_op jit(solution)/shard_map/pallas_call | solution.py:502
  (196 shorter events, 83.5 us)
Async XLA Ops:
  2.7 12.2 %collective-permute-start = (bf16[128,768]{1,0:T(8,128)(2,1)}, bf16[128,768]{1,0:T(8,128)(2,1)S(1)}, u32[]{:S(2)}, u32[]{:S(2)}) collective-permute-start(bf16[128,768]{1,0:T(8,128)(2,1)} %get-tuple-element.125), channel_id=1, source_target_pairs={{0,1},{1,0},{2,3},{3,2},{4,5},{5,4},{6,7},{7,6},{8,9},{9,8},{10,11... | collective-permute-start | bytes 589832 | tf_op jit(solution)/shard_map/ppermute | solution.py:569
  3.2 11.7 %collective-permute-start.1 = (bf16[128,768]{1,0:T(8,128)(2,1)S(1)}, bf16[128,768]{1,0:T(8,128)(2,1)S(1)}, u32[]{:S(2)}, u32[]{:S(2)}) collective-permute-start(bf16[128,768]{1,0:T(8,128)(2,1)S(1)} %get-tuple-element.127), channel_id=1, source_target_pairs={{0,2},{1,3},{2,0},{3,1},{4,6},{5,7},{6,4},{7,5},{8,10},{9,11},{10,... | collective-permute-start | bytes 589832 | tf_op jit(solution)/shard_map/ppermute | solution.py:569
  7.4 24.7 %collective-permute-start.3 = (bf16[144,768]{1,0:T(8,128)(2,1)}, bf16[144,768]{1,0:T(8,128)(2,1)}, u32[]{:S(2)}, u32[]{:S(2)}) collective-permute-start(bf16[144,768]{1,0:T(8,128)(2,1)} %get-tuple-element.122), channel_id=1, source_target_pairs={{0,1},{1,0},{2,3},{3,2},{4,5},{5,4},{6,7},{7,6},{8,9},{9,8},{10,11... | collective-permute-start | bytes 663560 | tf_op jit(solution)/shard_map/ppermute | solution.py:569
  7.5 24.5 %collective-permute-start.4 = (bf16[144,768]{1,0:T(8,128)(2,1)}, bf16[144,768]{1,0:T(8,128)(2,1)}, u32[]{:S(2)}, u32[]{:S(2)}) collective-permute-start(bf16[144,768]{1,0:T(8,128)(2,1)} %get-tuple-element.123), channel_id=1, source_target_pairs={{0,2},{1,3},{2,0},{3,1},{4,6},{5,7},{6,4},{7,5},{8,10},{9,11},{10,... | collective-permute-start | bytes 663560 | tf_op jit(solution)/shard_map/ppermute | solution.py:569
  14.9 17.1 %collective-permute-start.5 = (bf16[144,768]{1,0:T(8,128)(2,1)}, bf16[144,768]{1,0:T(8,128)(2,1)}, u32[]{:S(2)}, u32[]{:S(2)}) collective-permute-start(bf16[144,768]{1,0:T(8,128)(2,1)} %get-tuple-element.120), channel_id=1, source_target_pairs={{0,3},{1,2},{2,1},{3,0},{4,7},{5,6},{6,5},{7,4},{8,11},{9,10},{10,... | collective-permute-start | bytes 663560 | tf_op jit(solution)/shard_map/ppermute | solution.py:569
  62.0 53.5 %collective-permute-start.22 = (bf16[16,96,768]{2,1,0:T(8,128)(2,1)}, bf16[16,96,768]{2,1,0:T(8,128)(2,1)}, u32[]{:S(2)}, u32[]{:S(2)}) collective-permute-start(bf16[16,96,768]{2,1,0:T(8,128)(2,1)} %get-tuple-element.113), channel_id=1, source_target_pairs={{0,1},{1,0},{2,3},{3,2},{4,5},{5,4},{6,7},{7,6},{8,9},{9,8},{10,11... | collective-permute-start | bytes 7077896 | tf_op jit(solution)/shard_map/ppermute | solution.py:560
  98.7 20.7 %collective-permute-start.27 = (bf16[16,96,768]{2,1,0:T(8,128)(2,1)}, bf16[16,96,768]{2,1,0:T(8,128)(2,1)}, u32[]{:S(2)}, u32[]{:S(2)}) collective-permute-start(bf16[16,96,768]{2,1,0:T(8,128)(2,1)} %get-tuple-element.115), channel_id=1, source_target_pairs={{0,1},{1,0},{2,3},{3,2},{4,5},{5,4},{6,7},{7,6},{8,9},{9,8},{10,11... | collective-permute-start | bytes 7077896 | tf_op jit(solution)/shard_map/ppermute | solution.py:560
  115.3 10.7 %collective-permute-start.15 = (bf16[16,112,768]{2,1,0:T(8,128)(2,1)}, bf16[16,112,768]{2,1,0:T(8,128)(2,1)S(1)}, u32[]{:S(2)}, u32[]{:S(2)}) collective-permute-start(bf16[16,112,768]{2,1,0:T(8,128)(2,1)} %get-tuple-element.106), channel_id=1, source_target_pairs={{0,1},{1,0},{2,3},{3,2},{4,5},{5,4},{6,7},{7,6},{8,9},{9,8},{10,11... | collective-permute-start | bytes 8257544 | tf_op jit(solution)/shard_map/ppermute | solution.py:560
  117.2 16.3 %collective-permute-start.23 = (bf16[8,96,768]{2,1,0:T(8,128)(2,1)S(1)}, bf16[8,96,768]{2,1,0:T(8,128)(2,1)S(1)}, u32[]{:S(2)}, u32[]{:S(2)}) collective-permute-start(bf16[8,96,768]{2,1,0:T(8,128)(2,1)S(1)} %add_convert_fusion.2), channel_id=1, source_target_pairs={{0,2},{1,5},{2,0},{3,7},{4,6},{5,1},{6,4},{7,3},{8,10},{9,13},{10,... | collective-permute-start | bytes 3538952 | tf_op jit(solution)/shard_map/ppermute | solution.py:565
  120.9 31.5 %collective-permute-start.28 = (bf16[8,96,768]{2,1,0:T(8,128)(2,1)S(1)}, bf16[8,96,768]{2,1,0:T(8,128)(2,1)S(1)}, u32[]{:S(2)}, u32[]{:S(2)}) collective-permute-start(bf16[8,96,768]{2,1,0:T(8,128)(2,1)S(1)} %add_convert_fusion.1), channel_id=1, source_target_pairs={{0,2},{1,5},{2,0},{3,7},{4,6},{5,1},{6,4},{7,3},{8,10},{9,13},{10,... | collective-permute-start | bytes 3538952 | tf_op jit(solution)/shard_map/ppermute | solution.py:565
  123.9 33.0 %collective-permute-start.9 = (f32[8,128]{1,0:T(8,128)S(1)}, f32[8,128]{1,0:T(8,128)S(1)}, u32[]{:S(2)}, u32[]{:S(2)}) collective-permute-start(f32[8,128]{1,0:T(8,128)S(1)} %broadcast_in_dim.107), channel_id=1, source_target_pairs={{0,4},{4,0},{8,12},{12,8},{16,20},{20,16},{24,28},{28,24},{1,5},{5... | collective-permute-start | bytes 12296 | tf_op jit(solution)/shard_map/ppermute | solution.py:643
  128.1 47.7 %collective-permute-start.16 = (bf16[8,112,768]{2,1,0:T(8,128)(2,1)}, bf16[8,112,768]{2,1,0:T(8,128)(2,1)}, u32[]{:S(2)}, u32[]{:S(2)}) collective-permute-start(bf16[8,112,768]{2,1,0:T(8,128)(2,1)} %add_convert_fusion), channel_id=1, source_target_pairs={{0,2},{1,5},{2,0},{3,7},{4,6},{5,1},{6,4},{7,3},{8,10},{9,13},{10,... | collective-permute-start | bytes 4128776 | tf_op jit(solution)/shard_map/ppermute | solution.py:565
  136.2 25.9 %collective-permute-start.24 = (bf16[4,96,768]{2,1,0:T(8,128)(2,1)}, bf16[4,96,768]{2,1,0:T(8,128)(2,1)}, u32[]{:S(2)}, u32[]{:S(2)}) collective-permute-start(bf16[4,96,768]{2,1,0:T(8,128)(2,1)} %add_convert_fusion.7), channel_id=1, source_target_pairs={{0,4},{1,3},{2,6},{3,1},{4,0},{5,7},{6,2},{7,5},{8,12},{9,11},{10,... | collective-permute-start | bytes 1769480 | tf_op jit(solution)/shard_map/ppermute | solution.py:565
  155.0 16.4 %collective-permute-start.29 = (bf16[4,96,768]{2,1,0:T(8,128)(2,1)}, bf16[4,96,768]{2,1,0:T(8,128)(2,1)S(1)}, u32[]{:S(2)}, u32[]{:S(2)}) collective-permute-start(bf16[4,96,768]{2,1,0:T(8,128)(2,1)} %add_convert_fusion.6), channel_id=1, source_target_pairs={{0,4},{1,3},{2,6},{3,1},{4,0},{5,7},{6,2},{7,5},{8,12},{9,11},{10,... | collective-permute-start | bytes 1769480 | tf_op jit(solution)/shard_map/ppermute | solution.py:565
  158.6 68.4 %collective-permute-start.12 = (bf16[128,768]{1,0:T(8,128)(2,1)}, bf16[128,768]{1,0:T(8,128)(2,1)S(1)}, u32[]{:S(2)}, u32[]{:S(2)}) collective-permute-start(bf16[128,768]{1,0:T(8,128)(2,1)} %get-tuple-element.100), channel_id=1, source_target_pairs={{0,1},{1,0},{2,3},{3,2},{4,5},{5,4},{6,7},{7,6},{8,9},{9,8},{10,11... | collective-permute-start | bytes 589832 | tf_op jit(solution)/shard_map/ppermute | solution.py:569
  160.6 68.1 %collective-permute-start.13 = (bf16[128,768]{1,0:T(8,128)(2,1)}, bf16[128,768]{1,0:T(8,128)(2,1)}, u32[]{:S(2)}, u32[]{:S(2)}) collective-permute-start(bf16[128,768]{1,0:T(8,128)(2,1)} %get-tuple-element.101), channel_id=1, source_target_pairs={{0,2},{1,3},{2,0},{3,1},{4,6},{5,7},{6,4},{7,5},{8,10},{9,11},{10,... | collective-permute-start | bytes 589832 | tf_op jit(solution)/shard_map/ppermute | solution.py:569
  162.1 49.6 %collective-permute-start.11 = (f32[8,128]{1,0:T(8,128)S(1)}, f32[8,128]{1,0:T(8,128)S(1)}, u32[]{:S(2)}, u32[]{:S(2)}) collective-permute-start(f32[8,128]{1,0:T(8,128)S(1)} %fusion.16), channel_id=1, source_target_pairs={{0,16},{4,20},{8,24},{12,28},{16,0},{20,4},{24,8},{28,12},{1,17},{... | collective-permute-start | bytes 12296 | tf_op jit(solution)/shard_map/ppermute | solution.py:643
  181.1 14.0 %collective-permute-start.17 = (bf16[4,112,768]{2,1,0:T(8,128)(2,1)S(1)}, bf16[4,112,768]{2,1,0:T(8,128)(2,1)S(1)}, u32[]{:S(2)}, u32[]{:S(2)}) collective-permute-start(bf16[4,112,768]{2,1,0:T(8,128)(2,1)S(1)} %add_convert_fusion.5), channel_id=1, source_target_pairs={{0,4},{1,3},{2,6},{3,1},{4,0},{5,7},{6,2},{7,5},{8,12},{9,11},{10,... | collective-permute-start | bytes 2064392 | tf_op jit(solution)/shard_map/ppermute | solution.py:565
  192.5 9.8 %collective-permute-start.31 = (bf16[1,96,768]{2,1,0:T(8,128)(2,1)S(1)}, bf16[1,96,768]{2,1,0:T(8,128)(2,1)S(1)}, u32[]{:S(2)}, u32[]{:S(2)}) collective-permute-start(bf16[1,96,768]{2,1,0:T(8,128)(2,1)S(1)} %add_convert_fusion.14), channel_id=1, source_target_pairs={{0,16},{1,17},{2,18},{3,19},{4,20},{5,21},{6,22},{7,23},{8,24},{9,... | collective-permute-start | bytes 442376 | tf_op jit(solution)/shard_map/ppermute | solution.py:565
  196.3 12.6 %collective-permute-start.18 = (bf16[2,112,768]{2,1,0:T(8,128)(2,1)S(1)}, bf16[2,112,768]{2,1,0:T(8,128)(2,1)S(1)}, u32[]{:S(2)}, u32[]{:S(2)}) collective-permute-start(bf16[2,112,768]{2,1,0:T(8,128)(2,1)S(1)} %add_convert_fusion.8), channel_id=1, source_target_pairs={{0,8},{1,9},{2,10},{3,11},{4,12},{5,13},{6,14},{7,15},{8,0},{9,1},... | collective-permute-start | bytes 1032200 | tf_op jit(solution)/shard_map/ppermute | solution.py:565
  212.9 15.1 %collective-permute-start.7 = (bf16[128,768]{1,0:T(8,128)(2,1)S(1)}, bf16[128,768]{1,0:T(8,128)(2,1)S(1)}, u32[]{:S(2)}, u32[]{:S(2)}) collective-permute-start(bf16[128,768]{1,0:T(8,128)(2,1)S(1)} %copy-done.30), channel_id=1, source_target_pairs={{0,2},{1,3},{2,0},{3,1},{4,6},{5,7},{6,4},{7,5},{8,10},{9,11},{10,... | collective-permute-start | bytes 589832 | tf_op jit(solution)/shard_map/ppermute | solution.py:569
  218.2 20.0 %collective-permute-start.33 = (bf16[2,192,768]{2,1,0:T(8,128)(2,1)S(1)}, bf16[2,192,768]{2,1,0:T(8,128)(2,1)}, u32[]{:S(2)}, u32[]{:S(2)}) collective-permute-start(bf16[2,192,768]{2,1,0:T(8,128)(2,1)S(1)} %pad_maximum_fusion.near_ref), channel_id=1, source_target_pairs={{0,1},{1,0},{2,3},{3,2},{4,5},{5,4},{6,7},{7,6},{8,9},{9,8},{10,11... | collective-permute-start | bytes 1769480 | tf_op jit(solution)/shard_map/ppermute | solution.py:569
  226.9 10.5 %collective-permute-start.8 = (bf16[128,768]{1,0:T(8,128)(2,1)}, bf16[128,768]{1,0:T(8,128)(2,1)S(1)}, u32[]{:S(2)}, u32[]{:S(2)}) collective-permute-start(bf16[128,768]{1,0:T(8,128)(2,1)} %get-tuple-element.73), channel_id=1, source_target_pairs={{0,3},{1,2},{2,1},{3,0},{4,7},{5,6},{6,5},{7,4},{8,11},{9,10},{10,... | collective-permute-start | bytes 589832 | tf_op jit(solution)/shard_map/ppermute | solution.py:569
  228.0 13.0 %collective-permute-start.21 = (bf16[2,112,768]{2,1,0:T(8,128)(2,1)S(1)}, bf16[2,112,768]{2,1,0:T(8,128)(2,1)S(1)}, u32[]{:S(2)}, u32[]{:S(2)}) collective-permute-start(bf16[2,112,768]{2,1,0:T(8,128)(2,1)S(1)} %pad_maximum_fusion.1.near_ref), channel_id=1, source_target_pairs={{0,1},{1,0},{2,3},{3,2},{4,5},{5,4},{6,7},{7,6},{8,9},{9,8},{10,11... | collective-permute-start | bytes 1032200 | tf_op jit(solution)/shard_map/ppermute | solution.py:569
  (43 other events, 296.5 us)

commit v2 on v1

--- a/solution.py
+++ b/solution.py
@@ -10,6 +10,7 @@
 EPS = 1e-06
 LOG2E = 1.4426950408889634
 BLOCK = 768
+DIGITS = 16
 EXTRA = 16
 f32 = jnp.float32
 bf16 = jnp.bfloat16
@@ -192,7 +193,7 @@
                 douter_ref[part] = low_d
                 for i, v in enumerate((cot * hat, cot, low_d.astype(f32))):
                     lines[i] = lines[i] + jnp.sum(v, axis=0, keepdims=True)
-            for i, v in enumerate(lines):
+            for i, v in enumerate(lines + [valid_rows]):
                 small_ref[i : i + 1] = v
 
     full = lambda a: pl.BlockSpec(a.shape, lambda j: (0,) * a.ndim)
@@ -275,7 +276,7 @@
         assert 2 ** len(bits) == self.nseq and 2 ** len(dp_bits) == self.ndp
         rest = bits[2:] + dp_bits[1:]
         self.first = bits[0]
-        self.orders = [[bits[1], dp_bits[0]] + rest, [dp_bits[0], bits[1]] + rest]
+        self.orders = [[bits[1], dp_bits[0]] + rest, [dp_bits[0]] + rest + [bits[1]]]
         self.steps = len(self.orders[0])
         self.places = 1 << self.steps
 
@@ -318,19 +319,32 @@
             send_ref[at, offset : offset + rows] = tile
 
 
-def ffn_outer_grad(plan, me, active, d_outer):
+def count_bits(count_row):
+    lane = lax.broadcasted_iota(jnp.int32, count_row.shape, 1)
+    return ((count_row.astype(jnp.int32) >> jnp.minimum(lane, DIGITS)) & 1).astype(f32)
+
+
+def ffn_outer_grad(plan, me, active, d_outer, small2):
     n, inner = active.shape
     width = d_outer.shape[1]
     rows = inner // (plan.ndp * plan.nseq)
     per = BLOCK // rows
 
-    def kernel(me_ref, active_ref, d_ref, keep_ref, send_ref):
+    def kernel(me_ref, active_ref, d_ref, small_ref, keep_ref, send_ref):
         j = pl.program_id(0)
+
+        @pl.when(j == 0)
+        def _():
+            below = jnp.broadcast_to(count_bits(small_ref[3:4]), (EXTRA, width)).astype(bf16)
+            for p in range(plan.places):
+                keep_ref[p, rows:] = below
+                send_ref[p, rows:] = below
+
         result = dot(active_ref[...], d_ref[...], 0, 0)
         pieces = [((j * per + i) // plan.nseq, (j * per + i) % plan.nseq) for i in range(per)]
         scatter_pieces(plan, me_ref, result, pieces, keep_ref, send_ref, rows)
 
-    shape = jax.ShapeDtypeStruct((plan.places, rows, width), bf16)
+    shape = jax.ShapeDtypeStruct((plan.places, rows + EXTRA, width), bf16)
     spec = pl.BlockSpec(shape.shape, lambda j, m: (0, 0, 0))
     return pl.pallas_call(
         kernel,
@@ -340,28 +354,25 @@
             in_specs=[
                 pl.BlockSpec((n, BLOCK), lambda j, m: (0, j)),
                 pl.BlockSpec((n, width), lambda j, m: (0, 0)),
+                pl.BlockSpec(small2.shape, lambda j, m: (0, 0)),
             ],
             out_specs=[spec, spec],
         ),
         out_shape=[shape, shape],
         name="outer_grad",
-    )(me, active, d_outer)
-
-
-def ffn_backward(slope, d_outer, wo, wi, d_resid2, hat1, inv1, gain1, wout):
-    n, inner = slope.shape
-    width = d_outer.shape[1]
+    )(me, active, d_outer, small2)
+
+
+def ffn_backward(d_inner, wi, d_resid2, hat1, inv1, gain1, wout):
+    n, inner = d_inner.shape
+    width = d_resid2.shape[1]
 
     def kernel(
-        slope_ref, douter_ref, wo_ref, wi_ref, dres2_ref, hat1_ref, inv1_ref, gain_ref, wout_ref,
-        dinner_ref, dres1_ref, dattn_ref, dctx_ref, ib_ref, small_ref, acc,
+        dinner_ref, wi_ref, dres2_ref, hat1_ref, inv1_ref, gain_ref, wout_ref,
+        dres1_ref, dattn_ref, dctx_ref, small_ref, acc,
     ):
         j = pl.program_id(0)
-        d_active = dot(douter_ref[...], wo_ref[...], 1, 1)
-        d_inner = (d_active * slope_ref[...].astype(f32)).astype(bf16)
-        dinner_ref[...] = d_inner
-        ib_ref[...] = jnp.broadcast_to(jnp.sum(d_inner.astype(f32), axis=0, keepdims=True), ib_ref.shape)
-        back = dot(d_inner, wi_ref[...], 1, 1)
+        back = dot(dinner_ref[...], wi_ref[...], 1, 1)
 
         @pl.when(j == 0)
         def _():
@@ -384,14 +395,11 @@
 
     full = lambda a: pl.BlockSpec(a.shape, lambda j: (0,) * a.ndim)
     whole = lambda shape: pl.BlockSpec(shape, lambda j: (0,) * len(shape))
-    cols = pl.BlockSpec((n, BLOCK), lambda j: (0, j))
     return pl.pallas_call(
         kernel,
         grid=(inner // BLOCK,),
         in_specs=[
-            cols,
-            full(d_outer),
-            pl.BlockSpec((BLOCK, width), lambda j: (j, 0)),
+            pl.BlockSpec((n, BLOCK), lambda j: (0, j)),
             pl.BlockSpec((width, BLOCK), lambda j: (0, j)),
             full(d_resid2),
             full(hat1),
@@ -399,40 +407,36 @@
             full(gain1),
             full(wout),
         ],
-        out_specs=[
-            cols,
-            whole((n, width)),
-            whole((n, width)),
-            whole((n, width)),
-            pl.BlockSpec((8, BLOCK), lambda j: (0, j)),
-            whole((8, width)),
-        ],
+        out_specs=[whole((n, width)), whole((n, width)), whole((n, width)), whole((8, width))],
         scratch_shapes=[pltpu.VMEM((n, width), f32)],
         out_shape=[
-            jax.ShapeDtypeStruct((n, inner), bf16),
             jax.ShapeDtypeStruct((n, width), f32),
             jax.ShapeDtypeStruct((n, width), bf16),
             jax.ShapeDtypeStruct((n, width), bf16),
-            jax.ShapeDtypeStruct((8, inner), f32),
             jax.ShapeDtypeStruct((8, width), f32),
         ],
         name="ffn_bwd",
-    )(slope, d_outer, wo, wi, d_resid2, hat1, inv1, gain1, wout)
-
-
-def ffn_inner_grad(plan, me, n1t, d_inner):
+    )(d_inner, wi, d_resid2, hat1, inv1, gain1, wout)
+
+
+def ffn_inner_grad(plan, me, n1t, slope, d_outer, wo):
     width, n = n1t.shape
-    inner = d_inner.shape[1]
+    inner = slope.shape[1]
     rows = width // plan.ndp
     cols = inner // plan.nseq
 
-    def kernel(me_ref, n1t_ref, d_ref, keep_ref, send_ref):
+    def kernel(me_ref, n1t_ref, slope_ref, douter_ref, wo_ref, keep_ref, send_ref, dinner_ref, ib_ref):
         j = pl.program_id(0)
-        result = dot(n1t_ref[...], d_ref[...], 1, 0)
+        d_active = dot(douter_ref[...], wo_ref[...], 1, 1)
+        d_inner = (d_active * slope_ref[...].astype(f32)).astype(bf16)
+        dinner_ref[...] = d_inner
+        ib_ref[...] = jnp.broadcast_to(jnp.sum(d_inner.astype(f32), axis=0, keepdims=True), ib_ref.shape)
+        result = dot(n1t_ref[...], d_inner, 1, 0)
         scatter_pieces(plan, me_ref, result, [(i, j) for i in range(plan.ndp)], keep_ref, send_ref, rows)
 
     shape = jax.ShapeDtypeStruct((plan.places, rows, cols), bf16)
     spec = pl.BlockSpec(shape.shape, lambda j, m: (0, 0, 0))
+    block = pl.BlockSpec((n, cols), lambda j, m: (0, j))
     return pl.pallas_call(
         kernel,
         grid_spec=pltpu.PrefetchScalarGridSpec(
@@ -440,13 +444,20 @@
             grid=(plan.nseq,),
             in_specs=[
                 pl.BlockSpec((width, n), lambda j, m: (0, 0)),
-                pl.BlockSpec((n, cols), lambda j, m: (0, j)),
+                block,
+                pl.BlockSpec(d_outer.shape, lambda j, m: (0, 0)),
+                pl.BlockSpec((cols, width), lambda j, m: (j, 0)),
             ],
-            out_specs=[spec, spec],
+            out_specs=[spec, spec, block, pl.BlockSpec((8, cols), lambda j, m: (0, j))],
         ),
-        out_shape=[shape, shape],
+        out_shape=[
+            shape,
+            shape,
+            jax.ShapeDtypeStruct((n, inner), bf16),
+            jax.ShapeDtypeStruct((8, inner), f32),
+        ],
         name="inner_grad",
-    )(me, n1t, d_inner)
+    )(me, n1t, slope, d_outer, wo)
 
 
 def finish_tokens(me, factor, pieces):
@@ -596,6 +607,7 @@
         doc_segments,
     ):
         seg_dev, rows_dev, width = tokens.shape
+        assert rows_dev * nseq < (1 << DIGITS) and ndp * nseq <= 256
         assert seg_dev == nseq
         rows = rows_dev * nseq
         mem_rows = memory_init.shape[1]
@@ -630,18 +642,8 @@
         counts_here = jnp.sum(valid, axis=1)
         masked = jnp.where(valid[..., None] != 0, out_grad, jnp.zeros_like(out_grad))
         assert rows_dev <= 256
-        assert seg_dev + 8 <= EXTRA
-        low_counts = counts_here.astype(bf16)
-        below = jnp.broadcast_to(jnp.pad(low_counts, (8, EXTRA - 8 - seg_dev))[None, :], (seg_dev, EXTRA))
-        below = jnp.where(jnp.arange(EXTRA)[None, :] < 8, low_counts[:, None], below)
-        count_rows = jnp.broadcast_to(below[:, :, None], (seg_dev, EXTRA, width))
+        count_rows = jnp.broadcast_to(counts_here.astype(bf16)[:, None, None], (seg_dev, EXTRA, width))
         cot_pieces = to_segments(jnp.concatenate([masked, count_rows], axis=1))
-
-        group = sum(jnp.sum(p[rows_dev + 8 : rows_dev + 8 + seg_dev, :128].astype(f32), axis=0) for p in cot_pieces)
-        total = jnp.broadcast_to(group[None], (8, 128))
-        for b in range(ndp.bit_length() - 1):
-            total = total + lax.ppermute(total, "dp", [(i, i ^ (1 << b)) for i in range(ndp)])
-        factor = total[0, 0] / segs_total
 
         seg_global = dp_index * seg_dev + seq_index
         starts = jnp.cumsum(doc_segments) - doc_segments
@@ -676,30 +678,32 @@
 
         aligned = (width // ndp) % 16 == 0 and (ff // (ndp * nseq)) % 16 == 0 and ff // nseq == BLOCK
         if aligned:
-            keep, send = ffn_outer_grad(plan, me, active, d_outer)
+            keep, send = ffn_outer_grad(plan, me, active, d_outer, small2)
         else:
             grad = dot(active, d_outer, 0, 0).astype(bf16)
-            keep, send = place_pieces(plan, me, grad.reshape(ndp, nseq, -1, width))
+            below = jnp.broadcast_to(count_bits(small2[3:4]), (ndp, nseq, EXTRA, width)).astype(bf16)
+            blocks = jnp.concatenate([grad.reshape(ndp, nseq, -1, width), below], axis=2)
+            keep, send = place_pieces(plan, me, blocks)
         d_outer, keep, send = lax.optimization_barrier((d_outer, keep, send))
         outer = start_chunk(keep, send)
-        d_inner, d_resid1, d_attn, d_context, d_inner_bias, small1 = ffn_backward(
-            slope, d_outer, outer_weight, inner_weight, d_resid2, hat1, inv1, vecs[1:2], output_weight
+        if aligned:
+            keep, send, d_inner, d_inner_bias = ffn_inner_grad(plan, me, n1t, slope, d_outer, outer_weight)
+        else:
+            d_inner = (dot(d_outer, outer_weight, 1, 1) * slope.astype(f32)).astype(bf16)
+            d_inner_bias = jnp.broadcast_to(jnp.sum(d_inner.astype(f32), axis=0), (8, ff))
+            grad = dot(n1t, d_inner, 1, 0).astype(bf16)
+            grad = grad.reshape(ndp, width // ndp, nseq, ff // nseq).transpose(0, 2, 1, 3)
+            keep, send = place_pieces(plan, me, grad)
+        inner = start_chunk(keep, send)
+        outer = step_chunk(outer, 0)
+        d_resid1, d_attn, d_context, small1 = ffn_backward(
+            d_inner, inner_weight, d_resid2, hat1, inv1, vecs[1:2], output_weight
         )
-        outer = step_chunk(outer, 0)
+        inner = step_chunk(inner, 0)
         d_queries, d_keys, d_values = attention_backward(
             queries, keys, values, context, d_context, probs, 1, rows
         )
-        d_queries, d_inner = lax.optimization_barrier((d_queries, d_inner))
         outer = step_chunk(outer, 1)
-        if aligned:
-            keep, send = ffn_inner_grad(plan, me, n1t, d_inner)
-        else:
-            grad = dot(n1t, d_inner, 1, 0).astype(bf16)
-            grad = grad.reshape(ndp, width // ndp, nseq, ff // nseq).transpose(0, 2, 1, 3)
-            keep, send = place_pieces(plan, me, grad)
-        d_queries, keep, send = lax.optimization_barrier((d_queries, keep, send))
-        inner = start_chunk(keep, send)
-        outer = step_chunk(outer, 2)
         cut_pieces, small = inputs_backward(
             me,
             (d_queries, d_keys, d_values),
@@ -726,18 +730,20 @@
             below = jnp.broadcast_to(small.astype(bf16)[None], (ndp,) + small.shape)
             keep, send = place_pieces(plan, me, jnp.concatenate([blocks, below], axis=2))
         attn = start_chunk(keep, send)
-        inner = step_chunk(inner, 0)
-        for step in range(3, plan.steps):
+        for step in range(2, plan.steps):
             outer = step_chunk(outer, step)
         for step in range(1, plan.steps):
             inner = step_chunk(inner, step)
         for step in range(plan.steps):
             attn = step_chunk(attn, step)
-        ffn_near, ffn_far = gather_seq(jnp.concatenate([total_of(outer)[0], total_of(inner)[0]], axis=0).astype(bf16))
+        outer_rows = ff // (ndp * nseq)
+        outer = total_of(outer)[0]
+        total = jnp.sum(outer[outer_rows, :DIGITS] * (2.0 ** jnp.arange(DIGITS)).astype(f32))
+        factor = total / segs_total
+        ffn_near, ffn_far = gather_seq(jnp.concatenate([outer[:outer_rows], total_of(inner)[0]], axis=0).astype(bf16))
         attn_near, attn_far = gather_seq(total_of(attn)[0].astype(bf16))
 
         part = width // ndp
-        outer_rows = ff // (ndp * nseq)
         scale = factor.reshape(1)
         if aligned:
             tokens_grad = finish_tokens(me, scale, cut_pieces)

time: 249 us -> 264 us (1.060)
  waiting for transfers between devices: 51.2 us -> 64.8 us
  starting transfers between devices: 43.9 us -> 46.8 us
    ppermute x16, starting transfers between devices: 13.2 us -> 31.4 us  [swap_seq(): return lax.ppermute(x, 'seq', [(i, i ^ k) for i in range(nseq)])]
    ppermute x12, starting transfers between devices: 23.8 us -> 14.9 us  [step_chunk(): got = lax.ppermute(send, devices, plan.perm(step))]
    ppermute x16, waiting for transfers between devices: 10.6 us -> 18.8 us  [swap_seq(): return lax.ppermute(x, 'seq', [(i, i ^ k) for i in range(nseq)])]
    ppermute x12, waiting for transfers between devices: 38.6 us -> 46 us  [step_chunk(): got = lax.ppermute(send, devices, plan.perm(step))]
    ppermute x3 -> x0, starting transfers between devices: 6.28 us -> none  [per_device(): lax.ppermute(total, 'dp', [(i, i ^ 1 << b) for i in range(ndp)])]
    pallas_call x1, Pallas kernels: 15 us -> 10.8 us  [ffn_backward(): pl.pallas_call(kernel, grid=(inner // BLOCK,), in_specs=[pl.BlockSpec((n,...]
    pallas_call x1, Pallas kernels: 8.47 us -> 12.1 us  [ffn_inner_grad(): pl.pallas_call(kernel, grid_spec=pltpu.PrefetchScalarGridSpec(num_scalar_...]
    unnamed x66 -> x60, local copies, waits for them, and re-layouts: 1.93 us -> 5.18 us
  transfers between devices with their start and end apart: 34 -> 31, of which waited for: 14 -> 13; matrix products, arithmetic and copies ran while one was open for 17% -> 15% of each run, Pallas kernels for 28% -> 26%
where the time goes in v2:
time: 264 us; the launch traced here: 263 us
  Pallas kernels  101 us (38%)
  waiting for transfers between devices  64.8 us (25%)
  starting transfers between devices  46.8 us (18%)
  other arithmetic  30.8 us (12%)
  local copies, waits for them, and re-layouts  12.5 us (5%)
  matrix products  5.02 us (2%)
    ppermute x12, waiting for transfers between devices, step_chunk(): got = lax.ppermute(send, devices, plan.perm(step))  46 us
    ppermute x16, starting transfers between devices, swap_seq(): return lax.ppermute(x, 'seq', [(i, i ^ k) for i in range(nseq)])  31.4 us
    pallas_call x1, Pallas kernels, ffn_forward(): pl.pallas_call(kernel, grid=(inner // BLOCK,), in_specs=[full(flat), full...  21.4 us
    convert_element_type x12, other arithmetic, step_chunk(): send = total_of([t[half:] for t in terms]).astype(bf16)  19.1 us
    ppermute x16, waiting for transfers between devices, swap_seq(): return lax.ppermute(x, 'seq', [(i, i ^ k) for i in range(nseq)])  18.8 us
    ppermute x12, starting transfers between devices, step_chunk(): got = lax.ppermute(send, devices, plan.perm(step))  14.9 us
    pallas_call x1, Pallas kernels, attention_backward(): pl.pallas_call(attn_bwd_kernel, grid=(segs, pairs), in_specs=[spec] * 5 +...  12.4 us
    pallas_call x1, Pallas kernels, ffn_inner_grad(): pl.pallas_call(kernel, grid_spec=pltpu.PrefetchScalarGridSpec(num_scalar_...  12.1 us
  transfers between devices with their start and end apart: 31, of which 13 were waited for; matrix products, arithmetic and copies ran while one was open for 15% of the time, Pallas kernels for 26%

profile of v2, /device:TPU:0, one launch (start us, length us, event | category | flops | bytes accessed | tf_op | source)
XLA Modules:
  0.0 263.2 jit_solution(11148706708830587564)
XLA Ops:
  17.3 5.2 %collective-permute-done.1 = bf16[128,768]{1,0:T(8,128)(2,1)S(1)} collective-permute-done((bf16[128,768]{1,0:T(8,128)(2,1)S(1)}, bf16[128,768]{1,0:T(8,128)(2,1)S(1)}, u32[]{:S(2)}, u32[]{:S(2)}) %collective-permute-start.1) | collective-permute-done | bytes 196640 | tf_op jit(solution)/shard_map/ppermute | solution.py:580
  27.9 11.4 %attn_fwd.1 = (bf16[512,768]{1,0:T(8,128)(2,1)}, bf16[12,512,512]{2,1,0:T(8,128)(2,1)}) custom-call(bf16[512,768]{1,0:T(8,128)(2,1)} %add_convert_fusion.4.q_ref, bf16[512,768]{1,0:T(8,128)(2,1)} %convolution_convert_fusion.k_ref, bf16[512,768]{1,0:T(8,128)(2,1)} %add_convert_fusion.3.v_ref), custom_call_target="tpu_custom_call" | custom-call | tf_op jit(solution)/shard_map/attn_fwd/pallas_call | solution.py:80
  39.3 21.4 %ffn_fwd.1 = (f32[512,768]{1,0:T(8,128)}, f32[512,128]{1,0:T(8,128)}, bf16[768,512]{1,0:T(8,128)(2,1)}, bf16[512,3072]{1,0:T(8,128)(2,1)}, bf16[512,3072]{1,0:T(...) custom-call(bf16[512,768]{1,0:T(8,128)(2,1)} %copy-done, ...), custom_call_target="tpu_custom_call" | custom-call | tf_op jit(solution)/shard_map/ffn_fwd/pallas_call | solution.py:211
  60.8 8.8 %outer_grad.1 = (bf16[16,112,768]{2,1,0:T(8,128)(2,1)}, bf16[16,112,768]{2,1,0:T(8,128)(2,1)}) custom-call(s32[3]{0:T(128)} %pad_add_fusion.me_ref, bf16[512,3072]{1,0:T(8,128)(2,1)} %get-tuple-element.70.active_ref, bf16[512,768]{1,0:T(8,128)(2,1)} %get-tuple-element.78.d_ref.douter_ref, f32[8,768]{1,0:T(8,128)} %get-tuple-element.71.small_ref.s2_ref), custom_call_target="tpu_custom_call" | custom-call | tf_op jit(solution)/shard_map/outer_grad/pallas_call | solution.py:349
  69.6 12.1 %inner_grad.1 = (bf16[16,96,768]{2,1,0:T(8,128)(2,1)}, bf16[16,96,768]{2,1,0:T(8,128)(2,1)}, bf16[512,3072]{1,0:T(8,128)(2,1)}, f32[8,3072]{1,0:T(8,128)}) custom-call(s32[3]{0:T(128)} %pad_add_fusion.me_ref, bf16[768,512]{1,0:T(8,128)(2,1)} %get-tuple-element.76.n1t_ref, bf16[512,3072]{1,0:T(8,128)(2,1)} %get-tuple-element.77.slope_ref, ...), custom_call_target="tpu_custom_call" | custom-call | tf_op jit(solution)/shard_map/inner_grad/pallas_call | solution.py:440
  82.7 10.8 %ffn_bwd.1 = (f32[512,768]{1,0:T(8,128)}, bf16[512,768]{1,0:T(8,128)(2,1)}, bf16[512,768]{1,0:T(8,128)(2,1)}, f32[8,768]{1,0:T(8,128)}) custom-call(bf16[512,3072]{1,0:T(8,128)(2,1)} %get-tuple-element.79.dinner_ref, bf16[768,3072]{1,0:T(8,128)(2,1)} %wi_ref.3, f32[512,768]{1,0:T(8,128)} %get-tuple-element.80.dres2_ref, ...), custom_call_target="tpu_custom_call" | custom-call | tf_op jit(solution)/shard_map/ffn_bwd/pallas_call | solution.py:398
  93.5 12.4 %attn_bwd.1 = (bf16[512,768]{1,0:T(8,128)(2,1)}, bf16[512,768]{1,0:T(8,128)(2,1)}, bf16[512,768]{1,0:T(8,128)(2,1)}) custom-call(bf16[512,768]{1,0:T(8,128)(2,1)} %add_convert_fusion.4.q_ref, bf16[512,768]{1,0:T(8,128)(2,1)} %convolution_convert_fusion.k_ref, bf16[512,768]{1,0:T(8,128)(2,1)} %add_convert_fusion.3.v_ref, ...), custom_call_target="tpu_custom_call" | custom-call | tf_op jit(solution)/shard_map/attn_bwd/pallas_call | solution.py:99
  105.9 6.3 %inputs_bwd.1 = (bf16[128,768]{1,0:T(8,128)(2,1)}, bf16[128,768]{1,0:T(8,128)(2,1)}, bf16[128,768]{1,0:T(8,128)(2,1)}, bf16[128,768]{1,0:T(8,128)(2,1)}, f32[4,16,768]{2,1,0:T(8,128)}) custom-call(s32[3]{0:T(128)} %pad_add_fusion.me_ref, bf16[512,768]{1,0:T(8,128)(2,1)} %get-tuple-element.85.dq_ref.d0_ref, bf16[512,768]{1,0:T(8,128)(2,1)} %get-tuple-element.86.dk_ref.d1_ref, ...), custom_call_target="tpu_custom_call" | custom-call | tf_op jit(solution)/shard_map/inputs_bwd/pallas_call | solution.py:260
  112.2 9.9 %attn_grad.1 = (bf16[16,112,768]{2,1,0:T(8,128)(2,1)}, bf16[16,112,768]{2,1,0:T(8,128)(2,1)}) custom-call(s32[3]{0:T(128)} %pad_add_fusion.me_ref, bf16[512,768]{1,0:T(8,128)(2,1)} %copy-done, bf16[512,768]{1,0:T(8,128)(2,1)} %get-tuple-element.64.ctx_ref, bf16[512,768]{1,0:T(8,128)(2,1)} %get-tuple-element.85.dq_ref.d0_ref, ...), custom_call_target="tpu_custom_call" | custom-call | tf_op jit(solution)/shard_map/attn_grad/pallas_call | solution.py:537
  127.2 2.8 %add_convert_fusion.1 = bf16[8,112,768]{2,1,0:T(8,128)(2,1)} fusion(bf16[16,112,768]{2,1,0:T(8,128)(2,1)} %collective-permute-done.9, bf16[16,112,768]{2,1,0:T(8,128)(2,1)S(1)} %copy-done.1), kind=kLoop, calls=%fused_computation.1 | loop fusion | flops 2752512 | bytes 4128768 | tf_op jit(solution)/shard_map/convert_element_type | solution.py:575
  134.0 7.9 %collective-permute-done.25 = bf16[8,96,768]{2,1,0:T(8,128)(2,1)S(1)} collective-permute-done((bf16[8,96,768]{2,1,0:T(8,128)(2,1)S(1)}, bf16[8,96,768]{2,1,0:T(8,128)(2,1)S(1)}, u32[]{:S(2)}, u32[]{:S(2)}) %collective-permute-start.25) | collective-permute-done | bytes 1179680 | tf_op jit(solution)/shard_map/ppermute | solution.py:576
  149.3 9.6 %collective-permute-done.10 = bf16[8,112,768]{2,1,0:T(8,128)(2,1)} collective-permute-done((bf16[8,112,768]{2,1,0:T(8,128)(2,1)}, bf16[8,112,768]{2,1,0:T(8,128)(2,1)}, u32[]{:S(2)}, u32[]{:S(2)}) %collective-permute-start.10) | collective-permute-done | bytes 1376288 | tf_op jit(solution)/shard_map/ppermute | solution.py:576
  158.9 4.9 %collective-permute-start.8 = (bf16[128,768]{1,0:T(8,128)(2,1)}, bf16[128,768]{1,0:T(8,128)(2,1)S(1)}, u32[]{:S(2)}, u32[]{:S(2)}) collective-permute-start(bf16[128,768]{1,0:T(8,128)(2,1)} %get-tuple-element.68), channel_id=1, source_target_pairs={{0,3},{1,2},{2,1},{3,0},{4,7},{5,6},{6,5},{7,4},{8,11},{9,10},{10,... | collective-permute-start | bytes 589832 | tf_op jit(solution)/shard_map/ppermute | solution.py:580
  168.2 7.5 %collective-permute-done.18 = bf16[8,112,768]{2,1,0:T(8,128)(2,1)} collective-permute-done((bf16[8,112,768]{2,1,0:T(8,128)(2,1)}, bf16[8,112,768]{2,1,0:T(8,128)(2,1)}, u32[]{:S(2)}, u32[]{:S(2)}) %collective-permute-start.18) | collective-permute-done | bytes 1376288 | tf_op jit(solution)/shard_map/ppermute | solution.py:576
  182.5 12.9 %collective-permute-start.14 = (bf16[128,768]{1,0:T(8,128)(2,1)}, bf16[128,768]{1,0:T(8,128)(2,1)}, u32[]{:S(2)}, u32[]{:S(2)}) collective-permute-start(bf16[128,768]{1,0:T(8,128)(2,1)} %get-tuple-element.92), channel_id=1, source_target_pairs={{0,1},{1,0},{2,3},{3,2},{4,5},{5,4},{6,7},{7,6},{8,9},{9,8},{10,11... | collective-permute-start | bytes 589832 | tf_op jit(solution)/shard_map/ppermute | solution.py:580
  197.9 4.1 %collective-permute-start.12 = (bf16[2,112,768]{2,1,0:T(8,128)(2,1)S(1)}, bf16[2,112,768]{2,1,0:T(8,128)(2,1)S(1)}, u32[]{:S(2)}, u32[]{:S(2)}) collective-permute-start(bf16[2,112,768]{2,1,0:T(8,128)(2,1)S(1)} %add_convert_fusion.9), channel_id=1, source_target_pairs={{0,8},{1,17},{2,10},{3,19},{4,12},{5,21},{6,14},{7,23},{8,0},{9,25... | collective-permute-start | bytes 1032200 | tf_op jit(solution)/shard_map/ppermute | solution.py:576
  205.5 5.0 %collective-permute-done.12 = bf16[2,112,768]{2,1,0:T(8,128)(2,1)S(1)} collective-permute-done((bf16[2,112,768]{2,1,0:T(8,128)(2,1)S(1)}, bf16[2,112,768]{2,1,0:T(8,128)(2,1)S(1)}, u32[]{:S(2)}, u32[]{:S(2)}) %collective-permute-start.12) | collective-permute-done | bytes 344096 | tf_op jit(solution)/shard_map/ppermute | solution.py:576
  214.0 3.6 %collective-permute-done.20 = bf16[2,112,768]{2,1,0:T(8,128)(2,1)S(1)} collective-permute-done((bf16[2,112,768]{2,1,0:T(8,128)(2,1)S(1)}, bf16[2,112,768]{2,1,0:T(8,128)(2,1)S(1)}, u32[]{:S(2)}, u32[]{:S(2)}) %collective-permute-start.20) | collective-permute-done | bytes 344096 | tf_op jit(solution)/shard_map/ppermute | solution.py:576
  219.2 4.7 %collective-permute-done.13 = bf16[1,112,768]{2,1,0:T(8,128)(2,1)S(1)} collective-permute-done((bf16[1,112,768]{2,1,0:T(8,128)(2,1)S(1)}, bf16[1,112,768]{2,1,0:T(8,128)(2,1)S(1)}, u32[]{:S(2)}, u32[]{:S(2)}) %collective-permute-start.13) | collective-permute-done | bytes 172064 | tf_op jit(solution)/shard_map/ppermute | solution.py:576
  225.6 4.6 %collective-permute-done.21 = bf16[1,112,768]{2,1,0:T(8,128)(2,1)S(1)} collective-permute-done((bf16[1,112,768]{2,1,0:T(8,128)(2,1)S(1)}, bf16[1,112,768]{2,1,0:T(8,128)(2,1)S(1)}, u32[]{:S(2)}, u32[]{:S(2)}) %collective-permute-start.21) | collective-permute-done | bytes 172064 | tf_op jit(solution)/shard_map/ppermute | solution.py:576
  233.8 8.6 %collective-permute-done.22 = bf16[112,768]{1,0:T(8,128)(2,1)S(1)} collective-permute-done((bf16[112,768]{1,0:T(8,128)(2,1)S(1)}, bf16[112,768]{1,0:T(8,128)(2,1)S(1)}, u32[]{:S(2)}, u32[]{:S(2)}) %collective-permute-start.22) | collective-permute-done | bytes 172064 | tf_op jit(solution)/shard_map/ppermute | solution.py:580
  246.0 3.3 %collective-permute-done.16.refs_3_ = bf16[128,768]{1,0:T(8,128)(2,1)S(1)} collective-permute-done((bf16[128,768]{1,0:T(8,128)(2,1)S(1)}, bf16[128,768]{1,0:T(8,128)(2,1)S(1)}, u32[]{:S(2)}, u32[]{:S(2)}) %collective-permute-start.16) | collective-permute-done | bytes 196640 | tf_op jit(solution)/shard_map/ppermute | solution.py:580
  250.0 2.5 finish_tok.1
  260.4 2.8 %shard_map.332 = (f32[384,768]{1,0:T(8,128)}, f32[96,3072]{1,0:T(8,128)}) custom-call(s32[3]{0:T(128)} %pad_add_fusion.me_ref, f32[1]{0:T(128)} %bitcast.22.factor_ref, bf16[2,192,768]{2,1,0:T(8,128)(2,1)} %copy-done.6, bf16[2,192,768]{2,1,0:T(8,128)(2,1)} %copy-done.15), custom_call_target="tpu_custom_call" | custom-call | tf_op jit(solution)/shard_map/pallas_call | solution.py:513
  (174 shorter events, 77.4 us)
Async XLA Ops:
  4.7 34.6 %collective-permute-start.5 = (bf16[144,768]{1,0:T(8,128)(2,1)}, bf16[144,768]{1,0:T(8,128)(2,1)}, u32[]{:S(2)}, u32[]{:S(2)}) collective-permute-start(bf16[144,768]{1,0:T(8,128)(2,1)} %get-tuple-element.110), channel_id=1, source_target_pairs={{0,3},{1,2},{2,1},{3,0},{4,7},{5,6},{6,5},{7,4},{8,11},{9,10},{10,... | collective-permute-start | bytes 663560 | tf_op jit(solution)/shard_map/ppermute | solution.py:580
  7.1 32.2 %collective-permute-start.3 = (bf16[144,768]{1,0:T(8,128)(2,1)}, bf16[144,768]{1,0:T(8,128)(2,1)}, u32[]{:S(2)}, u32[]{:S(2)}) collective-permute-start(bf16[144,768]{1,0:T(8,128)(2,1)} %get-tuple-element.112), channel_id=1, source_target_pairs={{0,1},{1,0},{2,3},{3,2},{4,5},{5,4},{6,7},{7,6},{8,9},{9,8},{10,11... | collective-permute-start | bytes 663560 | tf_op jit(solution)/shard_map/ppermute | solution.py:580
  7.9 9.4 %collective-permute-start.2 = (bf16[128,768]{1,0:T(8,128)(2,1)S(1)}, bf16[128,768]{1,0:T(8,128)(2,1)S(1)}, u32[]{:S(2)}, u32[]{:S(2)}) collective-permute-start(bf16[128,768]{1,0:T(8,128)(2,1)S(1)} %get-tuple-element.116), channel_id=1, source_target_pairs={{0,3},{1,2},{2,1},{3,0},{4,7},{5,6},{6,5},{7,4},{8,11},{9,10},{10,... | collective-permute-start | bytes 589832 | tf_op jit(solution)/shard_map/ppermute | solution.py:580
  8.0 14.6 %collective-permute-start.1 = (bf16[128,768]{1,0:T(8,128)(2,1)S(1)}, bf16[128,768]{1,0:T(8,128)(2,1)S(1)}, u32[]{:S(2)}, u32[]{:S(2)}) collective-permute-start(bf16[128,768]{1,0:T(8,128)(2,1)S(1)} %get-tuple-element.117), channel_id=1, source_target_pairs={{0,2},{1,3},{2,0},{3,1},{4,6},{5,7},{6,4},{7,5},{8,10},{9,11},{10,... | collective-permute-start | bytes 589832 | tf_op jit(solution)/shard_map/ppermute | solution.py:580
  15.6 23.7 %collective-permute-start.4 = (bf16[144,768]{1,0:T(8,128)(2,1)}, bf16[144,768]{1,0:T(8,128)(2,1)}, u32[]{:S(2)}, u32[]{:S(2)}) collective-permute-start(bf16[144,768]{1,0:T(8,128)(2,1)} %get-tuple-element.113), channel_id=1, source_target_pairs={{0,2},{1,3},{2,0},{3,1},{4,6},{5,7},{6,4},{7,5},{8,10},{9,11},{10,... | collective-permute-start | bytes 663560 | tf_op jit(solution)/shard_map/ppermute | solution.py:580
  69.6 57.6 %collective-permute-start.9 = (bf16[16,112,768]{2,1,0:T(8,128)(2,1)}, bf16[16,112,768]{2,1,0:T(8,128)(2,1)}, u32[]{:S(2)}, u32[]{:S(2)}) collective-permute-start(bf16[16,112,768]{2,1,0:T(8,128)(2,1)} %get-tuple-element.75), channel_id=1, source_target_pairs={{0,1},{1,0},{2,3},{3,2},{4,5},{5,4},{6,7},{7,6},{8,9},{9,8},{10,11... | collective-permute-start | bytes 8257544 | tf_op jit(solution)/shard_map/ppermute | solution.py:571
  81.6 40.5 %collective-permute-start.24 = (bf16[16,96,768]{2,1,0:T(8,128)(2,1)}, bf16[16,96,768]{2,1,0:T(8,128)(2,1)S(1)}, u32[]{:S(2)}, u32[]{:S(2)}) collective-permute-start(bf16[16,96,768]{2,1,0:T(8,128)(2,1)} %get-tuple-element.105), channel_id=1, source_target_pairs={{0,1},{1,0},{2,3},{3,2},{4,5},{5,4},{6,7},{7,6},{8,9},{9,8},{10,11... | collective-permute-start | bytes 7077896 | tf_op jit(solution)/shard_map/ppermute | solution.py:571
  125.7 16.3 %collective-permute-start.25 = (bf16[8,96,768]{2,1,0:T(8,128)(2,1)S(1)}, bf16[8,96,768]{2,1,0:T(8,128)(2,1)S(1)}, u32[]{:S(2)}, u32[]{:S(2)}) collective-permute-start(bf16[8,96,768]{2,1,0:T(8,128)(2,1)S(1)} %add_convert_fusion.2), channel_id=1, source_target_pairs={{0,2},{1,5},{2,0},{3,7},{4,6},{5,1},{6,4},{7,3},{8,10},{9,13},{10,... | collective-permute-start | bytes 3538952 | tf_op jit(solution)/shard_map/ppermute | solution.py:576
  130.0 28.9 %collective-permute-start.10 = (bf16[8,112,768]{2,1,0:T(8,128)(2,1)}, bf16[8,112,768]{2,1,0:T(8,128)(2,1)}, u32[]{:S(2)}, u32[]{:S(2)}) collective-permute-start(bf16[8,112,768]{2,1,0:T(8,128)(2,1)} %add_convert_fusion.1), channel_id=1, source_target_pairs={{0,2},{1,5},{2,0},{3,7},{4,6},{5,1},{6,4},{7,3},{8,10},{9,13},{10,... | collective-permute-start | bytes 4128776 | tf_op jit(solution)/shard_map/ppermute | solution.py:576
  132.7 43.0 %collective-permute-start.18 = (bf16[8,112,768]{2,1,0:T(8,128)(2,1)}, bf16[8,112,768]{2,1,0:T(8,128)(2,1)}, u32[]{:S(2)}, u32[]{:S(2)}) collective-permute-start(bf16[8,112,768]{2,1,0:T(8,128)(2,1)} %add_convert_fusion), channel_id=1, source_target_pairs={{0,2},{1,5},{2,0},{3,7},{4,6},{5,1},{6,4},{7,3},{8,10},{9,13},{10,... | collective-permute-start | bytes 4128776 | tf_op jit(solution)/shard_map/ppermute | solution.py:576
  145.2 20.2 %collective-permute-start.26 = (bf16[4,96,768]{2,1,0:T(8,128)(2,1)}, bf16[4,96,768]{2,1,0:T(8,128)(2,1)}, u32[]{:S(2)}, u32[]{:S(2)}) collective-permute-start(bf16[4,96,768]{2,1,0:T(8,128)(2,1)} %add_convert_fusion.7), channel_id=1, source_target_pairs={{0,4},{1,9},{2,6},{3,11},{4,0},{5,13},{6,2},{7,15},{8,12},{9,1},{1... | collective-permute-start | bytes 1769480 | tf_op jit(solution)/shard_map/ppermute | solution.py:576
  146.7 32.2 %collective-permute-start.6 = (bf16[128,768]{1,0:T(8,128)(2,1)}, bf16[128,768]{1,0:T(8,128)(2,1)S(1)}, u32[]{:S(2)}, u32[]{:S(2)}) collective-permute-start(bf16[128,768]{1,0:T(8,128)(2,1)} %get-tuple-element.66), channel_id=1, source_target_pairs={{0,1},{1,0},{2,3},{3,2},{4,5},{5,4},{6,7},{7,6},{8,9},{9,8},{10,11... | collective-permute-start | bytes 589832 | tf_op jit(solution)/shard_map/ppermute | solution.py:580
  146.7 87.0 %collective-permute-start.7 = (bf16[128,768]{1,0:T(8,128)(2,1)}, bf16[128,768]{1,0:T(8,128)(2,1)S(1)}, u32[]{:S(2)}, u32[]{:S(2)}) collective-permute-start(bf16[128,768]{1,0:T(8,128)(2,1)} %get-tuple-element.67), channel_id=1, source_target_pairs={{0,2},{1,3},{2,0},{3,1},{4,6},{5,7},{6,4},{7,5},{8,10},{9,11},{10,... | collective-permute-start | bytes 589832 | tf_op jit(solution)/shard_map/ppermute | solution.py:580
  158.9 85.5 %collective-permute-start.8 = (bf16[128,768]{1,0:T(8,128)(2,1)}, bf16[128,768]{1,0:T(8,128)(2,1)S(1)}, u32[]{:S(2)}, u32[]{:S(2)}) collective-permute-start(bf16[128,768]{1,0:T(8,128)(2,1)} %get-tuple-element.68), channel_id=1, source_target_pairs={{0,3},{1,2},{2,1},{3,0},{4,7},{5,6},{6,5},{7,4},{8,11},{9,10},{10,... | collective-permute-start | bytes 589832 | tf_op jit(solution)/shard_map/ppermute | solution.py:580
  165.4 31.2 %collective-permute-start.11 = (bf16[4,112,768]{2,1,0:T(8,128)(2,1)S(1)}, bf16[4,112,768]{2,1,0:T(8,128)(2,1)S(1)}, u32[]{:S(2)}, u32[]{:S(2)}) collective-permute-start(bf16[4,112,768]{2,1,0:T(8,128)(2,1)S(1)} %add_convert_fusion.6), channel_id=1, source_target_pairs={{0,4},{1,9},{2,6},{3,11},{4,0},{5,13},{6,2},{7,15},{8,12},{9,1},{1... | collective-permute-start | bytes 2064392 | tf_op jit(solution)/shard_map/ppermute | solution.py:576
  178.9 19.0 %collective-permute-start.19 = (bf16[4,112,768]{2,1,0:T(8,128)(2,1)S(1)}, bf16[4,112,768]{2,1,0:T(8,128)(2,1)S(1)}, u32[]{:S(2)}, u32[]{:S(2)}) collective-permute-start(bf16[4,112,768]{2,1,0:T(8,128)(2,1)S(1)} %add_convert_fusion.5), channel_id=1, source_target_pairs={{0,4},{1,9},{2,6},{3,11},{4,0},{5,13},{6,2},{7,15},{8,12},{9,1},{1... | collective-permute-start | bytes 2064392 | tf_op jit(solution)/shard_map/ppermute | solution.py:576
  182.5 63.5 %collective-permute-start.14 = (bf16[128,768]{1,0:T(8,128)(2,1)}, bf16[128,768]{1,0:T(8,128)(2,1)}, u32[]{:S(2)}, u32[]{:S(2)}) collective-permute-start(bf16[128,768]{1,0:T(8,128)(2,1)} %get-tuple-element.92), channel_id=1, source_target_pairs={{0,1},{1,0},{2,3},{3,2},{4,5},{5,4},{6,7},{7,6},{8,9},{9,8},{10,11... | collective-permute-start | bytes 589832 | tf_op jit(solution)/shard_map/ppermute | solution.py:580
  197.9 12.6 %collective-permute-start.12 = (bf16[2,112,768]{2,1,0:T(8,128)(2,1)S(1)}, bf16[2,112,768]{2,1,0:T(8,128)(2,1)S(1)}, u32[]{:S(2)}, u32[]{:S(2)}) collective-permute-start(bf16[2,112,768]{2,1,0:T(8,128)(2,1)S(1)} %add_convert_fusion.9), channel_id=1, source_target_pairs={{0,8},{1,17},{2,10},{3,19},{4,12},{5,21},{6,14},{7,23},{8,0},{9,25... | collective-permute-start | bytes 1032200 | tf_op jit(solution)/shard_map/ppermute | solution.py:576
  204.3 13.3 %collective-permute-start.20 = (bf16[2,112,768]{2,1,0:T(8,128)(2,1)S(1)}, bf16[2,112,768]{2,1,0:T(8,128)(2,1)S(1)}, u32[]{:S(2)}, u32[]{:S(2)}) collective-permute-start(bf16[2,112,768]{2,1,0:T(8,128)(2,1)S(1)} %add_convert_fusion.8), channel_id=1, source_target_pairs={{0,8},{1,17},{2,10},{3,19},{4,12},{5,21},{6,14},{7,23},{8,0},{9,25... | collective-permute-start | bytes 1032200 | tf_op jit(solution)/shard_map/ppermute | solution.py:576
  210.5 35.5 %collective-permute-start.15 = (bf16[128,768]{1,0:T(8,128)(2,1)}, bf16[128,768]{1,0:T(8,128)(2,1)}, u32[]{:S(2)}, u32[]{:S(2)}) collective-permute-start(bf16[128,768]{1,0:T(8,128)(2,1)} %get-tuple-element.93), channel_id=1, source_target_pairs={{0,2},{1,3},{2,0},{3,1},{4,6},{5,7},{6,4},{7,5},{8,10},{9,11},{10,... | collective-permute-start | bytes 589832 | tf_op jit(solution)/shard_map/ppermute | solution.py:580
  230.2 12.2 %collective-permute-start.29 = (bf16[192,768]{1,0:T(8,128)(2,1)S(1)}, bf16[192,768]{1,0:T(8,128)(2,1)S(1)}, u32[]{:S(2)}, u32[]{:S(2)}) collective-permute-start(bf16[192,768]{1,0:T(8,128)(2,1)S(1)} %pad_maximum_fusion.2), channel_id=1, source_target_pairs={{0,2},{1,3},{2,0},{3,1},{4,6},{5,7},{6,4},{7,5},{8,10},{9,11},{10,... | collective-permute-start | bytes 884744 | tf_op jit(solution)/shard_map/ppermute | solution.py:580
  233.7 8.7 %collective-permute-start.22 = (bf16[112,768]{1,0:T(8,128)(2,1)S(1)}, bf16[112,768]{1,0:T(8,128)(2,1)S(1)}, u32[]{:S(2)}, u32[]{:S(2)}) collective-permute-start(bf16[112,768]{1,0:T(8,128)(2,1)S(1)} %bitcast.77), channel_id=1, source_target_pairs={{0,2},{1,3},{2,0},{3,1},{4,6},{5,7},{6,4},{7,5},{8,10},{9,11},{10,... | collective-permute-start | bytes 516104 | tf_op jit(solution)/shard_map/ppermute | solution.py:580
  242.4 10.0 %collective-permute-start.23 = (bf16[2,112,768]{2,1,0:T(8,128)(2,1)S(1)}, bf16[2,112,768]{2,1,0:T(8,128)(2,1)S(1)}, u32[]{:S(2)}, u32[]{:S(2)}) collective-permute-start(bf16[2,112,768]{2,1,0:T(8,128)(2,1)S(1)} %pad_maximum_fusion.1.near_ref), channel_id=1, source_target_pairs={{0,1},{1,0},{2,3},{3,2},{4,5},{5,4},{6,7},{7,6},{8,9},{9,8},{10,11... | collective-permute-start | bytes 1032200 | tf_op jit(solution)/shard_map/ppermute | solution.py:580
  244.4 15.1 %collective-permute-start.30 = (bf16[2,192,768]{2,1,0:T(8,128)(2,1)S(1)}, bf16[2,192,768]{2,1,0:T(8,128)(2,1)S(1)}, u32[]{:S(2)}, u32[]{:S(2)}) collective-permute-start(bf16[2,192,768]{2,1,0:T(8,128)(2,1)S(1)} %pad_maximum_fusion.near_ref), channel_id=1, source_target_pairs={{0,1},{1,0},{2,3},{3,2},{4,5},{5,4},{6,7},{7,6},{8,9},{9,8},{10,11... | collective-permute-start | bytes 1769480 | tf_op jit(solution)/shard_map/ppermute | solution.py:580
  (37 other events, 262.0 us)

commit v3 on v2

--- a/solution.py
+++ b/solution.py
@@ -10,8 +10,9 @@
 EPS = 1e-06
 LOG2E = 1.4426950408889634
 BLOCK = 768
+PART = 256
 DIGITS = 16
-EXTRA = 16
+EXTRA = 8
 f32 = jnp.float32
 bf16 = jnp.bfloat16
 
@@ -168,12 +169,17 @@
             n1t_ref[...] = normed.astype(bf16).T
             acc[...] = normed + vec_ref[3:4]
 
-        inner = dot(low[...], wi_ref[...], 1, 0) + ib_ref[...]
-        cdf, bell = upper_tail(inner)
-        active = (inner * cdf).astype(bf16)
-        active_ref[...] = active
-        slope_ref[...] = (cdf + inner * bell * 0.3989422804014327).astype(bf16)
-        acc[...] += dot(active, wo_ref[...], 1, 0)
+        left = low[...]
+        total = acc[...]
+        for c in range(0, BLOCK, PART):
+            part = slice(c, c + PART)
+            inner = dot(left, wi_ref[:, part], 1, 0) + ib_ref[:, part]
+            cdf, bell = upper_tail(inner)
+            active = (inner * cdf).astype(bf16)
+            active_ref[:, part] = active
+            slope_ref[:, part] = (cdf + inner * bell * 0.3989422804014327).astype(bf16)
+            total = total + dot(active, wo_ref[part], 1, 0)
+        acc[...] = total
 
         @pl.when(j == pl.num_programs(0) - 1)
         def _():
@@ -242,19 +248,20 @@
         for g, w in ((dq_ref, wq_ref), (dk_ref, wk_ref), (dv_ref, wv_ref)):
             d = d + dot(g[...], w[...], 1, 1)
         row = lax.broadcasted_iota(jnp.int32, (rows_dev, 1), 0)
-        memory = jnp.zeros((EXTRA, width), f32)
+        memory = jnp.zeros((2 * EXTRA, width), f32)
         for k in range(nseq):
             part = d[k * rows_dev : (k + 1) * rows_dev]
             is_mem = jnp.logical_and(row < mem_rows, jnp.logical_and(seq_me == k, first != 0))
             pieces[k][...] = jnp.where(is_mem, 0.0, part).astype(bf16)
-            memory = memory + jnp.where(is_mem[:EXTRA], part[:EXTRA], 0.0)
+            memory = memory + jnp.where(is_mem[: 2 * EXTRA], part[: 2 * EXTRA], 0.0)
         small_ref[0, 0:1] = jnp.sum(dq_ref[...].astype(f32), axis=0, keepdims=True)
         small_ref[0, 1:2] = jnp.sum(dv_ref[...].astype(f32), axis=0, keepdims=True)
         small_ref[0, 2:5] = s1_ref[0:3]
         small_ref[0, 5:8] = s2_ref[0:3]
         for r in range(ib_rows):
             small_ref[1, r : r + 1] = ib_ref[0:1, r * width : (r + 1) * width]
-        small_ref[2] = memory
+        small_ref[2] = memory[:EXTRA]
+        small_ref[3] = memory[EXTRA:]
 
     vmem = pl.BlockSpec(memory_space=pltpu.VMEM)
     got = pl.pallas_call(
@@ -460,13 +467,14 @@
     )(me, n1t, slope, d_outer, wo)
 
 
-def finish_tokens(me, factor, pieces):
+def finish_rows(me, factor, pieces, kind):
     count = len(pieces)
 
     def kernel(me_ref, factor_ref, *refs):
         out_ref = refs[count]
         for k in range(count):
-            out_ref[me_ref[1] ^ k] = refs[k][...].astype(f32) * factor_ref[0]
+            piece = refs[k][...]
+            out_ref[me_ref[1] ^ k] = piece if piece.dtype == kind else piece.astype(f32) * factor_ref[0]
 
     smem = pl.BlockSpec(memory_space=pltpu.SMEM)
     vmem = pl.BlockSpec(memory_space=pltpu.VMEM)
@@ -474,8 +482,7 @@
         kernel,
         in_specs=[smem, smem] + [vmem] * count,
         out_specs=vmem,
-        out_shape=jax.ShapeDtypeStruct((count,) + pieces[0].shape, f32),
-        name="finish_tok",
+        out_shape=jax.ShapeDtypeStruct((count,) + pieces[0].shape, kind),
     )(me, factor, *pieces)
 
 
@@ -560,6 +567,7 @@
     plan = Plan(mesh)
     ndp, nseq = plan.ndp, plan.nseq
     devices = ("dp", "seq")
+    sent = {}
 
     def total_of(terms):
         total = terms[0].astype(f32)
@@ -570,9 +578,12 @@
     def start_chunk(keep, send):
         return [keep, lax.ppermute(send, devices, plan.perm(-1))]
 
-    def step_chunk(terms, step):
+    def step_chunk(name, terms, step, after=None):
         half = terms[0].shape[0] // 2
+        if after is not None:
+            *terms, _ = lax.optimization_barrier((*terms, after))
         send = total_of([t[half:] for t in terms]).astype(bf16)
+        sent[name] = send
         got = lax.ppermute(send, devices, plan.perm(step))
         return [t[:half] for t in terms] + [got]
 
@@ -617,11 +628,8 @@
         segs_total = ndp * seg_dev
 
         def to_segments(x):
-            pieces = []
-            for k in range(nseq):
-                piece = lax.dynamic_index_in_dim(x, seq_index ^ k, axis=0, keepdims=False)
-                pieces.append(swap_seq(piece, k) if k else piece)
-            return pieces
+            pieces = [lax.dynamic_index_in_dim(x, seq_index ^ k, axis=0, keepdims=False) for k in range(nseq)]
+            return [swap_seq(p, k) if k else p for k, p in enumerate(pieces)], pieces
 
         def to_rows(pieces, finish):
             out = None
@@ -635,7 +643,9 @@
         source = seq_index ^ jnp.arange(nseq, dtype=jnp.int32)
         position = source[:, None] * rows_dev + jnp.arange(rows_dev, dtype=jnp.int32)[None, :]
         is_mem = (position < mem_rows).reshape(rows)
-        raw = jnp.concatenate(to_segments(tokens), axis=0)
+        pieces, sliced = to_segments(tokens)
+        raw = jnp.concatenate(pieces, axis=0)
+        out_grad, lm_mask, *_ = lax.optimization_barrier((out_grad, lm_mask, *sliced))
 
         here = seq_index * rows_dev + jnp.arange(rows_dev, dtype=jnp.int32)
         valid = jnp.where((here < mem_rows)[None, :], 0, lm_mask)
@@ -643,7 +653,7 @@
         masked = jnp.where(valid[..., None] != 0, out_grad, jnp.zeros_like(out_grad))
         assert rows_dev <= 256
         count_rows = jnp.broadcast_to(counts_here.astype(bf16)[:, None, None], (seg_dev, EXTRA, width))
-        cot_pieces = to_segments(jnp.concatenate([masked, count_rows], axis=1))
+        cot_pieces, _ = to_segments(jnp.concatenate([masked, count_rows], axis=1))
 
         seg_global = dp_index * seg_dev + seq_index
         starts = jnp.cumsum(doc_segments) - doc_segments
@@ -674,7 +684,7 @@
             rows_dev,
         )
         out_pieces = [swap_seq(p, k) if k else p for k, p in enumerate(out_pieces)]
-        layer_out = to_rows(out_pieces, lambda p: p)
+        layer_out = finish_rows(me, jnp.ones((1,), f32), out_pieces, bf16)
 
         aligned = (width // ndp) % 16 == 0 and (ff // (ndp * nseq)) % 16 == 0 and ff // nseq == BLOCK
         if aligned:
@@ -695,15 +705,15 @@
             grad = grad.reshape(ndp, width // ndp, nseq, ff // nseq).transpose(0, 2, 1, 3)
             keep, send = place_pieces(plan, me, grad)
         inner = start_chunk(keep, send)
-        outer = step_chunk(outer, 0)
+        outer = step_chunk("o", outer, 0)
         d_resid1, d_attn, d_context, small1 = ffn_backward(
             d_inner, inner_weight, d_resid2, hat1, inv1, vecs[1:2], output_weight
         )
-        inner = step_chunk(inner, 0)
+        inner = step_chunk("i", inner, 0)
         d_queries, d_keys, d_values = attention_backward(
             queries, keys, values, context, d_context, probs, 1, rows
         )
-        outer = step_chunk(outer, 1)
+        outer = step_chunk("o", outer, 1)
         cut_pieces, small = inputs_backward(
             me,
             (d_queries, d_keys, d_values),
@@ -731,22 +741,29 @@
             keep, send = place_pieces(plan, me, jnp.concatenate([blocks, below], axis=2))
         attn = start_chunk(keep, send)
         for step in range(2, plan.steps):
-            outer = step_chunk(outer, step)
-        for step in range(1, plan.steps):
-            inner = step_chunk(inner, step)
-        for step in range(plan.steps):
-            attn = step_chunk(attn, step)
+            outer = step_chunk("o", outer, step)
+        inner = step_chunk("i", inner, 1)
+        attn = step_chunk("t", attn, 0)
+        inner = step_chunk("i", inner, 2, sent["t"])
+        attn = step_chunk("t", attn, 1)
+        for step in range(3, plan.steps):
+            inner = step_chunk("i", inner, step, sent["t"])
+        for step in range(2, plan.steps):
+            attn = step_chunk("t", attn, step)
+            if step == 2:
+                after_third = sent["t"]
         outer_rows = ff // (ndp * nseq)
         outer = total_of(outer)[0]
         total = jnp.sum(outer[outer_rows, :DIGITS] * (2.0 ** jnp.arange(DIGITS)).astype(f32))
         factor = total / segs_total
+        *inner, _ = lax.optimization_barrier((*inner, after_third))
         ffn_near, ffn_far = gather_seq(jnp.concatenate([outer[:outer_rows], total_of(inner)[0]], axis=0).astype(bf16))
         attn_near, attn_far = gather_seq(total_of(attn)[0].astype(bf16))
 
         part = width // ndp
         scale = factor.reshape(1)
         if aligned:
-            tokens_grad = finish_tokens(me, scale, cut_pieces)
+            tokens_grad = finish_rows(me, scale, cut_pieces, f32)
             g_outer, g_inner = finish_weights(me, scale, ffn_near, ffn_far, [(0, outer_rows, 0), (outer_rows, part, 1)])
             got = finish_weights(me, scale, attn_near, attn_far, [(0, part, None), (part, EXTRA, None)])
             g_query, g_key, g_value, g_output = got[:4]
@@ -767,7 +784,7 @@
             small_parts = [p[part:] for p in attn_parts]
         mine = lambda x: lax.dynamic_slice_in_dim(x, dp_index * part, part, axis=1)
         vec_rows = mine(small_parts[0][:8])
-        g_memory = mine(small_parts[2][:mem_rows]).T
+        g_memory = mine(jnp.concatenate([small_parts[2], small_parts[3]])[:mem_rows]).T
         inner_part = ff // ndp
         g_inner_bias = lax.dynamic_slice_in_dim(
             small_parts[1][:ib_rows].reshape(-1), dp_index * inner_part, inner_part, axis=0

time: 264 us -> 257 us (0.973)
  other arithmetic: 30.8 us -> 12.5 us
  waiting for transfers between devices: 64.8 us -> 72.5 us
    ppermute x12, waiting for transfers between devices: 46 us -> 61.2 us  [step_chunk(): got = lax.ppermute(send, devices, plan.perm(step))]
    convert_element_type x12, other arithmetic: 19.1 us -> 5.35 us  [step_chunk(): send = total_of([t[half:] for t in terms]).astype(bf16)]
    ppermute x12, starting transfers between devices: 14.9 us -> 24.5 us  [step_chunk(): got = lax.ppermute(send, devices, plan.perm(step))]
    ppermute x16, starting transfers between devices: 31.4 us -> 23.8 us  [swap_seq(): return lax.ppermute(x, 'seq', [(i, i ^ k) for i in range(nseq)])]
    ppermute x16, waiting for transfers between devices: 18.8 us -> 11.2 us  [swap_seq(): return lax.ppermute(x, 'seq', [(i, i ^ k) for i in range(nseq)])]
  transfers between devices with their start and end apart: 31 -> 31, of which waited for: 13 -> 12; matrix products, arithmetic and copies ran while one was open for 15% -> 9% of each run, Pallas kernels for 26% -> 22%
where the time goes in v3:
time: 257 us; the launch traced here: 256 us
  Pallas kernels  103 us (40%)
  waiting for transfers between devices  72.5 us (28%)
  starting transfers between devices  48.8 us (19%)
  other arithmetic  12.5 us (5%)
  local copies, waits for them, and re-layouts  11.1 us (4%)
  matrix products  5.01 us (2%)
  between operations  2.77 us (1%)
    ppermute x12, waiting for transfers between devices, step_chunk(): got = lax.ppermute(send, devices, plan.perm(step))  61.2 us
    ppermute x12, starting transfers between devices, step_chunk(): got = lax.ppermute(send, devices, plan.perm(step))  24.5 us
    ppermute x16, starting transfers between devices, swap_seq(): return lax.ppermute(x, 'seq', [(i, i ^ k) for i in range(nseq)])  23.8 us
    pallas_call x1, Pallas kernels, ffn_forward(): pl.pallas_call(kernel, grid=(inner // BLOCK,), in_specs=[full(flat), full...  22.3 us
    pallas_call x1, Pallas kernels, attention_backward(): pl.pallas_call(attn_bwd_kernel, grid=(segs, pairs), in_specs=[spec] * 5 +...  12.4 us
    pallas_call x1, Pallas kernels, ffn_inner_grad(): pl.pallas_call(kernel, grid_spec=pltpu.PrefetchScalarGridSpec(num_scalar_...  12.2 us
    pallas_call x1, Pallas kernels, attention_forward(): pl.pallas_call(attn_fwd_kernel, grid=(segs, pairs), in_specs=[spec, spec,...  11.4 us
    ppermute x16, waiting for transfers between devices, swap_seq(): return lax.ppermute(x, 'seq', [(i, i ^ k) for i in range(nseq)])  11.2 us
  transfers between devices with their start and end apart: 31, of which 12 were waited for; matrix products, arithmetic and copies ran while one was open for 9% of the time, Pallas kernels for 22%

profile of v3, /device:TPU:0, one launch (start us, length us, event | category | flops | bytes accessed | tf_op | source)
XLA Modules:
  0.0 255.8 jit_solution(4479746156510877084)
XLA Ops:
  2.6 2.6 %collective-permute-start.2 = (bf16[128,768]{1,0:T(8,128)(2,1)S(1)}, bf16[128,768]{1,0:T(8,128)(2,1)S(1)}, u32[]{:S(2)}, u32[]{:S(2)}) collective-permute-start(bf16[128,768]{1,0:T(8,128)(2,1)S(1)} %get-tuple-element.152), channel_id=1, source_target_pairs={{0,3},{1,2},{2,1},{3,0},{4,7},{5,6},{6,5},{7,4},{8,11},{9,10},{10,... | collective-permute-start | bytes 589832 | tf_op jit(solution)/shard_map/ppermute | solution.py:591
  20.5 11.4 %attn_fwd.1 = (bf16[512,768]{1,0:T(8,128)(2,1)}, bf16[12,512,512]{2,1,0:T(8,128)(2,1)}) custom-call(bf16[512,768]{1,0:T(8,128)(2,1)} %add_convert_fusion.4.q_ref, bf16[512,768]{1,0:T(8,128)(2,1)} %convolution_convert_fusion.k_ref, bf16[512,768]{1,0:T(8,128)(2,1)} %add_convert_fusion.3.v_ref), custom_call_target="tpu_custom_call" | custom-call | tf_op jit(solution)/shard_map/attn_fwd/pallas_call | solution.py:81
  32.7 22.3 %ffn_fwd.1 = (f32[512,768]{1,0:T(8,128)}, f32[512,128]{1,0:T(8,128)}, bf16[768,512]{1,0:T(8,128)(2,1)}, bf16[512,3072]{1,0:T(8,128)(2,1)}, bf16[512,3072]{1,0:T(...) custom-call(bf16[512,768]{1,0:T(8,128)(2,1)} %copy-done, ...), custom_call_target="tpu_custom_call" | custom-call | tf_op jit(solution)/shard_map/ffn_fwd/pallas_call | solution.py:217
  55.0 8.7 %outer_grad.1 = (bf16[16,104,768]{2,1,0:T(8,128)(2,1)}, bf16[16,104,768]{2,1,0:T(8,128)(2,1)}) custom-call(s32[3]{0:T(128)} %pad_add_fusion.me_ref, bf16[512,3072]{1,0:T(8,128)(2,1)} %get-tuple-element.90.active_ref, bf16[512,768]{1,0:T(8,128)(2,1)} %get-tuple-element.98.d_ref.douter_ref, f32[8,768]{1,0:T(8,128)} %get-tuple-element.91.small_ref.s2_ref), custom_call_target="tpu_custom_call" | custom-call | tf_op jit(solution)/shard_map/outer_grad/pallas_call | solution.py:356
  63.6 12.2 %inner_grad.1 = (bf16[16,96,768]{2,1,0:T(8,128)(2,1)}, bf16[16,96,768]{2,1,0:T(8,128)(2,1)}, bf16[512,3072]{1,0:T(8,128)(2,1)}, f32[8,3072]{1,0:T(8,128)}) custom-call(s32[3]{0:T(128)} %pad_add_fusion.me_ref, bf16[768,512]{1,0:T(8,128)(2,1)} %get-tuple-element.96.n1t_ref, bf16[512,3072]{1,0:T(8,128)(2,1)} %get-tuple-element.97.slope_ref, ...), custom_call_target="tpu_custom_call" | custom-call | tf_op jit(solution)/shard_map/inner_grad/pallas_call | solution.py:447
  76.9 10.7 %ffn_bwd.1 = (f32[512,768]{1,0:T(8,128)}, bf16[512,768]{1,0:T(8,128)(2,1)}, bf16[512,768]{1,0:T(8,128)(2,1)}, f32[8,768]{1,0:T(8,128)}) custom-call(bf16[512,3072]{1,0:T(8,128)(2,1)} %get-tuple-element.99.dinner_ref, bf16[768,3072]{1,0:T(8,128)(2,1)} %wi_ref.3, f32[512,768]{1,0:T(8,128)} %get-tuple-element.100.dres2_ref, ...), custom_call_target="tpu_custom_call" | custom-call | tf_op jit(solution)/shard_map/ffn_bwd/pallas_call | solution.py:405
  87.6 12.4 %attn_bwd.1 = (bf16[512,768]{1,0:T(8,128)(2,1)}, bf16[512,768]{1,0:T(8,128)(2,1)}, bf16[512,768]{1,0:T(8,128)(2,1)}) custom-call(bf16[512,768]{1,0:T(8,128)(2,1)} %add_convert_fusion.4.q_ref, bf16[512,768]{1,0:T(8,128)(2,1)} %convolution_convert_fusion.k_ref, bf16[512,768]{1,0:T(8,128)(2,1)} %add_convert_fusion.3.v_ref, ...), custom_call_target="tpu_custom_call" | custom-call | tf_op jit(solution)/shard_map/attn_bwd/pallas_call | solution.py:100
  100.0 6.3 %inputs_bwd.1 = (bf16[128,768]{1,0:T(8,128)(2,1)}, bf16[128,768]{1,0:T(8,128)(2,1)}, bf16[128,768]{1,0:T(8,128)(2,1)}, bf16[128,768]{1,0:T(8,128)(2,1)}, f32[4,8,768]{2,1,0:T(8,128)}) custom-call(s32[3]{0:T(128)} %pad_add_fusion.me_ref, bf16[512,768]{1,0:T(8,128)(2,1)} %get-tuple-element.105.dq_ref.d0_ref, ...), custom_call_target="tpu_custom_call" | custom-call | tf_op jit(solution)/shard_map/inputs_bwd/pallas_call | solution.py:267
  106.2 9.7 %attn_grad.1 = (bf16[16,104,768]{2,1,0:T(8,128)(2,1)}, bf16[16,104,768]{2,1,0:T(8,128)(2,1)}) custom-call(s32[3]{0:T(128)} %pad_add_fusion.me_ref, bf16[512,768]{1,0:T(8,128)(2,1)} %copy-done, bf16[512,768]{1,0:T(8,128)(2,1)} %get-tuple-element.82.ctx_ref, bf16[512,768]{1,0:T(8,128)(2,1)} %get-tuple-element.105.dq_ref.d0_ref, ...), custom_call_target="tpu_custom_call" | custom-call | tf_op jit(solution)/shard_map/attn_grad/pallas_call | solution.py:544
  123.5 10.9 %collective-permute-done.25 = bf16[8,96,768]{2,1,0:T(8,128)(2,1)S(1)} collective-permute-done((bf16[8,96,768]{2,1,0:T(8,128)(2,1)S(1)}, bf16[8,96,768]{2,1,0:T(8,128)(2,1)S(1)}, u32[]{:S(2)}, u32[]{:S(2)}) %collective-permute-start.25) | collective-permute-done | bytes 1179680 | tf_op jit(solution)/shard_map/ppermute | solution.py:587
  138.9 9.1 %collective-permute-done.10 = bf16[8,104,768]{2,1,0:T(8,128)(2,1)S(1)} collective-permute-done((bf16[8,104,768]{2,1,0:T(8,128)(2,1)S(1)}, bf16[8,104,768]{2,1,0:T(8,128)(2,1)S(1)}, u32[]{:S(2)}, u32[]{:S(2)}) %collective-permute-start.10) | collective-permute-done | bytes 1277984 | tf_op jit(solution)/shard_map/ppermute | solution.py:587
  154.2 7.5 %collective-permute-done.18 = bf16[8,104,768]{2,1,0:T(8,128)(2,1)S(1)} collective-permute-done((bf16[8,104,768]{2,1,0:T(8,128)(2,1)S(1)}, bf16[8,104,768]{2,1,0:T(8,128)(2,1)S(1)}, u32[]{:S(2)}, u32[]{:S(2)}) %collective-permute-start.18) | collective-permute-done | bytes 1277984 | tf_op jit(solution)/shard_map/ppermute | solution.py:587
  165.0 2.6 %collective-permute-start.28 = (bf16[1,96,768]{2,1,0:T(8,128)(2,1)S(1)}, bf16[1,96,768]{2,1,0:T(8,128)(2,1)S(1)}, u32[]{:S(2)}, u32[]{:S(2)}) collective-permute-start(bf16[1,96,768]{2,1,0:T(8,128)(2,1)S(1)} %add_convert_fusion.15), channel_id=1, source_target_pairs={{0,16},{1,3},{2,18},{3,1},{4,20},{5,7},{6,22},{7,5},{8,24},{9,11},... | collective-permute-start | bytes 442376 | tf_op jit(solution)/shard_map/ppermute | solution.py:587
  169.5 9.9 %collective-permute-done.19 = bf16[4,104,768]{2,1,0:T(8,128)(2,1)S(1)} collective-permute-done((bf16[4,104,768]{2,1,0:T(8,128)(2,1)S(1)}, bf16[4,104,768]{2,1,0:T(8,128)(2,1)S(1)}, u32[]{:S(2)}, u32[]{:S(2)}) %collective-permute-start.19) | collective-permute-done | bytes 639008 | tf_op jit(solution)/shard_map/ppermute | solution.py:587
  181.9 2.7 %collective-permute-start.13 = (bf16[1,104,768]{2,1,0:T(8,128)(2,1)S(1)}, bf16[1,104,768]{2,1,0:T(8,128)(2,1)S(1)}, u32[]{:S(2)}, u32[]{:S(2)}) collective-permute-start(bf16[1,104,768]{2,1,0:T(8,128)(2,1)S(1)} %add_convert_fusion.13), channel_id=1, source_target_pairs={{0,16},{1,3},{2,18},{3,1},{4,20},{5,7},{6,22},{7,5},{8,24},{9,11},... | collective-permute-start | bytes 479240 | tf_op jit(solution)/shard_map/ppermute | solution.py:587
  184.6 9.4 %collective-permute-done.20 = bf16[2,104,768]{2,1,0:T(8,128)(2,1)S(1)} collective-permute-done((bf16[2,104,768]{2,1,0:T(8,128)(2,1)S(1)}, bf16[2,104,768]{2,1,0:T(8,128)(2,1)S(1)}, u32[]{:S(2)}, u32[]{:S(2)}) %collective-permute-start.20) | collective-permute-done | bytes 319520 | tf_op jit(solution)/shard_map/ppermute | solution.py:587
  194.1 2.5 collective-permute-start.21
  196.8 12.8 %collective-permute-done.21 = bf16[1,104,768]{2,1,0:T(8,128)(2,1)S(1)} collective-permute-done((bf16[1,104,768]{2,1,0:T(8,128)(2,1)S(1)}, bf16[1,104,768]{2,1,0:T(8,128)(2,1)S(1)}, u32[]{:S(2)}, u32[]{:S(2)}) %collective-permute-start.21) | collective-permute-done | bytes 159776 | tf_op jit(solution)/shard_map/ppermute | solution.py:587
  211.9 7.4 %collective-permute-start.6 = (bf16[128,768]{1,0:T(8,128)(2,1)S(1)}, bf16[128,768]{1,0:T(8,128)(2,1)S(1)}, u32[]{:S(2)}, u32[]{:S(2)}) collective-permute-start(bf16[128,768]{1,0:T(8,128)(2,1)S(1)} %copy-done.39), channel_id=1, source_target_pairs={{0,1},{1,0},{2,3},{3,2},{4,5},{5,4},{6,7},{7,6},{8,9},{9,8},{10,11... | collective-permute-start | bytes 589832 | tf_op jit(solution)/shard_map/ppermute | solution.py:591
  222.1 5.0 %collective-permute-done.7.refs_2_ = bf16[128,768]{1,0:T(8,128)(2,1)S(1)} collective-permute-done((bf16[128,768]{1,0:T(8,128)(2,1)S(1)}, bf16[128,768]{1,0:T(8,128)(2,1)S(1)}, u32[]{:S(2)}, u32[]{:S(2)}) %collective-permute-start.7) | collective-permute-done | bytes 196640 | tf_op jit(solution)/shard_map/ppermute | solution.py:591
  228.6 4.6 %collective-permute-start.16 = (bf16[128,768]{1,0:T(8,128)(2,1)}, bf16[128,768]{1,0:T(8,128)(2,1)S(1)}, u32[]{:S(2)}, u32[]{:S(2)}) collective-permute-start(bf16[128,768]{1,0:T(8,128)(2,1)} %get-tuple-element.114), channel_id=1, source_target_pairs={{0,3},{1,2},{2,1},{3,0},{4,7},{5,6},{6,5},{7,4},{8,11},{9,10},{10,... | collective-permute-start | bytes 589832 | tf_op jit(solution)/shard_map/ppermute | solution.py:591
  233.2 2.6 %collective-permute-done.8.refs_3_ = bf16[128,768]{1,0:T(8,128)(2,1)} collective-permute-done((bf16[128,768]{1,0:T(8,128)(2,1)S(1)}, bf16[128,768]{1,0:T(8,128)(2,1)}, u32[]{:S(2)}, u32[]{:S(2)}) %collective-permute-start.8) | collective-permute-done | bytes 196640 | tf_op jit(solution)/shard_map/ppermute | solution.py:591
  239.3 2.7 %collective-permute-done.16.refs_3_ = bf16[128,768]{1,0:T(8,128)(2,1)S(1)} collective-permute-done((bf16[128,768]{1,0:T(8,128)(2,1)}, bf16[128,768]{1,0:T(8,128)(2,1)S(1)}, u32[]{:S(2)}, u32[]{:S(2)}) %collective-permute-start.16) | collective-permute-done | bytes 196640 | tf_op jit(solution)/shard_map/ppermute | solution.py:591
  253.0 2.8 %shard_map.334 = (f32[384,768]{1,0:T(8,128)}, f32[96,3072]{1,0:T(8,128)}) custom-call(s32[3]{0:T(128)} %pad_add_fusion.me_ref, f32[1]{0:T(128)} %bitcast.18.factor_ref, bf16[2,192,768]{2,1,0:T(8,128)(2,1)} %copy-done.4, bf16[2,192,768]{2,1,0:T(8,128)(2,1)} %copy-done.14), custom_call_target="tpu_custom_call" | custom-call | tf_op jit(solution)/shard_map/pallas_call | solution.py:520
  (206 shorter events, 64.3 us)
Async XLA Ops:
  6.5 25.4 %collective-permute-start.5 = (bf16[136,768]{1,0:T(8,128)(2,1)S(1)}, bf16[136,768]{1,0:T(8,128)(2,1)S(1)}, u32[]{:S(2)}, u32[]{:S(2)}) collective-permute-start(bf16[136,768]{1,0:T(8,128)(2,1)S(1)} %get-tuple-element.146), channel_id=1, source_target_pairs={{0,3},{1,2},{2,1},{3,0},{4,7},{5,6},{6,5},{7,4},{8,11},{9,10},{10,... | collective-permute-start | bytes 626696 | tf_op jit(solution)/shard_map/ppermute | solution.py:591
  7.9 24.0 %collective-permute-start.3 = (bf16[136,768]{1,0:T(8,128)(2,1)S(1)}, bf16[136,768]{1,0:T(8,128)(2,1)S(1)}, u32[]{:S(2)}, u32[]{:S(2)}) collective-permute-start(bf16[136,768]{1,0:T(8,128)(2,1)S(1)} %get-tuple-element.148), channel_id=1, source_target_pairs={{0,1},{1,0},{2,3},{3,2},{4,5},{5,4},{6,7},{7,6},{8,9},{9,8},{10,11... | collective-permute-start | bytes 626696 | tf_op jit(solution)/shard_map/ppermute | solution.py:591
  14.1 17.8 %collective-permute-start.4 = (bf16[136,768]{1,0:T(8,128)(2,1)S(1)}, bf16[136,768]{1,0:T(8,128)(2,1)S(1)}, u32[]{:S(2)}, u32[]{:S(2)}) collective-permute-start(bf16[136,768]{1,0:T(8,128)(2,1)S(1)} %get-tuple-element.149), channel_id=1, source_target_pairs={{0,2},{1,3},{2,0},{3,1},{4,6},{5,7},{6,4},{7,5},{8,10},{9,11},{10,... | collective-permute-start | bytes 626696 | tf_op jit(solution)/shard_map/ppermute | solution.py:591
  75.8 40.2 %collective-permute-start.24 = (bf16[16,96,768]{2,1,0:T(8,128)(2,1)}, bf16[16,96,768]{2,1,0:T(8,128)(2,1)}, u32[]{:S(2)}, u32[]{:S(2)}) collective-permute-start(bf16[16,96,768]{2,1,0:T(8,128)(2,1)} %get-tuple-element.125), channel_id=1, source_target_pairs={{0,1},{1,0},{2,3},{3,2},{4,5},{5,4},{6,7},{7,6},{8,9},{9,8},{10,11... | collective-permute-start | bytes 7077896 | tf_op jit(solution)/shard_map/ppermute | solution.py:579
  75.8 44.4 %collective-permute-start.9 = (bf16[16,104,768]{2,1,0:T(8,128)(2,1)}, bf16[16,104,768]{2,1,0:T(8,128)(2,1)S(1)}, u32[]{:S(2)}, u32[]{:S(2)}) collective-permute-start(bf16[16,104,768]{2,1,0:T(8,128)(2,1)} %get-tuple-element.95), channel_id=1, source_target_pairs={{0,1},{1,0},{2,3},{3,2},{4,5},{5,4},{6,7},{7,6},{8,9},{9,8},{10,11... | collective-permute-start | bytes 7667720 | tf_op jit(solution)/shard_map/ppermute | solution.py:579
  118.1 16.3 %collective-permute-start.25 = (bf16[8,96,768]{2,1,0:T(8,128)(2,1)S(1)}, bf16[8,96,768]{2,1,0:T(8,128)(2,1)S(1)}, u32[]{:S(2)}, u32[]{:S(2)}) collective-permute-start(bf16[8,96,768]{2,1,0:T(8,128)(2,1)S(1)} %add_convert_fusion.2), channel_id=1, source_target_pairs={{0,2},{1,5},{2,0},{3,7},{4,6},{5,1},{6,4},{7,3},{8,10},{9,13},{10,... | collective-permute-start | bytes 3538952 | tf_op jit(solution)/shard_map/ppermute | solution.py:587
  120.6 27.5 %collective-permute-start.10 = (bf16[8,104,768]{2,1,0:T(8,128)(2,1)S(1)}, bf16[8,104,768]{2,1,0:T(8,128)(2,1)S(1)}, u32[]{:S(2)}, u32[]{:S(2)}) collective-permute-start(bf16[8,104,768]{2,1,0:T(8,128)(2,1)S(1)} %add_convert_fusion.1), channel_id=1, source_target_pairs={{0,2},{1,5},{2,0},{3,7},{4,6},{5,1},{6,4},{7,3},{8,10},{9,13},{10,... | collective-permute-start | bytes 3833864 | tf_op jit(solution)/shard_map/ppermute | solution.py:587
  121.4 40.4 %collective-permute-start.18 = (bf16[8,104,768]{2,1,0:T(8,128)(2,1)S(1)}, bf16[8,104,768]{2,1,0:T(8,128)(2,1)S(1)}, u32[]{:S(2)}, u32[]{:S(2)}) collective-permute-start(bf16[8,104,768]{2,1,0:T(8,128)(2,1)S(1)} %add_convert_fusion), channel_id=1, source_target_pairs={{0,2},{1,5},{2,0},{3,7},{4,6},{5,1},{6,4},{7,3},{8,10},{9,13},{10,... | collective-permute-start | bytes 3833864 | tf_op jit(solution)/shard_map/ppermute | solution.py:587
  135.7 16.3 %collective-permute-start.26 = (bf16[4,96,768]{2,1,0:T(8,128)(2,1)S(1)}, bf16[4,96,768]{2,1,0:T(8,128)(2,1)S(1)}, u32[]{:S(2)}, u32[]{:S(2)}) collective-permute-start(bf16[4,96,768]{2,1,0:T(8,128)(2,1)S(1)} %add_convert_fusion.7), channel_id=1, source_target_pairs={{0,4},{1,9},{2,6},{3,11},{4,0},{5,13},{6,2},{7,15},{8,12},{9,1},{1... | collective-permute-start | bytes 1769480 | tf_op jit(solution)/shard_map/ppermute | solution.py:587
  148.3 19.3 %collective-permute-start.11 = (bf16[4,104,768]{2,1,0:T(8,128)(2,1)S(1)}, bf16[4,104,768]{2,1,0:T(8,128)(2,1)S(1)}, u32[]{:S(2)}, u32[]{:S(2)}) collective-permute-start(bf16[4,104,768]{2,1,0:T(8,128)(2,1)S(1)} %add_convert_fusion.6), channel_id=1, source_target_pairs={{0,4},{1,9},{2,6},{3,11},{4,0},{5,13},{6,2},{7,15},{8,12},{9,1},{1... | collective-permute-start | bytes 1916936 | tf_op jit(solution)/shard_map/ppermute | solution.py:587
  152.1 12.1 %collective-permute-start.27 = (bf16[2,96,768]{2,1,0:T(8,128)(2,1)S(1)}, bf16[2,96,768]{2,1,0:T(8,128)(2,1)S(1)}, u32[]{:S(2)}, u32[]{:S(2)}) collective-permute-start(bf16[2,96,768]{2,1,0:T(8,128)(2,1)S(1)} %add_convert_fusion.10), channel_id=1, source_target_pairs={{0,8},{1,17},{2,10},{3,19},{4,12},{5,21},{6,14},{7,23},{8,0},{9,25... | collective-permute-start | bytes 884744 | tf_op jit(solution)/shard_map/ppermute | solution.py:587
  162.0 17.3 %collective-permute-start.19 = (bf16[4,104,768]{2,1,0:T(8,128)(2,1)S(1)}, bf16[4,104,768]{2,1,0:T(8,128)(2,1)S(1)}, u32[]{:S(2)}, u32[]{:S(2)}) collective-permute-start(bf16[4,104,768]{2,1,0:T(8,128)(2,1)S(1)} %add_convert_fusion.5), channel_id=1, source_target_pairs={{0,4},{1,9},{2,6},{3,11},{4,0},{5,13},{6,2},{7,15},{8,12},{9,1},{1... | collective-permute-start | bytes 1916936 | tf_op jit(solution)/shard_map/ppermute | solution.py:587
  165.0 16.7 %collective-permute-start.28 = (bf16[1,96,768]{2,1,0:T(8,128)(2,1)S(1)}, bf16[1,96,768]{2,1,0:T(8,128)(2,1)S(1)}, u32[]{:S(2)}, u32[]{:S(2)}) collective-permute-start(bf16[1,96,768]{2,1,0:T(8,128)(2,1)S(1)} %add_convert_fusion.15), channel_id=1, source_target_pairs={{0,16},{1,3},{2,18},{3,1},{4,20},{5,7},{6,22},{7,5},{8,24},{9,11},... | collective-permute-start | bytes 442376 | tf_op jit(solution)/shard_map/ppermute | solution.py:587
  167.8 14.0 %collective-permute-start.12 = (bf16[2,104,768]{2,1,0:T(8,128)(2,1)S(1)}, bf16[2,104,768]{2,1,0:T(8,128)(2,1)S(1)}, u32[]{:S(2)}, u32[]{:S(2)}) collective-permute-start(bf16[2,104,768]{2,1,0:T(8,128)(2,1)S(1)} %add_convert_fusion.9), channel_id=1, source_target_pairs={{0,8},{1,17},{2,10},{3,19},{4,12},{5,21},{6,14},{7,23},{8,0},{9,25... | collective-permute-start | bytes 958472 | tf_op jit(solution)/shard_map/ppermute | solution.py:587
  179.5 14.5 %collective-permute-start.20 = (bf16[2,104,768]{2,1,0:T(8,128)(2,1)S(1)}, bf16[2,104,768]{2,1,0:T(8,128)(2,1)S(1)}, u32[]{:S(2)}, u32[]{:S(2)}) collective-permute-start(bf16[2,104,768]{2,1,0:T(8,128)(2,1)S(1)} %add_convert_fusion.8), channel_id=1, source_target_pairs={{0,8},{1,17},{2,10},{3,19},{4,12},{5,21},{6,14},{7,23},{8,0},{9,25... | collective-permute-start | bytes 958472 | tf_op jit(solution)/shard_map/ppermute | solution.py:587
  181.9 14.7 %collective-permute-start.13 = (bf16[1,104,768]{2,1,0:T(8,128)(2,1)S(1)}, bf16[1,104,768]{2,1,0:T(8,128)(2,1)S(1)}, u32[]{:S(2)}, u32[]{:S(2)}) collective-permute-start(bf16[1,104,768]{2,1,0:T(8,128)(2,1)S(1)} %add_convert_fusion.13), channel_id=1, source_target_pairs={{0,16},{1,3},{2,18},{3,1},{4,20},{5,7},{6,22},{7,5},{8,24},{9,11},... | collective-permute-start | bytes 479240 | tf_op jit(solution)/shard_map/ppermute | solution.py:587
  194.1 15.4 %collective-permute-start.21 = (bf16[1,104,768]{2,1,0:T(8,128)(2,1)S(1)}, bf16[1,104,768]{2,1,0:T(8,128)(2,1)S(1)}, u32[]{:S(2)}, u32[]{:S(2)}) collective-permute-start(bf16[1,104,768]{2,1,0:T(8,128)(2,1)S(1)} %add_convert_fusion.12), channel_id=1, source_target_pairs={{0,16},{1,3},{2,18},{3,1},{4,20},{5,7},{6,22},{7,5},{8,24},{9,11},... | collective-permute-start | bytes 479240 | tf_op jit(solution)/shard_map/ppermute | solution.py:587
  211.3 17.3 %collective-permute-start.29 = (bf16[192,768]{1,0:T(8,128)(2,1)S(1)}, bf16[192,768]{1,0:T(8,128)(2,1)S(1)}, u32[]{:S(2)}, u32[]{:S(2)}) collective-permute-start(bf16[192,768]{1,0:T(8,128)(2,1)S(1)} %pad_maximum_fusion.2), channel_id=1, source_target_pairs={{0,2},{1,3},{2,0},{3,1},{4,6},{5,7},{6,4},{7,5},{8,10},{9,11},{10,... | collective-permute-start | bytes 884744 | tf_op jit(solution)/shard_map/ppermute | solution.py:591
  220.8 15.0 %collective-permute-start.8 = (bf16[128,768]{1,0:T(8,128)(2,1)S(1)}, bf16[128,768]{1,0:T(8,128)(2,1)}, u32[]{:S(2)}, u32[]{:S(2)}) collective-permute-start(bf16[128,768]{1,0:T(8,128)(2,1)S(1)} %copy-done.37), channel_id=1, source_target_pairs={{0,3},{1,2},{2,1},{3,0},{4,7},{5,6},{6,5},{7,4},{8,11},{9,10},{10,... | collective-permute-start | bytes 589832 | tf_op jit(solution)/shard_map/ppermute | solution.py:591
  220.9 24.3 %collective-permute-start.23 = (bf16[2,104,768]{2,1,0:T(8,128)(2,1)S(1)}, bf16[2,104,768]{2,1,0:T(8,128)(2,1)S(1)}, u32[]{:S(2)}, u32[]{:S(2)}) collective-permute-start(bf16[2,104,768]{2,1,0:T(8,128)(2,1)S(1)} %pad_maximum_fusion.1.near_ref), channel_id=1, source_target_pairs={{0,1},{1,0},{2,3},{3,2},{4,5},{5,4},{6,7},{7,6},{8,9},{9,8},{10,11... | collective-permute-start | bytes 958472 | tf_op jit(solution)/shard_map/ppermute | solution.py:591
  222.0 17.3 %collective-permute-start.14 = (bf16[128,768]{1,0:T(8,128)(2,1)}, bf16[128,768]{1,0:T(8,128)(2,1)S(1)}, u32[]{:S(2)}, u32[]{:S(2)}) collective-permute-start(bf16[128,768]{1,0:T(8,128)(2,1)} %get-tuple-element.112), channel_id=1, source_target_pairs={{0,1},{1,0},{2,3},{3,2},{4,5},{5,4},{6,7},{7,6},{8,9},{9,8},{10,11... | collective-permute-start | bytes 589832 | tf_op jit(solution)/shard_map/ppermute | solution.py:591
  227.0 12.2 %collective-permute-start.15 = (bf16[128,768]{1,0:T(8,128)(2,1)}, bf16[128,768]{1,0:T(8,128)(2,1)S(1)}, u32[]{:S(2)}, u32[]{:S(2)}) collective-permute-start(bf16[128,768]{1,0:T(8,128)(2,1)} %get-tuple-element.113), channel_id=1, source_target_pairs={{0,2},{1,3},{2,0},{3,1},{4,6},{5,7},{6,4},{7,5},{8,10},{9,11},{10,... | collective-permute-start | bytes 589832 | tf_op jit(solution)/shard_map/ppermute | solution.py:591
  228.6 13.5 %collective-permute-start.16 = (bf16[128,768]{1,0:T(8,128)(2,1)}, bf16[128,768]{1,0:T(8,128)(2,1)S(1)}, u32[]{:S(2)}, u32[]{:S(2)}) collective-permute-start(bf16[128,768]{1,0:T(8,128)(2,1)} %get-tuple-element.114), channel_id=1, source_target_pairs={{0,3},{1,2},{2,1},{3,0},{4,7},{5,6},{6,5},{7,4},{8,11},{9,10},{10,... | collective-permute-start | bytes 589832 | tf_op jit(solution)/shard_map/ppermute | solution.py:591
  235.8 16.4 %collective-permute-start.30 = (bf16[2,192,768]{2,1,0:T(8,128)(2,1)S(1)}, bf16[2,192,768]{2,1,0:T(8,128)(2,1)S(1)}, u32[]{:S(2)}, u32[]{:S(2)}) collective-permute-start(bf16[2,192,768]{2,1,0:T(8,128)(2,1)S(1)} %pad_maximum_fusion.near_ref), channel_id=1, source_target_pairs={{0,1},{1,0},{2,3},{3,2},{4,5},{5,4},{6,7},{7,6},{8,9},{9,8},{10,11... | collective-permute-start | bytes 1769480 | tf_op jit(solution)/shard_map/ppermute | solution.py:591
  (52 other events, 377.2 us)

commit v4 on v3

--- a/solution.py
+++ b/solution.py
@@ -10,7 +10,7 @@
 EPS = 1e-06
 LOG2E = 1.4426950408889634
 BLOCK = 768
-PART = 256
+PART = 768
 DIGITS = 16
 EXTRA = 8
 f32 = jnp.float32
@@ -370,16 +370,23 @@
     )(me, active, d_outer, small2)
 
 
-def ffn_backward(d_inner, wi, d_resid2, hat1, inv1, gain1, wout):
-    n, inner = d_inner.shape
-    width = d_resid2.shape[1]
+def ffn_backward(plan, me, slope, d_outer, wo, wi, n1t, d_resid2, hat1, inv1, gain1, wout):
+    n, inner = slope.shape
+    width = d_outer.shape[1]
+    rows = width // plan.ndp
+    cols = inner // plan.nseq
 
     def kernel(
-        dinner_ref, wi_ref, dres2_ref, hat1_ref, inv1_ref, gain_ref, wout_ref,
-        dres1_ref, dattn_ref, dctx_ref, small_ref, acc,
+        me_ref, slope_ref, douter_ref, wo_ref, wi_ref, n1t_ref, dres2_ref, hat1_ref, inv1_ref, gain_ref, wout_ref,
+        keep_ref, send_ref, dres1_ref, dattn_ref, dctx_ref, ib_ref, small_ref, acc,
     ):
         j = pl.program_id(0)
-        back = dot(dinner_ref[...], wi_ref[...], 1, 1)
+        d_active = dot(douter_ref[...], wo_ref[...], 1, 1)
+        d_inner = (d_active * slope_ref[...].astype(f32)).astype(bf16)
+        ib_ref[...] = jnp.broadcast_to(jnp.sum(d_inner.astype(f32), axis=0, keepdims=True), ib_ref.shape)
+        result = dot(n1t_ref[...], d_inner, 1, 0)
+        scatter_pieces(plan, me_ref, result, [(i, j) for i in range(plan.ndp)], keep_ref, send_ref, rows)
+        back = dot(d_inner, wi_ref[...], 1, 1)
 
         @pl.when(j == 0)
         def _():
@@ -400,71 +407,48 @@
             dctx_ref[...] = dot(low, wout_ref[...], 1, 1).astype(bf16)
             small_ref[...] = rows_of(d_normed * hat, d_normed, low.astype(f32))
 
-    full = lambda a: pl.BlockSpec(a.shape, lambda j: (0,) * a.ndim)
-    whole = lambda shape: pl.BlockSpec(shape, lambda j: (0,) * len(shape))
-    return pl.pallas_call(
-        kernel,
-        grid=(inner // BLOCK,),
-        in_specs=[
-            pl.BlockSpec((n, BLOCK), lambda j: (0, j)),
-            pl.BlockSpec((width, BLOCK), lambda j: (0, j)),
-            full(d_resid2),
-            full(hat1),
-            full(inv1),
-            full(gain1),
-            full(wout),
-        ],
-        out_specs=[whole((n, width)), whole((n, width)), whole((n, width)), whole((8, width))],
-        scratch_shapes=[pltpu.VMEM((n, width), f32)],
-        out_shape=[
-            jax.ShapeDtypeStruct((n, width), f32),
-            jax.ShapeDtypeStruct((n, width), bf16),
-            jax.ShapeDtypeStruct((n, width), bf16),
-            jax.ShapeDtypeStruct((8, width), f32),
-        ],
-        name="ffn_bwd",
-    )(d_inner, wi, d_resid2, hat1, inv1, gain1, wout)
-
-
-def ffn_inner_grad(plan, me, n1t, slope, d_outer, wo):
-    width, n = n1t.shape
-    inner = slope.shape[1]
-    rows = width // plan.ndp
-    cols = inner // plan.nseq
-
-    def kernel(me_ref, n1t_ref, slope_ref, douter_ref, wo_ref, keep_ref, send_ref, dinner_ref, ib_ref):
-        j = pl.program_id(0)
-        d_active = dot(douter_ref[...], wo_ref[...], 1, 1)
-        d_inner = (d_active * slope_ref[...].astype(f32)).astype(bf16)
-        dinner_ref[...] = d_inner
-        ib_ref[...] = jnp.broadcast_to(jnp.sum(d_inner.astype(f32), axis=0, keepdims=True), ib_ref.shape)
-        result = dot(n1t_ref[...], d_inner, 1, 0)
-        scatter_pieces(plan, me_ref, result, [(i, j) for i in range(plan.ndp)], keep_ref, send_ref, rows)
-
-    shape = jax.ShapeDtypeStruct((plan.places, rows, cols), bf16)
-    spec = pl.BlockSpec(shape.shape, lambda j, m: (0, 0, 0))
-    block = pl.BlockSpec((n, cols), lambda j, m: (0, j))
+    full = lambda a: pl.BlockSpec(a.shape, lambda j, m: (0,) * a.ndim)
+    whole = lambda shape: pl.BlockSpec(shape, lambda j, m: (0,) * len(shape))
+    chunk = jax.ShapeDtypeStruct((plan.places, rows, cols), bf16)
     return pl.pallas_call(
         kernel,
         grid_spec=pltpu.PrefetchScalarGridSpec(
             num_scalar_prefetch=1,
             grid=(plan.nseq,),
             in_specs=[
-                pl.BlockSpec((width, n), lambda j, m: (0, 0)),
-                block,
-                pl.BlockSpec(d_outer.shape, lambda j, m: (0, 0)),
+                pl.BlockSpec((n, cols), lambda j, m: (0, j)),
+                full(d_outer),
                 pl.BlockSpec((cols, width), lambda j, m: (j, 0)),
+                pl.BlockSpec((width, cols), lambda j, m: (0, j)),
+                full(n1t),
+                full(d_resid2),
+                full(hat1),
+                full(inv1),
+                full(gain1),
+                full(wout),
             ],
-            out_specs=[spec, spec, block, pl.BlockSpec((8, cols), lambda j, m: (0, j))],
+            out_specs=[
+                whole(chunk.shape),
+                whole(chunk.shape),
+                whole((n, width)),
+                whole((n, width)),
+                whole((n, width)),
+                pl.BlockSpec((8, cols), lambda j, m: (0, j)),
+                whole((8, width)),
+            ],
+            scratch_shapes=[pltpu.VMEM((n, width), f32)],
         ),
         out_shape=[
-            shape,
-            shape,
-            jax.ShapeDtypeStruct((n, inner), bf16),
+            chunk,
+            chunk,
+            jax.ShapeDtypeStruct((n, width), f32),
+            jax.ShapeDtypeStruct((n, width), bf16),
+            jax.ShapeDtypeStruct((n, width), bf16),
             jax.ShapeDtypeStruct((8, inner), f32),
+            jax.ShapeDtypeStruct((8, width), f32),
         ],
-        name="inner_grad",
-    )(me, n1t, slope, d_outer, wo)
+        name="ffn_bwd",
+    )(me, slope, d_outer, wo, wi, n1t, d_resid2, hat1, inv1, gain1, wout)
 
 
 def finish_rows(me, factor, pieces, kind):
@@ -567,7 +551,6 @@
     plan = Plan(mesh)
     ndp, nseq = plan.ndp, plan.nseq
     devices = ("dp", "seq")
-    sent = {}
 
     def total_of(terms):
         total = terms[0].astype(f32)
@@ -578,12 +561,9 @@
     def start_chunk(keep, send):
         return [keep, lax.ppermute(send, devices, plan.perm(-1))]
 
-    def step_chunk(name, terms, step, after=None):
+    def step_chunk(terms, step):
         half = terms[0].shape[0] // 2
-        if after is not None:
-            *terms, _ = lax.optimization_barrier((*terms, after))
         send = total_of([t[half:] for t in terms]).astype(bf16)
-        sent[name] = send
         got = lax.ppermute(send, devices, plan.perm(step))
         return [t[:half] for t in terms] + [got]
 
@@ -697,23 +677,27 @@
         d_outer, keep, send = lax.optimization_barrier((d_outer, keep, send))
         outer = start_chunk(keep, send)
         if aligned:
-            keep, send, d_inner, d_inner_bias = ffn_inner_grad(plan, me, n1t, slope, d_outer, outer_weight)
+            keep, send, d_resid1, d_attn, d_context, d_inner_bias, small1 = ffn_backward(
+                plan, me, slope, d_outer, outer_weight, inner_weight, n1t, d_resid2, hat1, inv1, vecs[1:2], output_weight
+            )
         else:
             d_inner = (dot(d_outer, outer_weight, 1, 1) * slope.astype(f32)).astype(bf16)
             d_inner_bias = jnp.broadcast_to(jnp.sum(d_inner.astype(f32), axis=0), (8, ff))
             grad = dot(n1t, d_inner, 1, 0).astype(bf16)
             grad = grad.reshape(ndp, width // ndp, nseq, ff // nseq).transpose(0, 2, 1, 3)
             keep, send = place_pieces(plan, me, grad)
+            d_normed = dot(d_inner, inner_weight, 1, 1) + d_resid2
+            d_resid1 = normalize_back(hat1, inv1[:, 0:1], d_normed * vecs[1:2])
+            d_attn = d_resid1.astype(bf16)
+            d_context = dot(d_attn, output_weight, 1, 1).astype(bf16)
+            small1 = rows_of(d_normed * hat1, d_normed, d_attn.astype(f32))
         inner = start_chunk(keep, send)
-        outer = step_chunk("o", outer, 0)
-        d_resid1, d_attn, d_context, small1 = ffn_backward(
-            d_inner, inner_weight, d_resid2, hat1, inv1, vecs[1:2], output_weight
-        )
-        inner = step_chunk("i", inner, 0)
+        outer = step_chunk(outer, 0)
         d_queries, d_keys, d_values = attention_backward(
             queries, keys, values, context, d_context, probs, 1, rows
         )
-        outer = step_chunk("o", outer, 1)
+        outer = step_chunk(outer, 1)
+        inner = step_chunk(inner, 0)
         cut_pieces, small = inputs_backward(
             me,
             (d_queries, d_keys, d_values),
@@ -741,22 +725,15 @@
             keep, send = place_pieces(plan, me, jnp.concatenate([blocks, below], axis=2))
         attn = start_chunk(keep, send)
         for step in range(2, plan.steps):
-            outer = step_chunk("o", outer, step)
-        inner = step_chunk("i", inner, 1)
-        attn = step_chunk("t", attn, 0)
-        inner = step_chunk("i", inner, 2, sent["t"])
-        attn = step_chunk("t", attn, 1)
-        for step in range(3, plan.steps):
-            inner = step_chunk("i", inner, step, sent["t"])
-        for step in range(2, plan.steps):
-            attn = step_chunk("t", attn, step)
-            if step == 2:
-                after_third = sent["t"]
+            outer = step_chunk(outer, step)
+        for step in range(1, plan.steps):
+            inner = step_chunk(inner, step)
+        for step in range(plan.steps):
+            attn = step_chunk(attn, step)
         outer_rows = ff // (ndp * nseq)
         outer = total_of(outer)[0]
         total = jnp.sum(outer[outer_rows, :DIGITS] * (2.0 ** jnp.arange(DIGITS)).astype(f32))
         factor = total / segs_total
-        *inner, _ = lax.optimization_barrier((*inner, after_third))
         ffn_near, ffn_far = gather_seq(jnp.concatenate([outer[:outer_rows], total_of(inner)[0]], axis=0).astype(bf16))
         attn_near, attn_far = gather_seq(total_of(attn)[0].astype(bf16))
 

time: 257 us -> 253 us (0.984)
  starting transfers between devices: 48.8 us -> 44 us
  other arithmetic: 12.5 us -> 16.1 us
    ppermute x12, starting transfers between devices: 24.5 us -> 21.3 us  [step_chunk(): got = lax.ppermute(send, devices, plan.perm(step))]
    ppermute x3, waiting for transfers between devices: 0.09 us -> 3.03 us  [start_chunk(): return [keep, lax.ppermute(send, devices, plan.perm(-1))]]
    ppermute x12, waiting for transfers between devices: 61.2 us -> 58.6 us  [step_chunk(): got = lax.ppermute(send, devices, plan.perm(step))]
    pallas_call x2 -> x1, Pallas kernels: 22.8 us -> 21.8 us  [ffn_backward(): pl.pallas_call(kernel, grid_spec=pltpu.PrefetchScalarGridSpec(num_scalar_...]
  transfers between devices with their start and end apart: 31 -> 31, of which waited for: 12 -> 13; matrix products, arithmetic and copies ran while one was open for 9% -> 10% of each run, Pallas kernels for 22% -> 19%
where the time goes in v4:
time: 253 us; the launch traced here: 252 us
  Pallas kernels  101 us (40%)
  waiting for transfers between devices  73.4 us (29%)
  starting transfers between devices  44 us (17%)
  other arithmetic  16.1 us (6%)
  local copies, waits for them, and re-layouts  9.76 us (4%)
  matrix products  5.09 us (2%)
  between operations  2.57 us (1%)
    ppermute x12, waiting for transfers between devices, step_chunk(): got = lax.ppermute(send, devices, plan.perm(step))  58.6 us
    ppermute x16, starting transfers between devices, swap_seq(): return lax.ppermute(x, 'seq', [(i, i ^ k) for i in range(nseq)])  22.2 us
    pallas_call x1, Pallas kernels, ffn_backward(): pl.pallas_call(kernel, grid_spec=pltpu.PrefetchScalarGridSpec(num_scalar_...  21.8 us
    pallas_call x1, Pallas kernels, ffn_forward(): pl.pallas_call(kernel, grid=(inner // BLOCK,), in_specs=[full(flat), full...  21.4 us
    ppermute x12, starting transfers between devices, step_chunk(): got = lax.ppermute(send, devices, plan.perm(step))  21.3 us
    pallas_call x1, Pallas kernels, attention_backward(): pl.pallas_call(attn_bwd_kernel, grid=(segs, pairs), in_specs=[spec] * 5 +...  12.5 us
    ppermute x16, waiting for transfers between devices, swap_seq(): return lax.ppermute(x, 'seq', [(i, i ^ k) for i in range(nseq)])  11.8 us
    pallas_call x1, Pallas kernels, attention_forward(): pl.pallas_call(attn_fwd_kernel, grid=(segs, pairs), in_specs=[spec, spec,...  11.4 us
  transfers between devices with their start and end apart: 31, of which 13 were waited for; matrix products, arithmetic and copies ran while one was open for 10% of the time, Pallas kernels for 19%

profile of v4, /device:TPU:0, one launch (start us, length us, event | category | flops | bytes accessed | tf_op | source)
XLA Modules:
  0.0 252.3 jit_solution(7285534481033876449)
XLA Ops:
  2.8 2.4 collective-permute-start.2
  22.6 11.4 %attn_fwd.1 = (bf16[512,768]{1,0:T(8,128)(2,1)}, bf16[12,512,512]{2,1,0:T(8,128)(2,1)}) custom-call(bf16[512,768]{1,0:T(8,128)(2,1)} %add_convert_fusion.4.q_ref, bf16[512,768]{1,0:T(8,128)(2,1)} %convolution_convert_fusion.k_ref, bf16[512,768]{1,0:T(8,128)(2,1)} %add_convert_fusion.3.v_ref), custom_call_target="tpu_custom_call" | custom-call | tf_op jit(solution)/shard_map/attn_fwd/pallas_call | solution.py:81
  34.0 21.4 %ffn_fwd.1 = (f32[512,768]{1,0:T(8,128)}, f32[512,128]{1,0:T(8,128)}, bf16[768,512]{1,0:T(8,128)(2,1)}, bf16[512,3072]{1,0:T(8,128)(2,1)}, bf16[512,3072]{1,0:T(...) custom-call(bf16[512,768]{1,0:T(8,128)(2,1)} %copy-done, ...), custom_call_target="tpu_custom_call" | custom-call | tf_op jit(solution)/shard_map/ffn_fwd/pallas_call | solution.py:217
  55.4 8.6 %outer_grad.1 = (bf16[16,104,768]{2,1,0:T(8,128)(2,1)}, bf16[16,104,768]{2,1,0:T(8,128)(2,1)}) custom-call(s32[3]{0:T(128)} %pad_add_fusion.me_ref, bf16[512,3072]{1,0:T(8,128)(2,1)} %get-tuple-element.74.active_ref, bf16[512,768]{1,0:T(8,128)(2,1)} %get-tuple-element.81.d_ref.douter_ref, f32[8,768]{1,0:T(8,128)} %get-tuple-element.75.small_ref.s2_ref), custom_call_target="tpu_custom_call" | custom-call | tf_op jit(solution)/shard_map/outer_grad/pallas_call | solution.py:356
  64.0 21.8 %ffn_bwd.1 = (bf16[16,96,768]{2,1,0:T(8,128)(2,1)}, bf16[16,96,768]{2,1,0:T(8,128)(2,1)}, f32[512,768]{1,0:T(8,128)}, bf16[512,768]{1,0:T(8,128)(2,1)}, bf16[512...) custom-call(s32[3]{0:T(128)} %pad_add_fusion.me_ref, bf16[512,3072]{1,0:T(8,128)(2,1)} %get-tuple-element.80.slope_ref, ...), custom_call_target="tpu_custom_call" | custom-call | tf_op jit(solution)/shard_map/ffn_bwd/pallas_call | solution.py:413
  85.9 12.5 %attn_bwd.1 = (bf16[512,768]{1,0:T(8,128)(2,1)}, bf16[512,768]{1,0:T(8,128)(2,1)}, bf16[512,768]{1,0:T(8,128)(2,1)}) custom-call(bf16[512,768]{1,0:T(8,128)(2,1)} %add_convert_fusion.4.q_ref, bf16[512,768]{1,0:T(8,128)(2,1)} %convolution_convert_fusion.k_ref, bf16[512,768]{1,0:T(8,128)(2,1)} %add_convert_fusion.3.v_ref, ...), custom_call_target="tpu_custom_call" | custom-call | tf_op jit(solution)/shard_map/attn_bwd/pallas_call | solution.py:100
  98.4 6.2 %inputs_bwd.1 = (bf16[128,768]{1,0:T(8,128)(2,1)}, bf16[128,768]{1,0:T(8,128)(2,1)}, bf16[128,768]{1,0:T(8,128)(2,1)}, bf16[128,768]{1,0:T(8,128)(2,1)}, f32[4,8,768]{2,1,0:T(8,128)}) custom-call(s32[3]{0:T(128)} %pad_add_fusion.me_ref, bf16[512,768]{1,0:T(8,128)(2,1)} %get-tuple-element.88.dq_ref.d0_ref, bf16[512,768]{1,0:T(8,128)(2,1)} %get-tuple-element.89.dk_ref.d1_ref, ...), custom_call_target="tpu_custom_call" | custom-call | tf_op jit(solution)/shard_map/inputs_bwd/pallas_call | solution.py:267
  104.7 9.9 %attn_grad.1 = (bf16[16,104,768]{2,1,0:T(8,128)(2,1)}, bf16[16,104,768]{2,1,0:T(8,128)(2,1)}) custom-call(s32[3]{0:T(128)} %pad_add_fusion.me_ref, bf16[512,768]{1,0:T(8,128)(2,1)} %copy-done, bf16[512,768]{1,0:T(8,128)(2,1)} %get-tuple-element.66.ctx_ref, bf16[512,768]{1,0:T(8,128)(2,1)} %get-tuple-element.88.dq_ref.d0_ref, ...), custom_call_target="tpu_custom_call" | custom-call | tf_op jit(solution)/shard_map/attn_grad/pallas_call | solution.py:528
  125.1 7.9 %collective-permute-done.25 = bf16[8,96,768]{2,1,0:T(8,128)(2,1)S(1)} collective-permute-done((bf16[8,96,768]{2,1,0:T(8,128)(2,1)S(1)}, bf16[8,96,768]{2,1,0:T(8,128)(2,1)S(1)}, u32[]{:S(2)}, u32[]{:S(2)}) %collective-permute-start.25) | collective-permute-done | bytes 1179680 | tf_op jit(solution)/shard_map/ppermute | solution.py:567
  135.8 10.9 %collective-permute-done.18 = bf16[8,104,768]{2,1,0:T(8,128)(2,1)S(1)} collective-permute-done((bf16[8,104,768]{2,1,0:T(8,128)(2,1)S(1)}, bf16[8,104,768]{2,1,0:T(8,128)(2,1)S(1)}, u32[]{:S(2)}, u32[]{:S(2)}) %collective-permute-start.18) | collective-permute-done | bytes 1277984 | tf_op jit(solution)/shard_map/ppermute | solution.py:567
  153.3 7.1 %collective-permute-done.10 = bf16[8,104,768]{2,1,0:T(8,128)(2,1)S(1)} collective-permute-done((bf16[8,104,768]{2,1,0:T(8,128)(2,1)S(1)}, bf16[8,104,768]{2,1,0:T(8,128)(2,1)S(1)}, u32[]{:S(2)}, u32[]{:S(2)}) %collective-permute-start.10) | collective-permute-done | bytes 1277984 | tf_op jit(solution)/shard_map/ppermute | solution.py:567
  163.2 2.7 %collective-permute-start.28 = (bf16[1,96,768]{2,1,0:T(8,128)(2,1)S(1)}, bf16[1,96,768]{2,1,0:T(8,128)(2,1)S(1)}, u32[]{:S(2)}, u32[]{:S(2)}) collective-permute-start(bf16[1,96,768]{2,1,0:T(8,128)(2,1)S(1)} %add_convert_fusion.15), channel_id=1, source_target_pairs={{0,16},{1,3},{2,18},{3,1},{4,20},{5,7},{6,22},{7,5},{8,24},{9,11},... | collective-permute-start | bytes 442376 | tf_op jit(solution)/shard_map/ppermute | solution.py:567
  167.7 10.3 %collective-permute-done.11 = bf16[4,104,768]{2,1,0:T(8,128)(2,1)S(1)} collective-permute-done((bf16[4,104,768]{2,1,0:T(8,128)(2,1)S(1)}, bf16[4,104,768]{2,1,0:T(8,128)(2,1)S(1)}, u32[]{:S(2)}, u32[]{:S(2)}) %collective-permute-start.11) | collective-permute-done | bytes 639008 | tf_op jit(solution)/shard_map/ppermute | solution.py:567
  180.9 2.7 %collective-permute-start.21 = (bf16[1,104,768]{2,1,0:T(8,128)(2,1)S(1)}, bf16[1,104,768]{2,1,0:T(8,128)(2,1)S(1)}, u32[]{:S(2)}, u32[]{:S(2)}) collective-permute-start(bf16[1,104,768]{2,1,0:T(8,128)(2,1)S(1)} %add_convert_fusion.12), channel_id=1, source_target_pairs={{0,16},{1,3},{2,18},{3,1},{4,20},{5,7},{6,22},{7,5},{8,24},{9,11},... | collective-permute-start | bytes 479240 | tf_op jit(solution)/shard_map/ppermute | solution.py:567
  183.6 9.3 %collective-permute-done.12 = bf16[2,104,768]{2,1,0:T(8,128)(2,1)S(1)} collective-permute-done((bf16[2,104,768]{2,1,0:T(8,128)(2,1)S(1)}, bf16[2,104,768]{2,1,0:T(8,128)(2,1)S(1)}, u32[]{:S(2)}, u32[]{:S(2)}) %collective-permute-start.12) | collective-permute-done | bytes 319520 | tf_op jit(solution)/shard_map/ppermute | solution.py:567
  196.6 11.1 %collective-permute-done.13 = bf16[1,104,768]{2,1,0:T(8,128)(2,1)S(1)} collective-permute-done((bf16[1,104,768]{2,1,0:T(8,128)(2,1)S(1)}, bf16[1,104,768]{2,1,0:T(8,128)(2,1)S(1)}, u32[]{:S(2)}, u32[]{:S(2)}) %collective-permute-start.13) | collective-permute-done | bytes 159776 | tf_op jit(solution)/shard_map/ppermute | solution.py:567
  209.4 7.7 %collective-permute-start.6 = (bf16[128,768]{1,0:T(8,128)(2,1)S(1)}, bf16[128,768]{1,0:T(8,128)(2,1)S(1)}, u32[]{:S(2)}, u32[]{:S(2)}) collective-permute-start(bf16[128,768]{1,0:T(8,128)(2,1)S(1)} %copy-done.33), channel_id=1, source_target_pairs={{0,1},{1,0},{2,3},{3,2},{4,5},{5,4},{6,7},{7,6},{8,9},{9,8},{10,11... | collective-permute-start | bytes 589832 | tf_op jit(solution)/shard_map/ppermute | solution.py:571
  219.5 5.4 %collective-permute-done.7.refs_2_ = bf16[128,768]{1,0:T(8,128)(2,1)S(1)} collective-permute-done((bf16[128,768]{1,0:T(8,128)(2,1)S(1)}, bf16[128,768]{1,0:T(8,128)(2,1)S(1)}, u32[]{:S(2)}, u32[]{:S(2)}) %collective-permute-start.7) | collective-permute-done | bytes 196640 | tf_op jit(solution)/shard_map/ppermute | solution.py:571
  225.4 3.4 %collective-permute-start.16 = (bf16[128,768]{1,0:T(8,128)(2,1)S(1)}, bf16[128,768]{1,0:T(8,128)(2,1)S(1)}, u32[]{:S(2)}, u32[]{:S(2)}) collective-permute-start(bf16[128,768]{1,0:T(8,128)(2,1)S(1)} %copy-done.30), channel_id=1, source_target_pairs={{0,3},{1,2},{2,1},{3,0},{4,7},{5,6},{6,5},{7,4},{8,11},{9,10},{10,... | collective-permute-start | bytes 589832 | tf_op jit(solution)/shard_map/ppermute | solution.py:571
  228.9 2.2 collective-permute-done.8.refs_3_
  231.7 2.2 shard_map.331
  235.2 3.3 %collective-permute-done.16.refs_3_ = bf16[128,768]{1,0:T(8,128)(2,1)S(1)} collective-permute-done((bf16[128,768]{1,0:T(8,128)(2,1)S(1)}, bf16[128,768]{1,0:T(8,128)(2,1)S(1)}, u32[]{:S(2)}, u32[]{:S(2)}) %collective-permute-start.16) | collective-permute-done | bytes 196640 | tf_op jit(solution)/shard_map/ppermute | solution.py:571
  239.2 2.5 shard_map.332
  249.4 2.8 %shard_map.334 = (f32[384,768]{1,0:T(8,128)}, f32[96,3072]{1,0:T(8,128)}) custom-call(s32[3]{0:T(128)} %pad_add_fusion.me_ref, f32[1]{0:T(128)} %bitcast.18.factor_ref, bf16[2,192,768]{2,1,0:T(8,128)(2,1)} %copy-done.4, bf16[2,192,768]{2,1,0:T(8,128)(2,1)} %copy-done.10), custom_call_target="tpu_custom_call" | custom-call | tf_op jit(solution)/shard_map/pallas_call | solution.py:504
  (176 shorter events, 64.3 us)
Async XLA Ops:
  2.8 12.4 %collective-permute-start.2 = (bf16[128,768]{1,0:T(8,128)(2,1)}, bf16[128,768]{1,0:T(8,128)(2,1)}, u32[]{:S(2)}, u32[]{:S(2)}) collective-permute-start(bf16[128,768]{1,0:T(8,128)(2,1)} %get-tuple-element.120), channel_id=1, source_target_pairs={{0,3},{1,2},{2,1},{3,0},{4,7},{5,6},{6,5},{7,4},{8,11},{9,10},{10,... | collective-permute-start | bytes 589832 | tf_op jit(solution)/shard_map/ppermute | solution.py:571
  5.2 10.8 %collective-permute-start.1 = (bf16[128,768]{1,0:T(8,128)(2,1)}, bf16[128,768]{1,0:T(8,128)(2,1)}, u32[]{:S(2)}, u32[]{:S(2)}) collective-permute-start(bf16[128,768]{1,0:T(8,128)(2,1)} %get-tuple-element.121), channel_id=1, source_target_pairs={{0,2},{1,3},{2,0},{3,1},{4,6},{5,7},{6,4},{7,5},{8,10},{9,11},{10,... | collective-permute-start | bytes 589832 | tf_op jit(solution)/shard_map/ppermute | solution.py:571
  7.2 26.7 %collective-permute-start.3 = (bf16[136,768]{1,0:T(8,128)(2,1)}, bf16[136,768]{1,0:T(8,128)(2,1)}, u32[]{:S(2)}, u32[]{:S(2)}) collective-permute-start(bf16[136,768]{1,0:T(8,128)(2,1)} %get-tuple-element.116), channel_id=1, source_target_pairs={{0,1},{1,0},{2,3},{3,2},{4,5},{5,4},{6,7},{7,6},{8,9},{9,8},{10,11... | collective-permute-start | bytes 626696 | tf_op jit(solution)/shard_map/ppermute | solution.py:571
  7.6 26.3 %collective-permute-start.4 = (bf16[136,768]{1,0:T(8,128)(2,1)S(1)}, bf16[136,768]{1,0:T(8,128)(2,1)}, u32[]{:S(2)}, u32[]{:S(2)}) collective-permute-start(bf16[136,768]{1,0:T(8,128)(2,1)S(1)} %get-tuple-element.117), channel_id=1, source_target_pairs={{0,2},{1,3},{2,0},{3,1},{4,6},{5,7},{6,4},{7,5},{8,10},{9,11},{10,... | collective-permute-start | bytes 626696 | tf_op jit(solution)/shard_map/ppermute | solution.py:571
  15.2 18.8 %collective-permute-start.5 = (bf16[136,768]{1,0:T(8,128)(2,1)S(1)}, bf16[136,768]{1,0:T(8,128)(2,1)}, u32[]{:S(2)}, u32[]{:S(2)}) collective-permute-start(bf16[136,768]{1,0:T(8,128)(2,1)S(1)} %get-tuple-element.114), channel_id=1, source_target_pairs={{0,3},{1,2},{2,1},{3,0},{4,7},{5,6},{6,5},{7,4},{8,11},{9,10},{10,... | collective-permute-start | bytes 626696 | tf_op jit(solution)/shard_map/ppermute | solution.py:571
  85.9 29.2 %collective-permute-start.24 = (bf16[16,96,768]{2,1,0:T(8,128)(2,1)}, bf16[16,96,768]{2,1,0:T(8,128)(2,1)}, u32[]{:S(2)}, u32[]{:S(2)}) collective-permute-start(bf16[16,96,768]{2,1,0:T(8,128)(2,1)} %get-tuple-element.108), channel_id=1, source_target_pairs={{0,1},{1,0},{2,3},{3,2},{4,5},{5,4},{6,7},{7,6},{8,9},{9,8},{10,11... | collective-permute-start | bytes 7077896 | tf_op jit(solution)/shard_map/ppermute | solution.py:562
  116.7 16.3 %collective-permute-start.25 = (bf16[8,96,768]{2,1,0:T(8,128)(2,1)S(1)}, bf16[8,96,768]{2,1,0:T(8,128)(2,1)S(1)}, u32[]{:S(2)}, u32[]{:S(2)}) collective-permute-start(bf16[8,96,768]{2,1,0:T(8,128)(2,1)S(1)} %add_convert_fusion.2), channel_id=1, source_target_pairs={{0,2},{1,5},{2,0},{3,7},{4,6},{5,1},{6,4},{7,3},{8,10},{9,13},{10,... | collective-permute-start | bytes 3538952 | tf_op jit(solution)/shard_map/ppermute | solution.py:567
  119.9 26.8 %collective-permute-start.18 = (bf16[8,104,768]{2,1,0:T(8,128)(2,1)S(1)}, bf16[8,104,768]{2,1,0:T(8,128)(2,1)S(1)}, u32[]{:S(2)}, u32[]{:S(2)}) collective-permute-start(bf16[8,104,768]{2,1,0:T(8,128)(2,1)S(1)} %add_convert_fusion), channel_id=1, source_target_pairs={{0,2},{1,5},{2,0},{3,7},{4,6},{5,1},{6,4},{7,3},{8,10},{9,13},{10,... | collective-permute-start | bytes 3833864 | tf_op jit(solution)/shard_map/ppermute | solution.py:567
  123.6 36.8 %collective-permute-start.10 = (bf16[8,104,768]{2,1,0:T(8,128)(2,1)S(1)}, bf16[8,104,768]{2,1,0:T(8,128)(2,1)S(1)}, u32[]{:S(2)}, u32[]{:S(2)}) collective-permute-start(bf16[8,104,768]{2,1,0:T(8,128)(2,1)S(1)} %add_convert_fusion.1), channel_id=1, source_target_pairs={{0,2},{1,5},{2,0},{3,7},{4,6},{5,1},{6,4},{7,3},{8,10},{9,13},{10,... | collective-permute-start | bytes 3833864 | tf_op jit(solution)/shard_map/ppermute | solution.py:567
  134.3 16.3 %collective-permute-start.26 = (bf16[4,96,768]{2,1,0:T(8,128)(2,1)S(1)}, bf16[4,96,768]{2,1,0:T(8,128)(2,1)S(1)}, u32[]{:S(2)}, u32[]{:S(2)}) collective-permute-start(bf16[4,96,768]{2,1,0:T(8,128)(2,1)S(1)} %add_convert_fusion.7), channel_id=1, source_target_pairs={{0,4},{1,9},{2,6},{3,11},{4,0},{5,13},{6,2},{7,15},{8,12},{9,1},{1... | collective-permute-start | bytes 1769480 | tf_op jit(solution)/shard_map/ppermute | solution.py:567
  146.9 19.0 %collective-permute-start.19 = (bf16[4,104,768]{2,1,0:T(8,128)(2,1)S(1)}, bf16[4,104,768]{2,1,0:T(8,128)(2,1)S(1)}, u32[]{:S(2)}, u32[]{:S(2)}) collective-permute-start(bf16[4,104,768]{2,1,0:T(8,128)(2,1)S(1)} %add_convert_fusion.5), channel_id=1, source_target_pairs={{0,4},{1,9},{2,6},{3,11},{4,0},{5,13},{6,2},{7,15},{8,12},{9,1},{1... | collective-permute-start | bytes 1916936 | tf_op jit(solution)/shard_map/ppermute | solution.py:567
  160.7 17.3 %collective-permute-start.11 = (bf16[4,104,768]{2,1,0:T(8,128)(2,1)S(1)}, bf16[4,104,768]{2,1,0:T(8,128)(2,1)S(1)}, u32[]{:S(2)}, u32[]{:S(2)}) collective-permute-start(bf16[4,104,768]{2,1,0:T(8,128)(2,1)S(1)} %add_convert_fusion.6), channel_id=1, source_target_pairs={{0,4},{1,9},{2,6},{3,11},{4,0},{5,13},{6,2},{7,15},{8,12},{9,1},{1... | collective-permute-start | bytes 1916936 | tf_op jit(solution)/shard_map/ppermute | solution.py:567
  163.2 16.5 %collective-permute-start.28 = (bf16[1,96,768]{2,1,0:T(8,128)(2,1)S(1)}, bf16[1,96,768]{2,1,0:T(8,128)(2,1)S(1)}, u32[]{:S(2)}, u32[]{:S(2)}) collective-permute-start(bf16[1,96,768]{2,1,0:T(8,128)(2,1)S(1)} %add_convert_fusion.15), channel_id=1, source_target_pairs={{0,16},{1,3},{2,18},{3,1},{4,20},{5,7},{6,22},{7,5},{8,24},{9,11},... | collective-permute-start | bytes 442376 | tf_op jit(solution)/shard_map/ppermute | solution.py:567
  166.1 14.8 %collective-permute-start.20 = (bf16[2,104,768]{2,1,0:T(8,128)(2,1)S(1)}, bf16[2,104,768]{2,1,0:T(8,128)(2,1)S(1)}, u32[]{:S(2)}, u32[]{:S(2)}) collective-permute-start(bf16[2,104,768]{2,1,0:T(8,128)(2,1)S(1)} %add_convert_fusion.8), channel_id=1, source_target_pairs={{0,8},{1,17},{2,10},{3,19},{4,12},{5,21},{6,14},{7,23},{8,0},{9,25... | collective-permute-start | bytes 958472 | tf_op jit(solution)/shard_map/ppermute | solution.py:567
  178.1 14.8 %collective-permute-start.12 = (bf16[2,104,768]{2,1,0:T(8,128)(2,1)S(1)}, bf16[2,104,768]{2,1,0:T(8,128)(2,1)S(1)}, u32[]{:S(2)}, u32[]{:S(2)}) collective-permute-start(bf16[2,104,768]{2,1,0:T(8,128)(2,1)S(1)} %add_convert_fusion.9), channel_id=1, source_target_pairs={{0,8},{1,17},{2,10},{3,19},{4,12},{5,21},{6,14},{7,23},{8,0},{9,25... | collective-permute-start | bytes 958472 | tf_op jit(solution)/shard_map/ppermute | solution.py:567
  180.9 13.9 %collective-permute-start.21 = (bf16[1,104,768]{2,1,0:T(8,128)(2,1)S(1)}, bf16[1,104,768]{2,1,0:T(8,128)(2,1)S(1)}, u32[]{:S(2)}, u32[]{:S(2)}) collective-permute-start(bf16[1,104,768]{2,1,0:T(8,128)(2,1)S(1)} %add_convert_fusion.12), channel_id=1, source_target_pairs={{0,16},{1,3},{2,18},{3,1},{4,20},{5,7},{6,22},{7,5},{8,24},{9,11},... | collective-permute-start | bytes 479240 | tf_op jit(solution)/shard_map/ppermute | solution.py:567
  193.1 14.6 %collective-permute-start.13 = (bf16[1,104,768]{2,1,0:T(8,128)(2,1)S(1)}, bf16[1,104,768]{2,1,0:T(8,128)(2,1)S(1)}, u32[]{:S(2)}, u32[]{:S(2)}) collective-permute-start(bf16[1,104,768]{2,1,0:T(8,128)(2,1)S(1)} %add_convert_fusion.13), channel_id=1, source_target_pairs={{0,16},{1,3},{2,18},{3,1},{4,20},{5,7},{6,22},{7,5},{8,24},{9,11},... | collective-permute-start | bytes 479240 | tf_op jit(solution)/shard_map/ppermute | solution.py:567
  195.0 23.6 %collective-permute-start.22 = (bf16[104,768]{1,0:T(8,128)(2,1)S(1)}, bf16[104,768]{1,0:T(8,128)(2,1)S(1)}, u32[]{:S(2)}, u32[]{:S(2)}) collective-permute-start(bf16[104,768]{1,0:T(8,128)(2,1)S(1)} %bitcast.68), channel_id=1, source_target_pairs={{0,2},{1,3},{2,0},{3,1},{4,6},{5,7},{6,4},{7,5},{8,10},{9,11},{10,... | collective-permute-start | bytes 479240 | tf_op jit(solution)/shard_map/ppermute | solution.py:571
  207.9 17.6 %collective-permute-start.29 = (bf16[192,768]{1,0:T(8,128)(2,1)S(1)}, bf16[192,768]{1,0:T(8,128)(2,1)S(1)}, u32[]{:S(2)}, u32[]{:S(2)}) collective-permute-start(bf16[192,768]{1,0:T(8,128)(2,1)S(1)} %pad_maximum_fusion.2), channel_id=1, source_target_pairs={{0,2},{1,3},{2,0},{3,1},{4,6},{5,7},{6,4},{7,5},{8,10},{9,11},{10,... | collective-permute-start | bytes 884744 | tf_op jit(solution)/shard_map/ppermute | solution.py:571
  217.6 13.4 %collective-permute-start.8 = (bf16[128,768]{1,0:T(8,128)(2,1)S(1)}, bf16[128,768]{1,0:T(8,128)(2,1)S(1)}, u32[]{:S(2)}, u32[]{:S(2)}) collective-permute-start(bf16[128,768]{1,0:T(8,128)(2,1)S(1)} %copy-done.31), channel_id=1, source_target_pairs={{0,3},{1,2},{2,1},{3,0},{4,7},{5,6},{6,5},{7,4},{8,11},{9,10},{10,... | collective-permute-start | bytes 589832 | tf_op jit(solution)/shard_map/ppermute | solution.py:571
  218.6 23.1 %collective-permute-start.23 = (bf16[2,104,768]{2,1,0:T(8,128)(2,1)S(1)}, bf16[2,104,768]{2,1,0:T(8,128)(2,1)S(1)}, u32[]{:S(2)}, u32[]{:S(2)}) collective-permute-start(bf16[2,104,768]{2,1,0:T(8,128)(2,1)S(1)} %pad_maximum_fusion.1.near_ref), channel_id=1, source_target_pairs={{0,1},{1,0},{2,3},{3,2},{4,5},{5,4},{6,7},{7,6},{8,9},{9,8},{10,11... | collective-permute-start | bytes 958472 | tf_op jit(solution)/shard_map/ppermute | solution.py:571
  219.4 15.7 %collective-permute-start.14 = (bf16[128,768]{1,0:T(8,128)(2,1)}, bf16[128,768]{1,0:T(8,128)(2,1)S(1)}, u32[]{:S(2)}, u32[]{:S(2)}) collective-permute-start(bf16[128,768]{1,0:T(8,128)(2,1)} %get-tuple-element.95), channel_id=1, source_target_pairs={{0,1},{1,0},{2,3},{3,2},{4,5},{5,4},{6,7},{7,6},{8,9},{9,8},{10,11... | collective-permute-start | bytes 589832 | tf_op jit(solution)/shard_map/ppermute | solution.py:571
  225.4 13.1 %collective-permute-start.16 = (bf16[128,768]{1,0:T(8,128)(2,1)S(1)}, bf16[128,768]{1,0:T(8,128)(2,1)S(1)}, u32[]{:S(2)}, u32[]{:S(2)}) collective-permute-start(bf16[128,768]{1,0:T(8,128)(2,1)S(1)} %copy-done.30), channel_id=1, source_target_pairs={{0,3},{1,2},{2,1},{3,0},{4,7},{5,6},{6,5},{7,4},{8,11},{9,10},{10,... | collective-permute-start | bytes 589832 | tf_op jit(solution)/shard_map/ppermute | solution.py:571
  231.0 17.6 %collective-permute-start.30 = (bf16[2,192,768]{2,1,0:T(8,128)(2,1)S(1)}, bf16[2,192,768]{2,1,0:T(8,128)(2,1)S(1)}, u32[]{:S(2)}, u32[]{:S(2)}) collective-permute-start(bf16[2,192,768]{2,1,0:T(8,128)(2,1)S(1)} %pad_maximum_fusion.near_ref), channel_id=1, source_target_pairs={{0,1},{1,0},{2,3},{3,2},{4,5},{5,4},{6,7},{7,6},{8,9},{9,8},{10,11... | collective-permute-start | bytes 1769480 | tf_op jit(solution)/shard_map/ppermute | solution.py:571
  (41 other events, 307.4 us)

commit v5 on v4

--- a/solution.py
+++ b/solution.py
@@ -470,17 +470,23 @@
     )(me, factor, *pieces)
 
 
-def finish_weights(me, factor, near, far, split):
+def finish_weights(me, factor, near, far, split, ndp):
     width = near.shape[2]
     count = 4
     shapes = []
     for start, rows, axis in split:
         if axis is None:
             shapes += [(rows, width)] * count
+        elif axis == "dp":
+            shapes.append((count, rows, width // ndp))
         else:
             shapes.append((count * rows, width) if axis == 0 else (rows, count * width))
 
     def kernel(me_ref, factor_ref, near_ref, far_ref, *outs):
+        if any(axis == "dp" for _, _, axis in split):
+            shape = (width, width // ndp)
+            column = lax.broadcasted_iota(jnp.int32, shape, 1) + me_ref[0] * (width // ndp)
+            pick = (lax.broadcasted_iota(jnp.int32, shape, 0) == column).astype(f32).astype(bf16)
         for s in range(count):
             diff = me_ref[1] ^ s
             at = diff >> 1
@@ -488,6 +494,10 @@
             for start, rows, axis in split:
                 part = slice(start, start + rows)
                 value = jnp.where((diff & 1) == 0, near_ref[at, part], far_ref[at, part])
+                if axis == "dp":
+                    outs[o][s] = dot(value, pick, 1, 0) * factor_ref[0]
+                    o += 1
+                    continue
                 value = value.astype(f32) * factor_ref[0]
                 if axis is None:
                     outs[o + s][...] = value
@@ -741,10 +751,15 @@
         scale = factor.reshape(1)
         if aligned:
             tokens_grad = finish_rows(me, scale, cut_pieces, f32)
-            g_outer, g_inner = finish_weights(me, scale, ffn_near, ffn_far, [(0, outer_rows, 0), (outer_rows, part, 1)])
-            got = finish_weights(me, scale, attn_near, attn_far, [(0, part, None), (part, EXTRA, None)])
+            g_outer, g_inner = finish_weights(
+                me, scale, ffn_near, ffn_far, [(0, outer_rows, 0), (outer_rows, part, 1)], ndp
+            )
+            got = finish_weights(
+                me, scale, attn_near, attn_far, [(0, part, None), (part, EXTRA, None), (part, EXTRA, "dp")], ndp
+            )
             g_query, g_key, g_value, g_output = got[:4]
-            small_parts = got[4:]
+            small_parts = got[4:8]
+            small_cols = got[8]
         else:
             finish = lambda x: x.astype(f32) * factor
             tokens_grad = to_rows(cut_pieces, finish)
@@ -759,9 +774,9 @@
             attn_parts = in_order(attn_near, attn_far)
             g_query, g_key, g_value, g_output = [p[:part] for p in attn_parts]
             small_parts = [p[part:] for p in attn_parts]
-        mine = lambda x: lax.dynamic_slice_in_dim(x, dp_index * part, part, axis=1)
-        vec_rows = mine(small_parts[0][:8])
-        g_memory = mine(jnp.concatenate([small_parts[2], small_parts[3]])[:mem_rows]).T
+            small_cols = lax.dynamic_slice_in_dim(jnp.stack(small_parts), dp_index * part, part, axis=2)
+        vec_rows = small_cols[0]
+        g_memory = jnp.concatenate([small_cols[2], small_cols[3]])[:mem_rows].T
         inner_part = ff // ndp
         g_inner_bias = lax.dynamic_slice_in_dim(
             small_parts[1][:ib_rows].reshape(-1), dp_index * inner_part, inner_part, axis=0

time: 253 us -> 253 us (level)
  no operation moved by 1% of the time
where the time goes in v5:
time: 253 us; the launch traced here: 252 us
  Pallas kernels  102 us (40%)
  waiting for transfers between devices  74 us (29%)
  starting transfers between devices  42.5 us (17%)
  other arithmetic  15.3 us (6%)
  local copies, waits for them, and re-layouts  10.7 us (4%)
  matrix products  5.08 us (2%)
  between operations  2.6 us (1%)
    ppermute x12, waiting for transfers between devices, step_chunk(): got = lax.ppermute(send, devices, plan.perm(step))  58.5 us
    pallas_call x1, Pallas kernels, ffn_backward(): pl.pallas_call(kernel, grid_spec=pltpu.PrefetchScalarGridSpec(num_scalar_...  21.7 us
    pallas_call x1, Pallas kernels, ffn_forward(): pl.pallas_call(kernel, grid=(inner // BLOCK,), in_specs=[full(flat), full...  21.4 us
    ppermute x12, starting transfers between devices, step_chunk(): got = lax.ppermute(send, devices, plan.perm(step))  21.3 us
    ppermute x16, starting transfers between devices, swap_seq(): return lax.ppermute(x, 'seq', [(i, i ^ k) for i in range(nseq)])  20.7 us
    pallas_call x1, Pallas kernels, attention_backward(): pl.pallas_call(attn_bwd_kernel, grid=(segs, pairs), in_specs=[spec] * 5 +...  12.4 us
    ppermute x16, waiting for transfers between devices, swap_seq(): return lax.ppermute(x, 'seq', [(i, i ^ k) for i in range(nseq)])  12.4 us
    pallas_call x1, Pallas kernels, attention_forward(): pl.pallas_call(attn_fwd_kernel, grid=(segs, pairs), in_specs=[spec, spec,...  11.4 us
  transfers between devices with their start and end apart: 31, of which 13 were waited for; matrix products, arithmetic and copies ran while one was open for 10% of the time, Pallas kernels for 19%

profile of v5, /device:TPU:0, one launch (start us, length us, event | category | flops | bytes accessed | tf_op | source)
XLA Modules:
  0.0 251.8 jit_solution(5312873804072558244)
XLA Ops:
  0.7 2.1 dynamic-slice_bitcast_fusion.3
  2.8 2.4 collective-permute-start.2
  22.6 11.4 %attn_fwd.1 = (bf16[512,768]{1,0:T(8,128)(2,1)}, bf16[12,512,512]{2,1,0:T(8,128)(2,1)}) custom-call(bf16[512,768]{1,0:T(8,128)(2,1)} %add_convert_fusion.4.q_ref, bf16[512,768]{1,0:T(8,128)(2,1)} %convolution_convert_fusion.k_ref, bf16[512,768]{1,0:T(8,128)(2,1)} %add_convert_fusion.3.v_ref), custom_call_target="tpu_custom_call" | custom-call | tf_op jit(solution)/shard_map/attn_fwd/pallas_call | solution.py:81
  34.0 21.4 %ffn_fwd.1 = (f32[512,768]{1,0:T(8,128)}, f32[512,128]{1,0:T(8,128)}, bf16[768,512]{1,0:T(8,128)(2,1)}, bf16[512,3072]{1,0:T(8,128)(2,1)}, bf16[512,3072]{1,0:T(...) custom-call(bf16[512,768]{1,0:T(8,128)(2,1)} %copy-done, ...), custom_call_target="tpu_custom_call" | custom-call | tf_op jit(solution)/shard_map/ffn_fwd/pallas_call | solution.py:217
  55.4 8.7 %outer_grad.1 = (bf16[16,104,768]{2,1,0:T(8,128)(2,1)}, bf16[16,104,768]{2,1,0:T(8,128)(2,1)}) custom-call(s32[3]{0:T(128)} %pad_add_fusion.me_ref, bf16[512,3072]{1,0:T(8,128)(2,1)} %get-tuple-element.72.active_ref, bf16[512,768]{1,0:T(8,128)(2,1)} %get-tuple-element.79.d_ref.douter_ref, f32[8,768]{1,0:T(8,128)} %get-tuple-element.73.small_ref.s2_ref), custom_call_target="tpu_custom_call" | custom-call | tf_op jit(solution)/shard_map/outer_grad/pallas_call | solution.py:356
  64.1 21.7 %ffn_bwd.1 = (bf16[16,96,768]{2,1,0:T(8,128)(2,1)}, bf16[16,96,768]{2,1,0:T(8,128)(2,1)}, f32[512,768]{1,0:T(8,128)}, bf16[512,768]{1,0:T(8,128)(2,1)}, bf16[512...) custom-call(s32[3]{0:T(128)} %pad_add_fusion.me_ref, bf16[512,3072]{1,0:T(8,128)(2,1)} %get-tuple-element.78.slope_ref, ...), custom_call_target="tpu_custom_call" | custom-call | tf_op jit(solution)/shard_map/ffn_bwd/pallas_call | solution.py:413
  85.9 12.4 %attn_bwd.1 = (bf16[512,768]{1,0:T(8,128)(2,1)}, bf16[512,768]{1,0:T(8,128)(2,1)}, bf16[512,768]{1,0:T(8,128)(2,1)}) custom-call(bf16[512,768]{1,0:T(8,128)(2,1)} %add_convert_fusion.4.q_ref, bf16[512,768]{1,0:T(8,128)(2,1)} %convolution_convert_fusion.k_ref, bf16[512,768]{1,0:T(8,128)(2,1)} %add_convert_fusion.3.v_ref, ...), custom_call_target="tpu_custom_call" | custom-call | tf_op jit(solution)/shard_map/attn_bwd/pallas_call | solution.py:100
  98.4 6.3 %inputs_bwd.1 = (bf16[128,768]{1,0:T(8,128)(2,1)}, bf16[128,768]{1,0:T(8,128)(2,1)}, bf16[128,768]{1,0:T(8,128)(2,1)}, bf16[128,768]{1,0:T(8,128)(2,1)}, f32[4,8,768]{2,1,0:T(8,128)}) custom-call(s32[3]{0:T(128)} %pad_add_fusion.me_ref, bf16[512,768]{1,0:T(8,128)(2,1)} %get-tuple-element.86.dq_ref.d0_ref, bf16[512,768]{1,0:T(8,128)(2,1)} %get-tuple-element.87.dk_ref.d1_ref, ...), custom_call_target="tpu_custom_call" | custom-call | tf_op jit(solution)/shard_map/inputs_bwd/pallas_call | solution.py:267
  104.6 9.9 %attn_grad.1 = (bf16[16,104,768]{2,1,0:T(8,128)(2,1)}, bf16[16,104,768]{2,1,0:T(8,128)(2,1)}) custom-call(s32[3]{0:T(128)} %pad_add_fusion.me_ref, bf16[512,768]{1,0:T(8,128)(2,1)} %copy-done, bf16[512,768]{1,0:T(8,128)(2,1)} %get-tuple-element.64.ctx_ref, bf16[512,768]{1,0:T(8,128)(2,1)} %get-tuple-element.86.dq_ref.d0_ref, ...), custom_call_target="tpu_custom_call" | custom-call | tf_op jit(solution)/shard_map/attn_grad/pallas_call | solution.py:538
  125.1 7.9 %collective-permute-done.25 = bf16[8,96,768]{2,1,0:T(8,128)(2,1)S(1)} collective-permute-done((bf16[8,96,768]{2,1,0:T(8,128)(2,1)S(1)}, bf16[8,96,768]{2,1,0:T(8,128)(2,1)S(1)}, u32[]{:S(2)}, u32[]{:S(2)}) %collective-permute-start.25) | collective-permute-done | bytes 1179680 | tf_op jit(solution)/shard_map/ppermute | solution.py:577
  135.8 10.8 %collective-permute-done.18 = bf16[8,104,768]{2,1,0:T(8,128)(2,1)S(1)} collective-permute-done((bf16[8,104,768]{2,1,0:T(8,128)(2,1)S(1)}, bf16[8,104,768]{2,1,0:T(8,128)(2,1)S(1)}, u32[]{:S(2)}, u32[]{:S(2)}) %collective-permute-start.18) | collective-permute-done | bytes 1277984 | tf_op jit(solution)/shard_map/ppermute | solution.py:577
  153.3 7.1 %collective-permute-done.10 = bf16[8,104,768]{2,1,0:T(8,128)(2,1)S(1)} collective-permute-done((bf16[8,104,768]{2,1,0:T(8,128)(2,1)S(1)}, bf16[8,104,768]{2,1,0:T(8,128)(2,1)S(1)}, u32[]{:S(2)}, u32[]{:S(2)}) %collective-permute-start.10) | collective-permute-done | bytes 1277984 | tf_op jit(solution)/shard_map/ppermute | solution.py:577
  163.2 2.7 %collective-permute-start.28 = (bf16[1,96,768]{2,1,0:T(8,128)(2,1)S(1)}, bf16[1,96,768]{2,1,0:T(8,128)(2,1)S(1)}, u32[]{:S(2)}, u32[]{:S(2)}) collective-permute-start(bf16[1,96,768]{2,1,0:T(8,128)(2,1)S(1)} %add_convert_fusion.15), channel_id=1, source_target_pairs={{0,16},{1,3},{2,18},{3,1},{4,20},{5,7},{6,22},{7,5},{8,24},{9,11},... | collective-permute-start | bytes 442376 | tf_op jit(solution)/shard_map/ppermute | solution.py:577
  167.7 10.3 %collective-permute-done.11 = bf16[4,104,768]{2,1,0:T(8,128)(2,1)S(1)} collective-permute-done((bf16[4,104,768]{2,1,0:T(8,128)(2,1)S(1)}, bf16[4,104,768]{2,1,0:T(8,128)(2,1)S(1)}, u32[]{:S(2)}, u32[]{:S(2)}) %collective-permute-start.11) | collective-permute-done | bytes 639008 | tf_op jit(solution)/shard_map/ppermute | solution.py:577
  180.9 2.7 %collective-permute-start.21 = (bf16[1,104,768]{2,1,0:T(8,128)(2,1)S(1)}, bf16[1,104,768]{2,1,0:T(8,128)(2,1)S(1)}, u32[]{:S(2)}, u32[]{:S(2)}) collective-permute-start(bf16[1,104,768]{2,1,0:T(8,128)(2,1)S(1)} %add_convert_fusion.12), channel_id=1, source_target_pairs={{0,16},{1,3},{2,18},{3,1},{4,20},{5,7},{6,22},{7,5},{8,24},{9,11},... | collective-permute-start | bytes 479240 | tf_op jit(solution)/shard_map/ppermute | solution.py:577
  183.6 9.3 %collective-permute-done.12 = bf16[2,104,768]{2,1,0:T(8,128)(2,1)S(1)} collective-permute-done((bf16[2,104,768]{2,1,0:T(8,128)(2,1)S(1)}, bf16[2,104,768]{2,1,0:T(8,128)(2,1)S(1)}, u32[]{:S(2)}, u32[]{:S(2)}) %collective-permute-start.12) | collective-permute-done | bytes 319520 | tf_op jit(solution)/shard_map/ppermute | solution.py:577
  196.6 11.1 %collective-permute-done.13 = bf16[1,104,768]{2,1,0:T(8,128)(2,1)S(1)} collective-permute-done((bf16[1,104,768]{2,1,0:T(8,128)(2,1)S(1)}, bf16[1,104,768]{2,1,0:T(8,128)(2,1)S(1)}, u32[]{:S(2)}, u32[]{:S(2)}) %collective-permute-start.13) | collective-permute-done | bytes 159776 | tf_op jit(solution)/shard_map/ppermute | solution.py:577
  209.4 7.7 %collective-permute-start.6 = (bf16[128,768]{1,0:T(8,128)(2,1)S(1)}, bf16[128,768]{1,0:T(8,128)(2,1)S(1)}, u32[]{:S(2)}, u32[]{:S(2)}) collective-permute-start(bf16[128,768]{1,0:T(8,128)(2,1)S(1)} %copy-done.33), channel_id=1, source_target_pairs={{0,1},{1,0},{2,3},{3,2},{4,5},{5,4},{6,7},{7,6},{8,9},{9,8},{10,11... | collective-permute-start | bytes 589832 | tf_op jit(solution)/shard_map/ppermute | solution.py:581
  219.4 5.4 %collective-permute-done.7.refs_2_ = bf16[128,768]{1,0:T(8,128)(2,1)S(1)} collective-permute-done((bf16[128,768]{1,0:T(8,128)(2,1)S(1)}, bf16[128,768]{1,0:T(8,128)(2,1)S(1)}, u32[]{:S(2)}, u32[]{:S(2)}) %collective-permute-start.7) | collective-permute-done | bytes 196640 | tf_op jit(solution)/shard_map/ppermute | solution.py:581
  225.4 5.6 %collective-permute-done.8.refs_3_ = bf16[128,768]{1,0:T(8,128)(2,1)S(1)} collective-permute-done((bf16[128,768]{1,0:T(8,128)(2,1)S(1)}, bf16[128,768]{1,0:T(8,128)(2,1)S(1)}, u32[]{:S(2)}, u32[]{:S(2)}) %collective-permute-start.8) | collective-permute-done | bytes 196640 | tf_op jit(solution)/shard_map/ppermute | solution.py:581
  231.7 2.2 shard_map.331
  238.4 2.5 shard_map.332
  241.6 2.3 shard_map.333
  249.0 2.8 %shard_map.334 = (f32[384,768]{1,0:T(8,128)}, f32[96,3072]{1,0:T(8,128)}) custom-call(s32[3]{0:T(128)} %pad_add_fusion.me_ref, f32[1]{0:T(128)} %bitcast.18.factor_ref, bf16[2,192,768]{2,1,0:T(8,128)(2,1)} %copy-done.4, bf16[2,192,768]{2,1,0:T(8,128)(2,1)} %copy-done.10), custom_call_target="tpu_custom_call" | custom-call | tf_op jit(solution)/shard_map/pallas_call | solution.py:514
  (176 shorter events, 62.6 us)
Async XLA Ops:
  2.8 12.4 %collective-permute-start.2 = (bf16[128,768]{1,0:T(8,128)(2,1)}, bf16[128,768]{1,0:T(8,128)(2,1)}, u32[]{:S(2)}, u32[]{:S(2)}) collective-permute-start(bf16[128,768]{1,0:T(8,128)(2,1)} %get-tuple-element.116), channel_id=1, source_target_pairs={{0,3},{1,2},{2,1},{3,0},{4,7},{5,6},{6,5},{7,4},{8,11},{9,10},{10,... | collective-permute-start | bytes 589832 | tf_op jit(solution)/shard_map/ppermute | solution.py:581
  5.2 10.8 %collective-permute-start.1 = (bf16[128,768]{1,0:T(8,128)(2,1)}, bf16[128,768]{1,0:T(8,128)(2,1)}, u32[]{:S(2)}, u32[]{:S(2)}) collective-permute-start(bf16[128,768]{1,0:T(8,128)(2,1)} %get-tuple-element.117), channel_id=1, source_target_pairs={{0,2},{1,3},{2,0},{3,1},{4,6},{5,7},{6,4},{7,5},{8,10},{9,11},{10,... | collective-permute-start | bytes 589832 | tf_op jit(solution)/shard_map/ppermute | solution.py:581
  7.2 26.8 %collective-permute-start.3 = (bf16[136,768]{1,0:T(8,128)(2,1)}, bf16[136,768]{1,0:T(8,128)(2,1)}, u32[]{:S(2)}, u32[]{:S(2)}) collective-permute-start(bf16[136,768]{1,0:T(8,128)(2,1)} %get-tuple-element.112), channel_id=1, source_target_pairs={{0,1},{1,0},{2,3},{3,2},{4,5},{5,4},{6,7},{7,6},{8,9},{9,8},{10,11... | collective-permute-start | bytes 626696 | tf_op jit(solution)/shard_map/ppermute | solution.py:581
  7.6 26.4 %collective-permute-start.4 = (bf16[136,768]{1,0:T(8,128)(2,1)S(1)}, bf16[136,768]{1,0:T(8,128)(2,1)}, u32[]{:S(2)}, u32[]{:S(2)}) collective-permute-start(bf16[136,768]{1,0:T(8,128)(2,1)S(1)} %get-tuple-element.113), channel_id=1, source_target_pairs={{0,2},{1,3},{2,0},{3,1},{4,6},{5,7},{6,4},{7,5},{8,10},{9,11},{10,... | collective-permute-start | bytes 626696 | tf_op jit(solution)/shard_map/ppermute | solution.py:581
  15.2 18.8 %collective-permute-start.5 = (bf16[136,768]{1,0:T(8,128)(2,1)S(1)}, bf16[136,768]{1,0:T(8,128)(2,1)}, u32[]{:S(2)}, u32[]{:S(2)}) collective-permute-start(bf16[136,768]{1,0:T(8,128)(2,1)S(1)} %get-tuple-element.110), channel_id=1, source_target_pairs={{0,3},{1,2},{2,1},{3,0},{4,7},{5,6},{6,5},{7,4},{8,11},{9,10},{10,... | collective-permute-start | bytes 626696 | tf_op jit(solution)/shard_map/ppermute | solution.py:581
  85.8 29.2 %collective-permute-start.24 = (bf16[16,96,768]{2,1,0:T(8,128)(2,1)}, bf16[16,96,768]{2,1,0:T(8,128)(2,1)}, u32[]{:S(2)}, u32[]{:S(2)}) collective-permute-start(bf16[16,96,768]{2,1,0:T(8,128)(2,1)} %get-tuple-element.106), channel_id=1, source_target_pairs={{0,1},{1,0},{2,3},{3,2},{4,5},{5,4},{6,7},{7,6},{8,9},{9,8},{10,11... | collective-permute-start | bytes 7077896 | tf_op jit(solution)/shard_map/ppermute | solution.py:572
  116.7 16.3 %collective-permute-start.25 = (bf16[8,96,768]{2,1,0:T(8,128)(2,1)S(1)}, bf16[8,96,768]{2,1,0:T(8,128)(2,1)S(1)}, u32[]{:S(2)}, u32[]{:S(2)}) collective-permute-start(bf16[8,96,768]{2,1,0:T(8,128)(2,1)S(1)} %add_convert_fusion.2), channel_id=1, source_target_pairs={{0,2},{1,5},{2,0},{3,7},{4,6},{5,1},{6,4},{7,3},{8,10},{9,13},{10,... | collective-permute-start | bytes 3538952 | tf_op jit(solution)/shard_map/ppermute | solution.py:577
  119.9 26.8 %collective-permute-start.18 = (bf16[8,104,768]{2,1,0:T(8,128)(2,1)S(1)}, bf16[8,104,768]{2,1,0:T(8,128)(2,1)S(1)}, u32[]{:S(2)}, u32[]{:S(2)}) collective-permute-start(bf16[8,104,768]{2,1,0:T(8,128)(2,1)S(1)} %add_convert_fusion), channel_id=1, source_target_pairs={{0,2},{1,5},{2,0},{3,7},{4,6},{5,1},{6,4},{7,3},{8,10},{9,13},{10,... | collective-permute-start | bytes 3833864 | tf_op jit(solution)/shard_map/ppermute | solution.py:577
  123.6 36.8 %collective-permute-start.10 = (bf16[8,104,768]{2,1,0:T(8,128)(2,1)S(1)}, bf16[8,104,768]{2,1,0:T(8,128)(2,1)S(1)}, u32[]{:S(2)}, u32[]{:S(2)}) collective-permute-start(bf16[8,104,768]{2,1,0:T(8,128)(2,1)S(1)} %add_convert_fusion.1), channel_id=1, source_target_pairs={{0,2},{1,5},{2,0},{3,7},{4,6},{5,1},{6,4},{7,3},{8,10},{9,13},{10,... | collective-permute-start | bytes 3833864 | tf_op jit(solution)/shard_map/ppermute | solution.py:577
  134.3 16.3 %collective-permute-start.26 = (bf16[4,96,768]{2,1,0:T(8,128)(2,1)S(1)}, bf16[4,96,768]{2,1,0:T(8,128)(2,1)S(1)}, u32[]{:S(2)}, u32[]{:S(2)}) collective-permute-start(bf16[4,96,768]{2,1,0:T(8,128)(2,1)S(1)} %add_convert_fusion.7), channel_id=1, source_target_pairs={{0,4},{1,9},{2,6},{3,11},{4,0},{5,13},{6,2},{7,15},{8,12},{9,1},{1... | collective-permute-start | bytes 1769480 | tf_op jit(solution)/shard_map/ppermute | solution.py:577
  146.9 19.0 %collective-permute-start.19 = (bf16[4,104,768]{2,1,0:T(8,128)(2,1)S(1)}, bf16[4,104,768]{2,1,0:T(8,128)(2,1)S(1)}, u32[]{:S(2)}, u32[]{:S(2)}) collective-permute-start(bf16[4,104,768]{2,1,0:T(8,128)(2,1)S(1)} %add_convert_fusion.5), channel_id=1, source_target_pairs={{0,4},{1,9},{2,6},{3,11},{4,0},{5,13},{6,2},{7,15},{8,12},{9,1},{1... | collective-permute-start | bytes 1916936 | tf_op jit(solution)/shard_map/ppermute | solution.py:577
  160.6 17.3 %collective-permute-start.11 = (bf16[4,104,768]{2,1,0:T(8,128)(2,1)S(1)}, bf16[4,104,768]{2,1,0:T(8,128)(2,1)S(1)}, u32[]{:S(2)}, u32[]{:S(2)}) collective-permute-start(bf16[4,104,768]{2,1,0:T(8,128)(2,1)S(1)} %add_convert_fusion.6), channel_id=1, source_target_pairs={{0,4},{1,9},{2,6},{3,11},{4,0},{5,13},{6,2},{7,15},{8,12},{9,1},{1... | collective-permute-start | bytes 1916936 | tf_op jit(solution)/shard_map/ppermute | solution.py:577
  163.2 16.6 %collective-permute-start.28 = (bf16[1,96,768]{2,1,0:T(8,128)(2,1)S(1)}, bf16[1,96,768]{2,1,0:T(8,128)(2,1)S(1)}, u32[]{:S(2)}, u32[]{:S(2)}) collective-permute-start(bf16[1,96,768]{2,1,0:T(8,128)(2,1)S(1)} %add_convert_fusion.15), channel_id=1, source_target_pairs={{0,16},{1,3},{2,18},{3,1},{4,20},{5,7},{6,22},{7,5},{8,24},{9,11},... | collective-permute-start | bytes 442376 | tf_op jit(solution)/shard_map/ppermute | solution.py:577
  166.0 14.8 %collective-permute-start.20 = (bf16[2,104,768]{2,1,0:T(8,128)(2,1)S(1)}, bf16[2,104,768]{2,1,0:T(8,128)(2,1)S(1)}, u32[]{:S(2)}, u32[]{:S(2)}) collective-permute-start(bf16[2,104,768]{2,1,0:T(8,128)(2,1)S(1)} %add_convert_fusion.8), channel_id=1, source_target_pairs={{0,8},{1,17},{2,10},{3,19},{4,12},{5,21},{6,14},{7,23},{8,0},{9,25... | collective-permute-start | bytes 958472 | tf_op jit(solution)/shard_map/ppermute | solution.py:577
  178.1 14.8 %collective-permute-start.12 = (bf16[2,104,768]{2,1,0:T(8,128)(2,1)S(1)}, bf16[2,104,768]{2,1,0:T(8,128)(2,1)S(1)}, u32[]{:S(2)}, u32[]{:S(2)}) collective-permute-start(bf16[2,104,768]{2,1,0:T(8,128)(2,1)S(1)} %add_convert_fusion.9), channel_id=1, source_target_pairs={{0,8},{1,17},{2,10},{3,19},{4,12},{5,21},{6,14},{7,23},{8,0},{9,25... | collective-permute-start | bytes 958472 | tf_op jit(solution)/shard_map/ppermute | solution.py:577
  180.9 13.9 %collective-permute-start.21 = (bf16[1,104,768]{2,1,0:T(8,128)(2,1)S(1)}, bf16[1,104,768]{2,1,0:T(8,128)(2,1)S(1)}, u32[]{:S(2)}, u32[]{:S(2)}) collective-permute-start(bf16[1,104,768]{2,1,0:T(8,128)(2,1)S(1)} %add_convert_fusion.12), channel_id=1, source_target_pairs={{0,16},{1,3},{2,18},{3,1},{4,20},{5,7},{6,22},{7,5},{8,24},{9,11},... | collective-permute-start | bytes 479240 | tf_op jit(solution)/shard_map/ppermute | solution.py:577
  193.0 14.6 %collective-permute-start.13 = (bf16[1,104,768]{2,1,0:T(8,128)(2,1)S(1)}, bf16[1,104,768]{2,1,0:T(8,128)(2,1)S(1)}, u32[]{:S(2)}, u32[]{:S(2)}) collective-permute-start(bf16[1,104,768]{2,1,0:T(8,128)(2,1)S(1)} %add_convert_fusion.13), channel_id=1, source_target_pairs={{0,16},{1,3},{2,18},{3,1},{4,20},{5,7},{6,22},{7,5},{8,24},{9,11},... | collective-permute-start | bytes 479240 | tf_op jit(solution)/shard_map/ppermute | solution.py:577
  195.0 23.6 %collective-permute-start.22 = (bf16[104,768]{1,0:T(8,128)(2,1)S(1)}, bf16[104,768]{1,0:T(8,128)(2,1)S(1)}, u32[]{:S(2)}, u32[]{:S(2)}) collective-permute-start(bf16[104,768]{1,0:T(8,128)(2,1)S(1)} %bitcast.72), channel_id=1, source_target_pairs={{0,2},{1,3},{2,0},{3,1},{4,6},{5,7},{6,4},{7,5},{8,10},{9,11},{10,... | collective-permute-start | bytes 479240 | tf_op jit(solution)/shard_map/ppermute | solution.py:581
  207.8 26.0 %collective-permute-start.29 = (bf16[192,768]{1,0:T(8,128)(2,1)S(1)}, bf16[192,768]{1,0:T(8,128)(2,1)S(1)}, u32[]{:S(2)}, u32[]{:S(2)}) collective-permute-start(bf16[192,768]{1,0:T(8,128)(2,1)S(1)} %pad_maximum_fusion.2), channel_id=1, source_target_pairs={{0,2},{1,3},{2,0},{3,1},{4,6},{5,7},{6,4},{7,5},{8,10},{9,11},{10,... | collective-permute-start | bytes 884744 | tf_op jit(solution)/shard_map/ppermute | solution.py:581
  217.6 13.4 %collective-permute-start.8 = (bf16[128,768]{1,0:T(8,128)(2,1)S(1)}, bf16[128,768]{1,0:T(8,128)(2,1)S(1)}, u32[]{:S(2)}, u32[]{:S(2)}) collective-permute-start(bf16[128,768]{1,0:T(8,128)(2,1)S(1)} %copy-done.30), channel_id=1, source_target_pairs={{0,3},{1,2},{2,1},{3,0},{4,7},{5,6},{6,5},{7,4},{8,11},{9,10},{10,... | collective-permute-start | bytes 589832 | tf_op jit(solution)/shard_map/ppermute | solution.py:581
  218.6 22.3 %collective-permute-start.23 = (bf16[2,104,768]{2,1,0:T(8,128)(2,1)S(1)}, bf16[2,104,768]{2,1,0:T(8,128)(2,1)S(1)}, u32[]{:S(2)}, u32[]{:S(2)}) collective-permute-start(bf16[2,104,768]{2,1,0:T(8,128)(2,1)S(1)} %pad_maximum_fusion.1.near_ref), channel_id=1, source_target_pairs={{0,1},{1,0},{2,3},{3,2},{4,5},{5,4},{6,7},{7,6},{8,9},{9,8},{10,11... | collective-permute-start | bytes 958472 | tf_op jit(solution)/shard_map/ppermute | solution.py:581
  219.4 17.8 %collective-permute-start.14 = (bf16[128,768]{1,0:T(8,128)(2,1)}, bf16[128,768]{1,0:T(8,128)(2,1)S(1)}, u32[]{:S(2)}, u32[]{:S(2)}) collective-permute-start(bf16[128,768]{1,0:T(8,128)(2,1)} %get-tuple-element.93), channel_id=1, source_target_pairs={{0,1},{1,0},{2,3},{3,2},{4,5},{5,4},{6,7},{7,6},{8,9},{9,8},{10,11... | collective-permute-start | bytes 589832 | tf_op jit(solution)/shard_map/ppermute | solution.py:581
  224.9 12.3 %collective-permute-start.15 = (bf16[128,768]{1,0:T(8,128)(2,1)}, bf16[128,768]{1,0:T(8,128)(2,1)S(1)}, u32[]{:S(2)}, u32[]{:S(2)}) collective-permute-start(bf16[128,768]{1,0:T(8,128)(2,1)} %get-tuple-element.94), channel_id=1, source_target_pairs={{0,2},{1,3},{2,0},{3,1},{4,6},{5,7},{6,4},{7,5},{8,10},{9,11},{10,... | collective-permute-start | bytes 589832 | tf_op jit(solution)/shard_map/ppermute | solution.py:581
  233.9 14.2 %collective-permute-start.30 = (bf16[2,192,768]{2,1,0:T(8,128)(2,1)S(1)}, bf16[2,192,768]{2,1,0:T(8,128)(2,1)S(1)}, u32[]{:S(2)}, u32[]{:S(2)}) collective-permute-start(bf16[2,192,768]{2,1,0:T(8,128)(2,1)S(1)} %pad_maximum_fusion.near_ref), channel_id=1, source_target_pairs={{0,1},{1,0},{2,3},{3,2},{4,5},{5,4},{6,7},{7,6},{8,9},{9,8},{10,11... | collective-permute-start | bytes 1769480 | tf_op jit(solution)/shard_map/ppermute | solution.py:581
  (41 other events, 304.5 us)

commit v6 on v5

--- a/solution.py
+++ b/solution.py
@@ -561,6 +561,7 @@
     plan = Plan(mesh)
     ndp, nseq = plan.ndp, plan.nseq
     devices = ("dp", "seq")
+    sent = {}
 
     def total_of(terms):
         total = terms[0].astype(f32)
@@ -571,9 +572,10 @@
     def start_chunk(keep, send):
         return [keep, lax.ppermute(send, devices, plan.perm(-1))]
 
-    def step_chunk(terms, step):
+    def step_chunk(name, terms, step):
         half = terms[0].shape[0] // 2
         send = total_of([t[half:] for t in terms]).astype(bf16)
+        sent.setdefault(name, []).append(send)
         got = lax.ppermute(send, devices, plan.perm(step))
         return [t[:half] for t in terms] + [got]
 
@@ -607,6 +609,7 @@
         lm_mask,
         doc_segments,
     ):
+        sent.clear()
         seg_dev, rows_dev, width = tokens.shape
         assert rows_dev * nseq < (1 << DIGITS) and ndp * nseq <= 256
         assert seg_dev == nseq
@@ -702,12 +705,12 @@
             d_context = dot(d_attn, output_weight, 1, 1).astype(bf16)
             small1 = rows_of(d_normed * hat1, d_normed, d_attn.astype(f32))
         inner = start_chunk(keep, send)
-        outer = step_chunk(outer, 0)
+        outer = step_chunk("o", outer, 0)
         d_queries, d_keys, d_values = attention_backward(
             queries, keys, values, context, d_context, probs, 1, rows
         )
-        outer = step_chunk(outer, 1)
-        inner = step_chunk(inner, 0)
+        outer = step_chunk("o", outer, 1)
+        inner = step_chunk("i", inner, 0)
         cut_pieces, small = inputs_backward(
             me,
             (d_queries, d_keys, d_values),
@@ -735,11 +738,13 @@
             keep, send = place_pieces(plan, me, jnp.concatenate([blocks, below], axis=2))
         attn = start_chunk(keep, send)
         for step in range(2, plan.steps):
-            outer = step_chunk(outer, step)
+            outer = step_chunk("o", outer, step)
         for step in range(1, plan.steps):
-            inner = step_chunk(inner, step)
+            inner = step_chunk("i", inner, step)
         for step in range(plan.steps):
-            attn = step_chunk(attn, step)
+            attn = step_chunk("t", attn, step)
+        *outer, _ = lax.optimization_barrier((*outer, sent["t"][1]))
+        *inner, _ = lax.optimization_barrier((*inner, sent["t"][2]))
         outer_rows = ff // (ndp * nseq)
         outer = total_of(outer)[0]
         total = jnp.sum(outer[outer_rows, :DIGITS] * (2.0 ** jnp.arange(DIGITS)).astype(f32))

time: 253 us -> 257 us (1.016)
  waiting for transfers between devices: 74 us -> 78.6 us
    ppermute x12, waiting for transfers between devices: 58.5 us -> 63.3 us  [step_chunk(): got = lax.ppermute(send, devices, plan.perm(step))]
    ppermute x3, waiting for transfers between devices: 3.04 us -> 0.41 us  [start_chunk(): return [keep, lax.ppermute(send, devices, plan.perm(-1))]]
  transfers between devices with their start and end apart: 31 -> 31, of which waited for: 13 -> 13; matrix products, arithmetic and copies ran while one was open for 10% -> 10% of each run, Pallas kernels for 19% -> 18%
where the time goes in v6:
time: 257 us; the launch traced here: 256 us
  Pallas kernels  101 us (39%)
  waiting for transfers between devices  78.6 us (31%)
  starting transfers between devices  40.4 us (16%)
  other arithmetic  15.3 us (6%)
  local copies, waits for them, and re-layouts  12.4 us (5%)
  matrix products  5.01 us (2%)
  between operations  2.79 us (1%)
    ppermute x12, waiting for transfers between devices, step_chunk(): got = lax.ppermute(send, devices, plan.perm(step))  63.3 us
    pallas_call x1, Pallas kernels, ffn_backward(): pl.pallas_call(kernel, grid_spec=pltpu.PrefetchScalarGridSpec(num_scalar_...  21.8 us
    pallas_call x1, Pallas kernels, ffn_forward(): pl.pallas_call(kernel, grid=(inner // BLOCK,), in_specs=[full(flat), full...  21.4 us
    ppermute x12, starting transfers between devices, step_chunk(): got = lax.ppermute(send, devices, plan.perm(step))  20.3 us
    ppermute x16, starting transfers between devices, swap_seq(): return lax.ppermute(x, 'seq', [(i, i ^ k) for i in range(nseq)])  19.5 us
    ppermute x16, waiting for transfers between devices, swap_seq(): return lax.ppermute(x, 'seq', [(i, i ^ k) for i in range(nseq)])  14.8 us
    pallas_call x1, Pallas kernels, attention_backward(): pl.pallas_call(attn_bwd_kernel, grid=(segs, pairs), in_specs=[spec] * 5 +...  12.4 us
    pallas_call x1, Pallas kernels, attention_forward(): pl.pallas_call(attn_fwd_kernel, grid=(segs, pairs), in_specs=[spec, spec,...  11.3 us
  transfers between devices with their start and end apart: 31, of which 13 were waited for; matrix products, arithmetic and copies ran while one was open for 10% of the time, Pallas kernels for 18%

profile of v6, /device:TPU:0, one launch (start us, length us, event | category | flops | bytes accessed | tf_op | source)
XLA Modules:
  0.0 256.0 jit_solution(1059264102006534646)
XLA Ops:
  2.7 2.4 collective-permute-start.2
  22.1 11.3 %attn_fwd.1 = (bf16[512,768]{1,0:T(8,128)(2,1)}, bf16[12,512,512]{2,1,0:T(8,128)(2,1)}) custom-call(bf16[512,768]{1,0:T(8,128)(2,1)} %add_convert_fusion.4.q_ref, bf16[512,768]{1,0:T(8,128)(2,1)} %convolution_convert_fusion.k_ref, bf16[512,768]{1,0:T(8,128)(2,1)} %add_convert_fusion.3.v_ref), custom_call_target="tpu_custom_call" | custom-call | tf_op jit(solution)/shard_map/attn_fwd/pallas_call | solution.py:81
  34.3 21.4 %ffn_fwd.1 = (f32[512,768]{1,0:T(8,128)}, f32[512,128]{1,0:T(8,128)}, bf16[768,512]{1,0:T(8,128)(2,1)}, bf16[512,3072]{1,0:T(8,128)(2,1)}, bf16[512,3072]{1,0:T(...) custom-call(bf16[512,768]{1,0:T(8,128)(2,1)} %copy-done, ...), custom_call_target="tpu_custom_call" | custom-call | tf_op jit(solution)/shard_map/ffn_fwd/pallas_call | solution.py:217
  55.7 8.7 %outer_grad.1 = (bf16[16,104,768]{2,1,0:T(8,128)(2,1)}, bf16[16,104,768]{2,1,0:T(8,128)(2,1)}) custom-call(s32[3]{0:T(128)} %pad_add_fusion.me_ref, bf16[512,3072]{1,0:T(8,128)(2,1)} %get-tuple-element.84.active_ref, bf16[512,768]{1,0:T(8,128)(2,1)} %get-tuple-element.91.d_ref.douter_ref, f32[8,768]{1,0:T(8,128)} %get-tuple-element.85.small_ref.s2_ref), custom_call_target="tpu_custom_call" | custom-call | tf_op jit(solution)/shard_map/outer_grad/pallas_call | solution.py:356
  64.4 21.8 %ffn_bwd.1 = (bf16[16,96,768]{2,1,0:T(8,128)(2,1)}, bf16[16,96,768]{2,1,0:T(8,128)(2,1)}, f32[512,768]{1,0:T(8,128)}, bf16[512,768]{1,0:T(8,128)(2,1)}, bf16[512...) custom-call(s32[3]{0:T(128)} %pad_add_fusion.me_ref, bf16[512,3072]{1,0:T(8,128)(2,1)} %get-tuple-element.90.slope_ref, ...), custom_call_target="tpu_custom_call" | custom-call | tf_op jit(solution)/shard_map/ffn_bwd/pallas_call | solution.py:413
  86.7 12.4 %attn_bwd.1 = (bf16[512,768]{1,0:T(8,128)(2,1)}, bf16[512,768]{1,0:T(8,128)(2,1)}, bf16[512,768]{1,0:T(8,128)(2,1)}) custom-call(bf16[512,768]{1,0:T(8,128)(2,1)} %add_convert_fusion.4.q_ref, bf16[512,768]{1,0:T(8,128)(2,1)} %convolution_convert_fusion.k_ref, bf16[512,768]{1,0:T(8,128)(2,1)} %add_convert_fusion.3.v_ref, ...), custom_call_target="tpu_custom_call" | custom-call | tf_op jit(solution)/shard_map/attn_bwd/pallas_call | solution.py:100
  99.2 6.2 %inputs_bwd.1 = (bf16[128,768]{1,0:T(8,128)(2,1)}, bf16[128,768]{1,0:T(8,128)(2,1)}, bf16[128,768]{1,0:T(8,128)(2,1)}, bf16[128,768]{1,0:T(8,128)(2,1)}, f32[4,8,768]{2,1,0:T(8,128)}) custom-call(s32[3]{0:T(128)} %pad_add_fusion.me_ref, bf16[512,768]{1,0:T(8,128)(2,1)} %get-tuple-element.98.dq_ref.d0_ref, bf16[512,768]{1,0:T(8,128)(2,1)} %get-tuple-element.99.dk_ref.d1_ref, ...), custom_call_target="tpu_custom_call" | custom-call | tf_op jit(solution)/shard_map/inputs_bwd/pallas_call | solution.py:267
  105.4 9.7 %attn_grad.1 = (bf16[16,104,768]{2,1,0:T(8,128)(2,1)}, bf16[16,104,768]{2,1,0:T(8,128)(2,1)}) custom-call(s32[3]{0:T(128)} %pad_add_fusion.me_ref, bf16[512,768]{1,0:T(8,128)(2,1)} %copy-done, bf16[512,768]{1,0:T(8,128)(2,1)} %get-tuple-element.76.ctx_ref, bf16[512,768]{1,0:T(8,128)(2,1)} %get-tuple-element.98.dq_ref.d0_ref, ...), custom_call_target="tpu_custom_call" | custom-call | tf_op jit(solution)/shard_map/attn_grad/pallas_call | solution.py:538
  122.1 11.4 %collective-permute-done.25 = bf16[8,96,768]{2,1,0:T(8,128)(2,1)S(1)} collective-permute-done((bf16[8,96,768]{2,1,0:T(8,128)(2,1)S(1)}, bf16[8,96,768]{2,1,0:T(8,128)(2,1)S(1)}, u32[]{:S(2)}, u32[]{:S(2)}) %collective-permute-start.25) | collective-permute-done | bytes 1179680 | tf_op jit(solution)/shard_map/ppermute | solution.py:579
  136.8 10.4 %collective-permute-done.10 = bf16[8,104,768]{2,1,0:T(8,128)(2,1)S(1)} collective-permute-done((bf16[8,104,768]{2,1,0:T(8,128)(2,1)S(1)}, bf16[8,104,768]{2,1,0:T(8,128)(2,1)S(1)}, u32[]{:S(2)}, u32[]{:S(2)}) %collective-permute-start.10) | collective-permute-done | bytes 1277984 | tf_op jit(solution)/shard_map/ppermute | solution.py:579
  149.0 2.5 collective-permute-done.26
  154.4 6.5 %collective-permute-done.15 = bf16[8,104,768]{2,1,0:T(8,128)(2,1)S(1)} collective-permute-done((bf16[8,104,768]{2,1,0:T(8,128)(2,1)S(1)}, bf16[8,104,768]{2,1,0:T(8,128)(2,1)S(1)}, u32[]{:S(2)}, u32[]{:S(2)}) %collective-permute-start.15) | collective-permute-done | bytes 1277984 | tf_op jit(solution)/shard_map/ppermute | solution.py:579
  167.7 2.5 collective-permute-start.12
  170.3 8.6 %collective-permute-done.19 = bf16[4,104,768]{2,1,0:T(8,128)(2,1)S(1)} collective-permute-done((bf16[4,104,768]{2,1,0:T(8,128)(2,1)S(1)}, bf16[4,104,768]{2,1,0:T(8,128)(2,1)S(1)}, u32[]{:S(2)}, u32[]{:S(2)}) %collective-permute-start.19) | collective-permute-done | bytes 639008 | tf_op jit(solution)/shard_map/ppermute | solution.py:579
  181.9 2.7 %collective-permute-start.13 = (bf16[1,104,768]{2,1,0:T(8,128)(2,1)S(1)}, bf16[1,104,768]{2,1,0:T(8,128)(2,1)S(1)}, u32[]{:S(2)}, u32[]{:S(2)}) collective-permute-start(bf16[1,104,768]{2,1,0:T(8,128)(2,1)S(1)} %add_convert_fusion.13), channel_id=1, source_target_pairs={{0,16},{1,3},{2,18},{3,1},{4,20},{5,7},{6,22},{7,5},{8,24},{9,11},... | collective-permute-start | bytes 479240 | tf_op jit(solution)/shard_map/ppermute | solution.py:579
  184.5 9.6 %collective-permute-done.20 = bf16[2,104,768]{2,1,0:T(8,128)(2,1)S(1)} collective-permute-done((bf16[2,104,768]{2,1,0:T(8,128)(2,1)S(1)}, bf16[2,104,768]{2,1,0:T(8,128)(2,1)S(1)}, u32[]{:S(2)}, u32[]{:S(2)}) %collective-permute-start.20) | collective-permute-done | bytes 319520 | tf_op jit(solution)/shard_map/ppermute | solution.py:579
  196.2 12.4 %collective-permute-done.21 = bf16[1,104,768]{2,1,0:T(8,128)(2,1)S(1)} collective-permute-done((bf16[1,104,768]{2,1,0:T(8,128)(2,1)S(1)}, bf16[1,104,768]{2,1,0:T(8,128)(2,1)S(1)}, u32[]{:S(2)}, u32[]{:S(2)}) %collective-permute-start.21) | collective-permute-done | bytes 159776 | tf_op jit(solution)/shard_map/ppermute | solution.py:579
  211.1 7.4 %collective-permute-start.6 = (bf16[128,768]{1,0:T(8,128)(2,1)S(1)}, bf16[128,768]{1,0:T(8,128)(2,1)S(1)}, u32[]{:S(2)}, u32[]{:S(2)}) collective-permute-start(bf16[128,768]{1,0:T(8,128)(2,1)S(1)} %copy-done.43), channel_id=1, source_target_pairs={{0,1},{1,0},{2,3},{3,2},{4,5},{5,4},{6,7},{7,6},{8,9},{9,8},{10,11... | collective-permute-start | bytes 589832 | tf_op jit(solution)/shard_map/ppermute | solution.py:583
  221.0 5.2 %collective-permute-done.7.refs_2_ = bf16[128,768]{1,0:T(8,128)(2,1)S(1)} collective-permute-done((bf16[128,768]{1,0:T(8,128)(2,1)S(1)}, bf16[128,768]{1,0:T(8,128)(2,1)S(1)}, u32[]{:S(2)}, u32[]{:S(2)}) %collective-permute-start.7) | collective-permute-done | bytes 196640 | tf_op jit(solution)/shard_map/ppermute | solution.py:583
  227.7 7.0 %collective-permute-done.8.refs_3_ = bf16[128,768]{1,0:T(8,128)(2,1)S(1)} collective-permute-done((bf16[128,768]{1,0:T(8,128)(2,1)S(1)}, bf16[128,768]{1,0:T(8,128)(2,1)S(1)}, u32[]{:S(2)}, u32[]{:S(2)}) %collective-permute-start.8) | collective-permute-done | bytes 196640 | tf_op jit(solution)/shard_map/ppermute | solution.py:583
  235.4 2.2 shard_map.331
  242.6 2.5 shard_map.332
  245.8 2.3 shard_map.333
  253.1 2.8 %shard_map.334 = (f32[384,768]{1,0:T(8,128)}, f32[96,3072]{1,0:T(8,128)}) custom-call(s32[3]{0:T(128)} %pad_add_fusion.me_ref, f32[1]{0:T(128)} %bitcast.18.factor_ref, bf16[2,192,768]{2,1,0:T(8,128)(2,1)} %copy-done.5, bf16[2,192,768]{2,1,0:T(8,128)(2,1)} %copy-done.15), custom_call_target="tpu_custom_call" | custom-call | tf_op jit(solution)/shard_map/pallas_call | solution.py:514
  (212 shorter events, 63.2 us)
Async XLA Ops:
  2.7 12.4 %collective-permute-start.2 = (bf16[128,768]{1,0:T(8,128)(2,1)S(1)}, bf16[128,768]{1,0:T(8,128)(2,1)S(1)}, u32[]{:S(2)}, u32[]{:S(2)}) collective-permute-start(bf16[128,768]{1,0:T(8,128)(2,1)S(1)} %get-tuple-element.140), channel_id=1, source_target_pairs={{0,3},{1,2},{2,1},{3,0},{4,7},{5,6},{6,5},{7,4},{8,11},{9,10},{10,... | collective-permute-start | bytes 589832 | tf_op jit(solution)/shard_map/ppermute | solution.py:583
  7.1 26.4 %collective-permute-start.3 = (bf16[136,768]{1,0:T(8,128)(2,1)S(1)}, bf16[136,768]{1,0:T(8,128)(2,1)S(1)}, u32[]{:S(2)}, u32[]{:S(2)}) collective-permute-start(bf16[136,768]{1,0:T(8,128)(2,1)S(1)} %get-tuple-element.136), channel_id=1, source_target_pairs={{0,1},{1,0},{2,3},{3,2},{4,5},{5,4},{6,7},{7,6},{8,9},{9,8},{10,11... | collective-permute-start | bytes 626696 | tf_op jit(solution)/shard_map/ppermute | solution.py:583
  7.5 26.0 %collective-permute-start.4 = (bf16[136,768]{1,0:T(8,128)(2,1)S(1)}, bf16[136,768]{1,0:T(8,128)(2,1)S(1)}, u32[]{:S(2)}, u32[]{:S(2)}) collective-permute-start(bf16[136,768]{1,0:T(8,128)(2,1)S(1)} %get-tuple-element.137), channel_id=1, source_target_pairs={{0,2},{1,3},{2,0},{3,1},{4,6},{5,7},{6,4},{7,5},{8,10},{9,11},{10,... | collective-permute-start | bytes 626696 | tf_op jit(solution)/shard_map/ppermute | solution.py:583
  15.1 18.4 %collective-permute-start.5 = (bf16[136,768]{1,0:T(8,128)(2,1)S(1)}, bf16[136,768]{1,0:T(8,128)(2,1)S(1)}, u32[]{:S(2)}, u32[]{:S(2)}) collective-permute-start(bf16[136,768]{1,0:T(8,128)(2,1)S(1)} %get-tuple-element.134), channel_id=1, source_target_pairs={{0,3},{1,2},{2,1},{3,0},{4,7},{5,6},{6,5},{7,4},{8,11},{9,10},{10,... | collective-permute-start | bytes 626696 | tf_op jit(solution)/shard_map/ppermute | solution.py:583
  86.2 29.0 %collective-permute-start.24 = (bf16[16,96,768]{2,1,0:T(8,128)(2,1)}, bf16[16,96,768]{2,1,0:T(8,128)(2,1)}, u32[]{:S(2)}, u32[]{:S(2)}) collective-permute-start(bf16[16,96,768]{2,1,0:T(8,128)(2,1)} %get-tuple-element.124), channel_id=1, source_target_pairs={{0,1},{1,0},{2,3},{3,2},{4,5},{5,4},{6,7},{7,6},{8,9},{9,8},{10,11... | collective-permute-start | bytes 7077896 | tf_op jit(solution)/shard_map/ppermute | solution.py:573
  86.2 32.5 %collective-permute-start.9 = (bf16[16,104,768]{2,1,0:T(8,128)(2,1)}, bf16[16,104,768]{2,1,0:T(8,128)(2,1)S(1)}, u32[]{:S(2)}, u32[]{:S(2)}) collective-permute-start(bf16[16,104,768]{2,1,0:T(8,128)(2,1)} %get-tuple-element.89), channel_id=1, source_target_pairs={{0,1},{1,0},{2,3},{3,2},{4,5},{5,4},{6,7},{7,6},{8,9},{9,8},{10,11... | collective-permute-start | bytes 7667720 | tf_op jit(solution)/shard_map/ppermute | solution.py:573
  117.2 16.3 %collective-permute-start.25 = (bf16[8,96,768]{2,1,0:T(8,128)(2,1)S(1)}, bf16[8,96,768]{2,1,0:T(8,128)(2,1)S(1)}, u32[]{:S(2)}, u32[]{:S(2)}) collective-permute-start(bf16[8,96,768]{2,1,0:T(8,128)(2,1)S(1)} %add_convert_fusion.2), channel_id=1, source_target_pairs={{0,2},{1,5},{2,0},{3,7},{4,6},{5,1},{6,4},{7,3},{8,10},{9,13},{10,... | collective-permute-start | bytes 3538952 | tf_op jit(solution)/shard_map/ppermute | solution.py:579
  119.1 28.1 %collective-permute-start.10 = (bf16[8,104,768]{2,1,0:T(8,128)(2,1)S(1)}, bf16[8,104,768]{2,1,0:T(8,128)(2,1)S(1)}, u32[]{:S(2)}, u32[]{:S(2)}) collective-permute-start(bf16[8,104,768]{2,1,0:T(8,128)(2,1)S(1)} %add_convert_fusion.1), channel_id=1, source_target_pairs={{0,2},{1,5},{2,0},{3,7},{4,6},{5,1},{6,4},{7,3},{8,10},{9,13},{10,... | collective-permute-start | bytes 3833864 | tf_op jit(solution)/shard_map/ppermute | solution.py:579
  120.5 40.4 %collective-permute-start.15 = (bf16[8,104,768]{2,1,0:T(8,128)(2,1)S(1)}, bf16[8,104,768]{2,1,0:T(8,128)(2,1)S(1)}, u32[]{:S(2)}, u32[]{:S(2)}) collective-permute-start(bf16[8,104,768]{2,1,0:T(8,128)(2,1)S(1)} %add_convert_fusion), channel_id=1, source_target_pairs={{0,2},{1,5},{2,0},{3,7},{4,6},{5,1},{6,4},{7,3},{8,10},{9,13},{10,... | collective-permute-start | bytes 3833864 | tf_op jit(solution)/shard_map/ppermute | solution.py:579
  135.2 16.3 %collective-permute-start.26 = (bf16[4,96,768]{2,1,0:T(8,128)(2,1)S(1)}, bf16[4,96,768]{2,1,0:T(8,128)(2,1)S(1)}, u32[]{:S(2)}, u32[]{:S(2)}) collective-permute-start(bf16[4,96,768]{2,1,0:T(8,128)(2,1)S(1)} %add_convert_fusion.7), channel_id=1, source_target_pairs={{0,4},{1,9},{2,6},{3,11},{4,0},{5,13},{6,2},{7,15},{8,12},{9,1},{1... | collective-permute-start | bytes 1769480 | tf_op jit(solution)/shard_map/ppermute | solution.py:579
  147.5 20.1 %collective-permute-start.11 = (bf16[4,104,768]{2,1,0:T(8,128)(2,1)S(1)}, bf16[4,104,768]{2,1,0:T(8,128)(2,1)S(1)}, u32[]{:S(2)}, u32[]{:S(2)}) collective-permute-start(bf16[4,104,768]{2,1,0:T(8,128)(2,1)S(1)} %add_convert_fusion.6), channel_id=1, source_target_pairs={{0,4},{1,9},{2,6},{3,11},{4,0},{5,13},{6,2},{7,15},{8,12},{9,1},{1... | collective-permute-start | bytes 1916936 | tf_op jit(solution)/shard_map/ppermute | solution.py:579
  152.8 11.9 %collective-permute-start.27 = (bf16[2,96,768]{2,1,0:T(8,128)(2,1)S(1)}, bf16[2,96,768]{2,1,0:T(8,128)(2,1)S(1)}, u32[]{:S(2)}, u32[]{:S(2)}) collective-permute-start(bf16[2,96,768]{2,1,0:T(8,128)(2,1)S(1)} %add_convert_fusion.10), channel_id=1, source_target_pairs={{0,8},{1,17},{2,10},{3,19},{4,12},{5,21},{6,14},{7,23},{8,0},{9,25... | collective-permute-start | bytes 884744 | tf_op jit(solution)/shard_map/ppermute | solution.py:579
  161.2 17.7 %collective-permute-start.19 = (bf16[4,104,768]{2,1,0:T(8,128)(2,1)S(1)}, bf16[4,104,768]{2,1,0:T(8,128)(2,1)S(1)}, u32[]{:S(2)}, u32[]{:S(2)}) collective-permute-start(bf16[4,104,768]{2,1,0:T(8,128)(2,1)S(1)} %add_convert_fusion.5), channel_id=1, source_target_pairs={{0,4},{1,9},{2,6},{3,11},{4,0},{5,13},{6,2},{7,15},{8,12},{9,1},{1... | collective-permute-start | bytes 1916936 | tf_op jit(solution)/shard_map/ppermute | solution.py:579
  165.8 15.9 %collective-permute-start.28 = (bf16[1,96,768]{2,1,0:T(8,128)(2,1)S(1)}, bf16[1,96,768]{2,1,0:T(8,128)(2,1)S(1)}, u32[]{:S(2)}, u32[]{:S(2)}) collective-permute-start(bf16[1,96,768]{2,1,0:T(8,128)(2,1)S(1)} %add_convert_fusion.15), channel_id=1, source_target_pairs={{0,16},{1,3},{2,18},{3,1},{4,20},{5,7},{6,22},{7,5},{8,24},{9,11},... | collective-permute-start | bytes 442376 | tf_op jit(solution)/shard_map/ppermute | solution.py:579
  167.7 14.0 %collective-permute-start.12 = (bf16[2,104,768]{2,1,0:T(8,128)(2,1)S(1)}, bf16[2,104,768]{2,1,0:T(8,128)(2,1)S(1)}, u32[]{:S(2)}, u32[]{:S(2)}) collective-permute-start(bf16[2,104,768]{2,1,0:T(8,128)(2,1)S(1)} %add_convert_fusion.9), channel_id=1, source_target_pairs={{0,8},{1,17},{2,10},{3,19},{4,12},{5,21},{6,14},{7,23},{8,0},{9,25... | collective-permute-start | bytes 958472 | tf_op jit(solution)/shard_map/ppermute | solution.py:579
  179.0 15.1 %collective-permute-start.20 = (bf16[2,104,768]{2,1,0:T(8,128)(2,1)S(1)}, bf16[2,104,768]{2,1,0:T(8,128)(2,1)S(1)}, u32[]{:S(2)}, u32[]{:S(2)}) collective-permute-start(bf16[2,104,768]{2,1,0:T(8,128)(2,1)S(1)} %add_convert_fusion.8), channel_id=1, source_target_pairs={{0,8},{1,17},{2,10},{3,19},{4,12},{5,21},{6,14},{7,23},{8,0},{9,25... | collective-permute-start | bytes 958472 | tf_op jit(solution)/shard_map/ppermute | solution.py:579
  181.9 14.3 %collective-permute-start.13 = (bf16[1,104,768]{2,1,0:T(8,128)(2,1)S(1)}, bf16[1,104,768]{2,1,0:T(8,128)(2,1)S(1)}, u32[]{:S(2)}, u32[]{:S(2)}) collective-permute-start(bf16[1,104,768]{2,1,0:T(8,128)(2,1)S(1)} %add_convert_fusion.13), channel_id=1, source_target_pairs={{0,16},{1,3},{2,18},{3,1},{4,20},{5,7},{6,22},{7,5},{8,24},{9,11},... | collective-permute-start | bytes 479240 | tf_op jit(solution)/shard_map/ppermute | solution.py:579
  194.2 14.3 %collective-permute-start.21 = (bf16[1,104,768]{2,1,0:T(8,128)(2,1)S(1)}, bf16[1,104,768]{2,1,0:T(8,128)(2,1)S(1)}, u32[]{:S(2)}, u32[]{:S(2)}) collective-permute-start(bf16[1,104,768]{2,1,0:T(8,128)(2,1)S(1)} %add_convert_fusion.12), channel_id=1, source_target_pairs={{0,16},{1,3},{2,18},{3,1},{4,20},{5,7},{6,22},{7,5},{8,24},{9,11},... | collective-permute-start | bytes 479240 | tf_op jit(solution)/shard_map/ppermute | solution.py:579
  210.4 27.1 %collective-permute-start.29 = (bf16[192,768]{1,0:T(8,128)(2,1)S(1)}, bf16[192,768]{1,0:T(8,128)(2,1)S(1)}, u32[]{:S(2)}, u32[]{:S(2)}) collective-permute-start(bf16[192,768]{1,0:T(8,128)(2,1)S(1)} %pad_maximum_fusion.2), channel_id=1, source_target_pairs={{0,2},{1,3},{2,0},{3,1},{4,6},{5,7},{6,4},{7,5},{8,10},{9,11},{10,... | collective-permute-start | bytes 884744 | tf_op jit(solution)/shard_map/ppermute | solution.py:583
  219.9 14.8 %collective-permute-start.8 = (bf16[128,768]{1,0:T(8,128)(2,1)S(1)}, bf16[128,768]{1,0:T(8,128)(2,1)S(1)}, u32[]{:S(2)}, u32[]{:S(2)}) collective-permute-start(bf16[128,768]{1,0:T(8,128)(2,1)S(1)} %copy-done.39), channel_id=1, source_target_pairs={{0,3},{1,2},{2,1},{3,0},{4,7},{5,6},{6,5},{7,4},{8,11},{9,10},{10,... | collective-permute-start | bytes 589832 | tf_op jit(solution)/shard_map/ppermute | solution.py:583
  220.0 25.1 %collective-permute-start.23 = (bf16[2,104,768]{2,1,0:T(8,128)(2,1)S(1)}, bf16[2,104,768]{2,1,0:T(8,128)(2,1)S(1)}, u32[]{:S(2)}, u32[]{:S(2)}) collective-permute-start(bf16[2,104,768]{2,1,0:T(8,128)(2,1)S(1)} %pad_maximum_fusion.1.near_ref), channel_id=1, source_target_pairs={{0,1},{1,0},{2,3},{3,2},{4,5},{5,4},{6,7},{7,6},{8,9},{9,8},{10,11... | collective-permute-start | bytes 958472 | tf_op jit(solution)/shard_map/ppermute | solution.py:583
  220.9 18.9 %collective-permute-start.16 = (bf16[128,768]{1,0:T(8,128)(2,1)}, bf16[128,768]{1,0:T(8,128)(2,1)S(1)}, u32[]{:S(2)}, u32[]{:S(2)}) collective-permute-start(bf16[128,768]{1,0:T(8,128)(2,1)} %get-tuple-element.115), channel_id=1, source_target_pairs={{0,1},{1,0},{2,3},{3,2},{4,5},{5,4},{6,7},{7,6},{8,9},{9,8},{10,11... | collective-permute-start | bytes 589832 | tf_op jit(solution)/shard_map/ppermute | solution.py:583
  226.2 13.7 %collective-permute-start.17 = (bf16[128,768]{1,0:T(8,128)(2,1)S(1)}, bf16[128,768]{1,0:T(8,128)(2,1)S(1)}, u32[]{:S(2)}, u32[]{:S(2)}) collective-permute-start(bf16[128,768]{1,0:T(8,128)(2,1)S(1)} %copy-done.42), channel_id=1, source_target_pairs={{0,2},{1,3},{2,0},{3,1},{4,6},{5,7},{6,4},{7,5},{8,10},{9,11},{10,... | collective-permute-start | bytes 589832 | tf_op jit(solution)/shard_map/ppermute | solution.py:583
  237.6 14.7 %collective-permute-start.30 = (bf16[2,192,768]{2,1,0:T(8,128)(2,1)S(1)}, bf16[2,192,768]{2,1,0:T(8,128)(2,1)S(1)}, u32[]{:S(2)}, u32[]{:S(2)}) collective-permute-start(bf16[2,192,768]{2,1,0:T(8,128)(2,1)S(1)} %pad_maximum_fusion.near_ref), channel_id=1, source_target_pairs={{0,1},{1,0},{2,3},{3,2},{4,5},{5,4},{6,7},{7,6},{8,9},{9,8},{10,11... | collective-permute-start | bytes 1769480 | tf_op jit(solution)/shard_map/ppermute | solution.py:583
  (57 other events, 658.7 us)
